TPU v7x, 512 devices: a whole 4x4x16 slice. The times are simulated.
512 devices in a mesh: src: 64 (over z_hi, y, x, core), fac: 8 (over z_lo).
Axes of the slice: x: 4, y: 4, z: 16 (z_hi: 2, z_lo: 8; z = z_hi * 8 + z_lo), core: 2. Of those that a mesh axis runs over, the one named last changes fastest.
Arguments:
- lower_inverse: bfloat16 [8, 1024, 2, 1024], P('fac', 'src'), as said below
- coupling: bfloat16 [8, 1024, 2, 1024], P('fac', 'src'), as said below
- source_cell: int32 [8192], P('src'), may hold values from 0 to 8191
- source_wave: float32 [8192, 2], P('src'), may hold values from -6 to 6
- inflow_field: bfloat16 [8192, 2, 1024], P('src'), may hold values from -6 to 6
- receiver_cell: int32 [8192, 128], P('src'), may hold values from 0 to 8191
- observed: float32 [8192, 2, 128], P('src'), may hold values from -6 to 6
- adjoint: bfloat16 [8192, 8, 2, 1024], P('src', 'fac'), may hold values from -16 to 16
Outputs:
- wavefield: float32 [8192, 8, 2, 1024], P('src', 'fac')
- data_residual: float32 [8192, 2, 128], P('src')
- gradient: float32 [8, 1024], P('fac', 'src')
Inputs may be any that keep to these rules, and one draw needn't show every extreme that they name: lower_inverse[i, j, p, k] is zero where k > j. coupling[i, j, p, k] is zero where k < j.
All inputs are finite; a program needn't handle non-finite values.
Results may differ from a plain program's by a relative error of at most 0.025.
Values may be sent and summed in bfloat16 or wider, within the bound.
No kernel may reach another device: no remote copies, remote signals or barrier semaphores. Data moves between devices by JAX's collectives and lax.ppermute only.
A program may use at most 64 MiB of HBM per device.

v0:
```python
import math

import jax
import jax.numpy as jnp
from jax import lax
from jax.sharding import PartitionSpec as P


def from_behind(shard, axis, by):
    size = lax.axis_size(axis)
    pairs = [(i, i + by) for i in range(size) if 0 <= i + by < size]
    return lax.ppermute(shard, axis, pairs)


def complex_apply(vector, matrix):
    width = matrix.shape[0]
    joined = matrix.reshape(width, 2 * width)
    real_row = jnp.concatenate([vector[:, 0], -vector[:, 1]], axis=1)
    imag_row = jnp.concatenate([vector[:, 1], vector[:, 0]], axis=1)
    stacked = jnp.stack([real_row, imag_row], axis=1).reshape(-1, 2 * width)
    contract_dims = (((1,), (1,)), ((), ()))
    result = lax.dot_general(stacked, joined, contract_dims, preferred_element_type=jnp.float32)
    return result.reshape(vector.shape[0], 2, width)


def source_block(cells, wave, owner, width):
    cell_ids = owner * width + lax.broadcasted_iota(jnp.int32, (width,), 0)
    hit = cells[:, None] == cell_ids[None, :]
    return jnp.where(hit[:, None, :], wave[:, :, None], jnp.zeros((), jnp.float32))


def block_solve(previous, cells, wave, owner, lower_full, coupling_full):
    width = lower_full.shape[0]
    term = source_block(cells, wave, owner, width)
    reduced = (term - complex_apply(previous, coupling_full)).astype(jnp.bfloat16)
    return complex_apply(reduced, lower_full)


def per_device(
    lower_inverse,
    coupling,
    source_cell,
    source_wave,
    inflow_field,
    receiver_cell,
    observed,
    adjoint,
):
    owner = lax.axis_index("fac")
    fac_count = lax.axis_size("fac")
    width = lower_inverse.shape[3]
    sources = source_cell.shape[0]
    whole_lower, whole_coupling = (
        lax.all_gather(lower_inverse, "src", axis=1, tiled=True),
        lax.all_gather(coupling, "src", axis=1, tiled=True),
    )
    lower_full = whole_lower[0]
    coupling_full = whole_coupling[0]
    empty_field = jnp.zeros((sources, 2, width), jnp.float32)

    def section_step(section, carry):
        current, received = carry

        def compute():
            return block_solve(received, source_cell, source_wave, owner, lower_full, coupling_full)

        def unchanged():
            return current

        current = lax.cond(section == owner, compute, unchanged)
        received = from_behind(current.astype(jnp.bfloat16), "fac", 1)
        return (current, received)

    current, received = lax.fori_loop(0, fac_count, section_step, (empty_field, inflow_field))
    local_ids = receiver_cell - owner * width
    inside = (local_ids >= 0) & (local_ids < width)
    clipped = jnp.clip(local_ids, 0, width - 1)
    index_both = jnp.broadcast_to(clipped[:, None, :], observed.shape)
    values = jnp.take_along_axis(current, index_both, axis=2)
    values = jnp.where(inside[:, None, :], values, jnp.zeros((), jnp.float32))
    picked = lax.psum(values.astype(jnp.bfloat16), "fac").astype(jnp.float32)
    scale = 1.0 / math.sqrt(sources * lax.axis_size("src"))
    terms = jnp.sum(current * adjoint[:, 0].astype(jnp.float32), axis=(0, 1)) * scale
    gradient = lax.psum_scatter(terms[None, :], "src", scatter_dimension=1, tiled=True)
    return (current[:, None], picked - observed, gradient)


def solution(mesh):
    placed = (
        P("fac", "src", None, None),
        P("fac", "src", None, None),
        P("src"),
        P("src", None),
        P("src", None, None),
        P("src", None),
        P("src", None, None),
        P("src", "fac", None, None),
    )
    return jax.shard_map(
        per_device,
        mesh=mesh,
        in_specs=placed,
        out_specs=(P("src", "fac", None, None), P("src", None, None), P("fac", "src")),
        check_vma=False,
    )
```

profile of v0, /device:TPU:6, one launch (start us, length us, event | category | flops | bytes accessed | tf_op | source)
XLA Modules:
  0.0 1569.2 jit_solution(6800192813153071421)
XLA Ops:
  7.2 0.0 all-gather.5.cloned.1.call-start
  7.2 0.7 all-gather.5.cloned.1.call-update
  7.9 0.0 all-gather.3.cloned.1.call-start
  7.9 0.7 all-gather.3.cloned.1.call-update
  8.6 0.0 reduce-scatter.4.cloned.1.call-start
  8.7 1.1 copy.19
  9.9 0.9 broadcast_add_fusion
  10.7 0.9 compare_and_fusion
  11.6 0.2 shift-left_or_fusion
  11.8 136.4 %all-gather.5.cloned.1.call-done = bf16[1,1024,2,1024]{3,2,0,1:T(2,128)(2,1)} async-done(((bf16[1,16,2,1024]{3,2,0,1:T(2,128)(2,1)}), bf16[1,1024,2,1024]{3,2,0,1:T(2,128)(2,1)}) %all-gather.5.cloned.1.call-update) | async-done | bytes 4194320 | tf_op jit(solution)/shard_map/all_gather | solution.py:54
  148.2 127.0 %all-gather.3.cloned.1.call-done = bf16[1,1024,2,1024]{3,2,0,1:T(2,128)(2,1)} async-done(((bf16[1,16,2,1024]{3,2,0,1:T(2,128)(2,1)}), bf16[1,1024,2,1024]{3,2,0,1:T(2,128)(2,1)}) %all-gather.3.cloned.1.call-update) | async-done | bytes 4194320 | tf_op jit(solution)/shard_map/all_gather | solution.py:55
  275.2 0.1 broadcast_in_dim.64
  275.3 221.2 %while.18 = (s32[]{:T(128)}, f32[128,2,1024]{2,0,1:T(8,128)S(1)}, bf16[128,2,1024]{2,0,1:T(8,128)(2,1)S(1)}, s32[]{:T(128)}, s32[128]{0:T(128)}, /*index=5*/f32[...) while((s32[]{:T(128)}, f32[128,2,1024]{2,0,1:T(8,128)S(1)}, ...), condition=%wide.region_3.4_spmd, body=%wide.region_0.3_spmd.sunk | while | flops 2154169344 | bytes 39597816 | solution.py:74
  275.3 23.8 %conditional.2 = (f32[128,2,1024]{2,0,1:T(8,128)S(1)}) conditional(s32[]{:T(128)} %convert_element_type.39, f32[128,2,1024]{2,0,1:T(8,128)S(1)} %get-tuple-element.280, (s32[128]{0:T(128)}, s32[]{:T(128)}, f32[128,2]{0,1:T(2,128)}, bf16[128,2,1024]{2,0,1:T(8,128)(2,1)S(1)}, bf16[1,1024,2,1024]{3,2,1,0:T(2,128)(2,1)}, ...), branch_computations={%region_1.0_spmd, %region_2.2_spmd} | conditional | flops 2153907200 | bytes 35927604 | solution.py:70
  275.3 0.8 broadcast_compare_fusion
  276.2 0.1 maximum_bitcast_fusion
  276.3 0.0 copy-start.2
  276.3 7.8 reshape.71
  284.1 0.0 copy-done.2
  284.1 3.5 fusion
  287.7 0.1 maximum_bitcast_fusion.2
  287.8 7.8 reshape.72
  295.6 3.5 fusion.4
  299.1 0.1 convert_element_type.40
  299.2 1.3 collective-permute-start
  300.5 11.8 collective-permute-done
  312.3 0.1 convert_element_type.40
  312.4 28.2 %collective-permute-start = (bf16[128,2,1024]{2,0,1:T(8,128)(2,1)S(1)}, bf16[128,2,1024]{2,0,1:T(8,128)(2,1)S(1)}, u32[]{:S(2)}, u32[]{:S(2)}) collective-permute-start(bf16[128,2,1024]{2,0,1:T(8,128)(2,1)S(1)} %convert_element_type.40), channel_id=1, source_target_pairs={{0,1},{1,2},{2,3},{3,4},{4,5},{5,6},{6,7},{8,9},{9,10},{10,11},{11... | collective-permute-start | bytes 1572872 | tf_op jit(solution)/shard_map/while/body/eval_jaxpr/ppermute | solution.py:12
  340.6 11.1 collective-permute-done
  351.7 0.1 convert_element_type.40
  351.7 4.4 collective-permute-start
  356.2 10.2 collective-permute-done
  366.3 0.1 convert_element_type.40
  366.4 26.3 %collective-permute-start = (bf16[128,2,1024]{2,0,1:T(8,128)(2,1)S(1)}, bf16[128,2,1024]{2,0,1:T(8,128)(2,1)S(1)}, u32[]{:S(2)}, u32[]{:S(2)}) collective-permute-start(bf16[128,2,1024]{2,0,1:T(8,128)(2,1)S(1)} %convert_element_type.40), channel_id=1, source_target_pairs={{0,1},{1,2},{2,3},{3,4},{4,5},{5,6},{6,7},{8,9},{9,10},{10,11},{11... | collective-permute-start | bytes 1572872 | tf_op jit(solution)/shard_map/while/body/eval_jaxpr/ppermute | solution.py:12
  392.7 9.6 collective-permute-done
  402.3 0.1 convert_element_type.40
  402.4 4.4 collective-permute-start
  406.8 8.6 collective-permute-done
  415.5 0.1 convert_element_type.40
  415.5 26.6 %collective-permute-start = (bf16[128,2,1024]{2,0,1:T(8,128)(2,1)S(1)}, bf16[128,2,1024]{2,0,1:T(8,128)(2,1)S(1)}, u32[]{:S(2)}, u32[]{:S(2)}) collective-permute-start(bf16[128,2,1024]{2,0,1:T(8,128)(2,1)S(1)} %convert_element_type.40), channel_id=1, source_target_pairs={{0,1},{1,2},{2,3},{3,4},{4,5},{5,6},{6,7},{8,9},{9,10},{10,11},{11... | collective-permute-start | bytes 1572872 | tf_op jit(solution)/shard_map/while/body/eval_jaxpr/ppermute | solution.py:12
  442.1 8.0 collective-permute-done
  450.1 0.1 convert_element_type.40
  450.2 4.4 collective-permute-start
  454.6 7.1 collective-permute-done
  461.7 0.1 convert_element_type.40
  461.8 28.0 %collective-permute-start = (bf16[128,2,1024]{2,0,1:T(8,128)(2,1)S(1)}, bf16[128,2,1024]{2,0,1:T(8,128)(2,1)S(1)}, u32[]{:S(2)}, u32[]{:S(2)}) collective-permute-start(bf16[128,2,1024]{2,0,1:T(8,128)(2,1)S(1)} %convert_element_type.40), channel_id=1, source_target_pairs={{0,1},{1,2},{2,3},{3,4},{4,5},{5,6},{6,7},{8,9},{9,10},{10,11},{11... | collective-permute-start | bytes 1572872 | tf_op jit(solution)/shard_map/while/body/eval_jaxpr/ppermute | solution.py:12
  489.8 6.6 collective-permute-done
  496.4 0.0 copy-start
  496.5 310.7 %gather_fusion = bf16[32768]{0:T(1024)(128)(2,1)S(1)} fusion(f32[128,2,1024]{2,0,1:T(8,128)S(1)} %get-tuple-element.168, s32[32768]{0:T(1024)S(1)} %bitcast.40), kind=kCustom, calls=%fused_computation | custom fusion | bytes 524288 | tf_op jit(solution)/shard_map/jit(take_along_axis)/gather | solution.py:79
  807.1 0.0 copy-done
  807.2 0.0 copy-start.1
  807.2 0.2 fusion.12
  807.4 1.0 copy.24
  808.4 0.0 reduce-scatter.4.cloned.1.call-update
  808.4 0.0 all-reduce.2.cloned.1.call-start
  808.5 0.9 fusion.14
  809.4 0.0 all-reduce.2.cloned.1.call-update
  809.4 1.8 copy.28
  811.2 595.6 %reduce-scatter.4.cloned.1.call-done = f32[16,1]{1,0:T(8,128)} async-done(((f32[1024,1]{1,0:T(8,128)}), f32[16,1]{1,0:T(8,128)}) %reduce-scatter.4.cloned.1.call-update) | async-done | bytes 80
  1406.7 1.3 copy.25
  1408.0 153.1 %all-reduce.2.cloned.1.call-done = bf16[128,2,128]{2,1,0:T(2,128)(2,1)} async-done(((bf16[128,2,128]{2,1,0:T(2,128)(2,1)}), bf16[128,2,128]{2,1,0:T(2,128)(2,1)}) %all-reduce.2.cloned.1.call-update) | async-done | bytes 65552 | tf_op jit(solution)/shard_map/psum | solution.py:81
  1561.1 0.0 copy-done.1
  1561.1 1.5 convert_subtract_fusion
  (13 shorter events, 0.1 us)
Async XLA Ops:
  7.2 141.0 %all-gather.5.cloned.1.call-start = ((), (), s32[]{:S(2)}) async-start(), calls=%async_computation.2 | async-start | bytes 4259840 | tf_op jit(solution)/shard_map/all_gather | solution.py:54
  7.9 267.3 %all-gather.3.cloned.1.call-start = ((), (), s32[]{:S(2)}) async-start(), calls=%async_computation.1 | async-start | bytes 4259840 | tf_op jit(solution)/shard_map/all_gather | solution.py:55
  8.6 1398.1 %reduce-scatter.4.cloned.1.call-start = ((), (), s32[]{:S(2)}) async-start(), calls=%async_computation.4 | async-start | bytes 532480
  276.3 7.8 copy-start.2
  299.2 13.2 collective-permute-start
  312.4 39.2 %collective-permute-start = (bf16[128,2,1024]{2,0,1:T(8,128)(2,1)S(1)}, bf16[128,2,1024]{2,0,1:T(8,128)(2,1)S(1)}, u32[]{:S(2)}, u32[]{:S(2)}) collective-permute-start(bf16[128,2,1024]{2,0,1:T(8,128)(2,1)S(1)} %convert_element_type.40), channel_id=1, source_target_pairs={{0,1},{1,2},{2,3},{3,4},{4,5},{5,6},{6,7},{8,9},{9,10},{10,11},{11... | collective-permute-start | bytes 1572872 | tf_op jit(solution)/shard_map/while/body/eval_jaxpr/ppermute | solution.py:12
  351.7 14.6 collective-permute-start
  366.4 35.9 %collective-permute-start = (bf16[128,2,1024]{2,0,1:T(8,128)(2,1)S(1)}, bf16[128,2,1024]{2,0,1:T(8,128)(2,1)S(1)}, u32[]{:S(2)}, u32[]{:S(2)}) collective-permute-start(bf16[128,2,1024]{2,0,1:T(8,128)(2,1)S(1)} %convert_element_type.40), channel_id=1, source_target_pairs={{0,1},{1,2},{2,3},{3,4},{4,5},{5,6},{6,7},{8,9},{9,10},{10,11},{11... | collective-permute-start | bytes 1572872 | tf_op jit(solution)/shard_map/while/body/eval_jaxpr/ppermute | solution.py:12
  402.4 13.1 collective-permute-start
  415.5 34.6 %collective-permute-start = (bf16[128,2,1024]{2,0,1:T(8,128)(2,1)S(1)}, bf16[128,2,1024]{2,0,1:T(8,128)(2,1)S(1)}, u32[]{:S(2)}, u32[]{:S(2)}) collective-permute-start(bf16[128,2,1024]{2,0,1:T(8,128)(2,1)S(1)} %convert_element_type.40), channel_id=1, source_target_pairs={{0,1},{1,2},{2,3},{3,4},{4,5},{5,6},{6,7},{8,9},{9,10},{10,11},{11... | collective-permute-start | bytes 1572872 | tf_op jit(solution)/shard_map/while/body/eval_jaxpr/ppermute | solution.py:12
  450.2 11.5 collective-permute-start
  461.8 34.7 %collective-permute-start = (bf16[128,2,1024]{2,0,1:T(8,128)(2,1)S(1)}, bf16[128,2,1024]{2,0,1:T(8,128)(2,1)S(1)}, u32[]{:S(2)}, u32[]{:S(2)}) collective-permute-start(bf16[128,2,1024]{2,0,1:T(8,128)(2,1)S(1)} %convert_element_type.40), channel_id=1, source_target_pairs={{0,1},{1,2},{2,3},{3,4},{4,5},{5,6},{6,7},{8,9},{9,10},{10,11},{11... | collective-permute-start | bytes 1572872 | tf_op jit(solution)/shard_map/while/body/eval_jaxpr/ppermute | solution.py:12
  496.4 310.7 %copy-start = (bf16[128,1,2,1024]{3,2,1,0:T(2,128)(2,1)S(1)}, bf16[128,1,2,1024]{3,2,1,0:T(2,128)(2,1)}, u32[]{:S(2)}) copy-start(bf16[128,1,2,1024]{3,2,1,0:T(2,128)(2,1)} %param.19) | copy-start | bytes 1572868
  807.2 754.0 %copy-start.1 = (f32[128,2,128]{2,1,0:T(2,128)S(1)}, f32[128,2,128]{2,1,0:T(2,128)}, u32[]{:S(2)}) copy-start(f32[128,2,128]{2,1,0:T(2,128)} %param.18) | copy-start | bytes 393220
  808.4 752.7 %all-reduce.2.cloned.1.call-start = ((), (), s32[]{:S(2)}) async-start(), calls=%async_computation.3 | async-start | bytes 131072 | tf_op jit(solution)/shard_map/psum | solution.py:81
Sparse Core Ops, SparseCore 0:
  12.4 135.6 all-gather.4
  152.6 122.5 all-gather.2
  808.6 598.1 reduce-scatter.3
  1410.3 150.7 all-reduce.1
where the time goes:
time: 1570 us
  waiting for transfers between devices  1090 us (69%)
  local copies, waits for them, and re-layouts  332 us (21%)
  starting transfers between devices  124 us (8%)
    unnamed x5, waiting for transfers between devices  597 us
    gather x1, local copies, waits for them, and re-layouts, per_device(): values = jnp.take_along_axis(current, index_both, axis=2)  311 us
    psum x1, waiting for transfers between devices, per_device(): picked = lax.psum(values.astype(jnp.bfloat16), 'fac').astype(jnp.float32)  153 us
    all_gather x1, waiting for transfers between devices, per_device(): lax.all_gather(lower_inverse, 'src', axis=1, tiled=True)  136 us
    all_gather x1, waiting for transfers between devices, per_device(): lax.all_gather(coupling, 'src', axis=1, tiled=True)  127 us
    ppermute x8, starting transfers between devices, from_behind(): return lax.ppermute(shard, axis, pairs)  124 us
    ppermute x8, waiting for transfers between devices, from_behind(): return lax.ppermute(shard, axis, pairs)  73 us
  transfers between devices with their start and end apart: 12, of which 12 were waited for; matrix products, arithmetic and copies ran while one was open for 0% of the time, Pallas kernels for 0%

commit v1 on v0

v1 whole, which is shorter than its diff:
```python
import functools
import math

import jax
import jax.numpy as jnp
from jax import lax
from jax.experimental import pallas as pl
from jax.experimental.pallas import tpu as pltpu
from jax.sharding import Mesh, PartitionSpec as P

SRC = ("zh", "y", "x", "c")
CHUNKS = 4
GROUP = 256
LIMIT = 16 << 20
F32, BF16 = jnp.float32, jnp.bfloat16
NT = (((1,), (1,)), ((), ()))


def dot_nt(rows, block):
    return lax.dot_general(rows, block, NT, preferred_element_type=F32)


def group_block(w_ref, group, part, low, high):
    half = group // 2
    tiles = [
        w_ref[c, half, 4 * y + x, part, :, low:high]
        for y in (2 * (group % 2), 2 * (group % 2) + 1)
        for x in range(4)
        for c in range(2)
    ]
    return jnp.concatenate(tiles, axis=0)


def stage_kernel(step, chunks, sc_ref, x_ref, inflow_ref, cells_ref, wave_ref, w_ref, y_ref, field_ref, _w, v_ref):
    owner = sc_ref[0]
    chunk = step - owner
    m, width = x_ref.shape[1], x_ref.shape[2]
    groups = width // GROUP

    @pl.when((chunk >= 0) & (chunk < chunks))
    def _():
        @pl.when(owner == 0)
        def _():
            v_ref[:, 0 : 2 * m] = inflow_ref[...].reshape(1, 2 * m, width)

        @pl.when(owner != 0)
        def _():
            v_ref[:, 0 : 2 * m] = x_ref[...].reshape(1, 2 * m, width)

        straight = v_ref[0]
        crossed = jnp.concatenate([-straight[m:], straight[:m]], axis=0)
        cells = cells_ref[chunk] - owner * width
        waves = wave_ref[chunk]
        lanes = lax.broadcasted_iota(jnp.int32, (m, GROUP), 1)
        reduced = []
        for g in range(groups):
            low = GROUP * g
            acc = dot_nt(straight[:, low:], group_block(w_ref, g, 0, low + GROUP, width + GROUP))
            acc += dot_nt(crossed[:, low:], group_block(w_ref, g, 1, low + GROUP, width + GROUP))
            hit = lanes + low == cells
            term = jnp.concatenate([jnp.where(hit, waves[:, p : p + 1], 0.0) for p in range(2)], axis=0)
            reduced.append((term - acc).astype(BF16))
        straight = jnp.concatenate(reduced, axis=1)
        crossed = jnp.concatenate([-straight[m:], straight[:m]], axis=0)
        for g in range(groups):
            low, high = GROUP * g, GROUP * (g + 1)
            acc = dot_nt(straight[:, :high], group_block(w_ref, g, 0, 0, high))
            acc += dot_nt(crossed[:, :high], group_block(w_ref, g, 1, 0, high))
            acc = acc.reshape(2, m, GROUP)
            field_ref[:, :, low:high] = acc
            y_ref[:, :, low:high] = acc.astype(BF16)


def post_kernel(step, chunks, sc_ref, field_ref, adjoint_ref, cells_ref, _w, _p, _g, wave_out, picked_out, grad_out):
    owner = sc_ref[0]
    chunk = step - owner
    m, width = field_ref.shape[1], field_ref.shape[2]

    @pl.when((chunk >= 0) & (chunk < chunks))
    def _():
        field = field_ref[...]
        wave_out[chunk] = field
        prod = field * adjoint_ref[chunk].astype(F32)
        grad_out[...] += jnp.sum(prod.reshape(2 * m // 8, 8, width), axis=0)
        local = cells_ref[chunk] - owner * width
        tile, lane = local >> 7, local & 127
        for p in range(2):
            got = jnp.zeros((m, 128), F32)
            for t in range(width // 128):
                part = field_ref[p, :, 128 * t : 128 * (t + 1)]
                part = jnp.take_along_axis(part, lane, axis=1, mode="promise_in_bounds")
                got = jnp.where(tile == t, part, got)
            picked_out[chunk, p] = got


def place_kernel(sc_ref, own_ref, own_other_ref, far_ref, far_other_ref, out_ref, sems):
    half, core = sc_ref[1], sc_ref[2]
    pieces = (
        (own_ref, core, half),
        (own_other_ref, 1 - core, half),
        (far_ref, core, 1 - half),
        (far_other_ref, 1 - core, 1 - half),
    )
    copies = [
        pltpu.make_async_copy(ref, out_ref.at[c, h], sems.at[i]) for i, (ref, c, h) in enumerate(pieces)
    ]
    for copy in copies:
        copy.start()
    for copy in copies:
        copy.wait()


def swap(array, axis):
    return lax.ppermute(array, axis, [(0, 1), (1, 0)])


def plane_gather(piece):
    plane = lax.axis_size(("y", "x"))
    spread = jnp.broadcast_to(piece[None], (plane,) + piece.shape)
    return lax.all_to_all(spread, ("y", "x"), 0, 0, tiled=True)


def gather_factor(packed, where):
    far = swap(packed, "zh")
    own = plane_gather(packed)
    own_other = swap(own, "c")
    own, far = lax.optimization_barrier((own, far))
    far = plane_gather(far)
    far_other = swap(far, "c")
    anywhere = pl.BlockSpec(memory_space=pl.ANY)
    return pl.pallas_call(
        place_kernel,
        out_shape=pltpu.VMEM((2, 2) + own.shape, own.dtype),
        in_specs=[pl.BlockSpec(memory_space=pltpu.SMEM)] + [anywhere] * 4,
        out_specs=pl.BlockSpec(memory_space=pltpu.VMEM),
        scratch_shapes=[pltpu.SemaphoreType.DMA((4,))],
        compiler_params=pltpu.CompilerParams(vmem_limit_bytes=LIMIT),
        name="place",
    )(where, own, own_other, far, far_other)


def per_device(lower, coupling, source_cell, source_wave, inflow, receiver_cell, observed, adjoint):
    owner = lax.axis_index("fac")
    stages = lax.axis_size("fac")
    src = lax.axis_index(SRC)
    width = lower.shape[3]
    rows = lower.shape[1]
    sources = source_cell.shape[0]
    m = sources // CHUNKS

    split = (src // (GROUP // rows) + 1) * GROUP
    low = jnp.pad(lower[0].transpose(1, 0, 2), ((0, 0), (0, 0), (0, GROUP)))
    high = jnp.pad(coupling[0].transpose(1, 0, 2), ((0, 0), (0, 0), (GROUP, 0)))
    packed = jnp.where(lax.broadcasted_iota(jnp.int32, low.shape, 2) < split, low, high)
    where = jnp.stack([owner, lax.axis_index("zh"), lax.axis_index("c")])
    factor = gather_factor(packed, where)

    def by_chunk(array):
        return array.reshape((CHUNKS, m) + array.shape[1:])

    inflow = by_chunk(inflow).transpose(0, 2, 1, 3)
    adjoint = by_chunk(adjoint[:, 0]).transpose(0, 2, 1, 3)
    observed = by_chunk(observed).transpose(0, 2, 1, 3)
    cells, waves, receivers = by_chunk(source_cell[:, None]), by_chunk(source_wave), by_chunk(receiver_cell)

    vmem = pl.BlockSpec(memory_space=pltpu.VMEM)
    smem = pl.BlockSpec(memory_space=pltpu.SMEM)
    stage = lambda t: pl.pallas_call(
        functools.partial(stage_kernel, t, CHUNKS),
        out_shape=(
            pltpu.VMEM((2, m, width), BF16),
            pltpu.VMEM((2, m, width), F32),
            pltpu.VMEM(factor.shape, BF16),
        ),
        in_specs=[smem] + [vmem] * 5,
        out_specs=(vmem, vmem, vmem),
        input_output_aliases={5: 2},
        scratch_shapes=[pltpu.VMEM((1, 2 * m, width), BF16)],
        cost_estimate=pl.CostEstimate(
            flops=int(2 * 2 * 2 * m * 2 * width * width * 0.625),
            bytes_accessed=4 * width * (width + GROUP),
            transcendentals=0,
        ),
        compiler_params=pltpu.CompilerParams(vmem_limit_bytes=LIMIT),
        name="stage",
    )
    post = lambda t: pl.pallas_call(
        functools.partial(post_kernel, t, CHUNKS),
        out_shape=(
            pltpu.VMEM((CHUNKS, 2, m, width), F32),
            pltpu.VMEM((CHUNKS, 2, m, receivers.shape[2]), F32),
            pltpu.VMEM((8, width), F32),
        ),
        in_specs=[smem] + [vmem] * 6,
        out_specs=(vmem, vmem, vmem),
        input_output_aliases={4: 0, 5: 1, 6: 2},
        cost_estimate=pl.CostEstimate(flops=8 * m * width, bytes_accessed=24 * m * width, transcendentals=0),
        compiler_params=pltpu.CompilerParams(vmem_limit_bytes=LIMIT),
        name="post",
    )
    field_all = jnp.zeros((CHUNKS, 2, m, width), F32)
    picked = jnp.zeros((CHUNKS, 2, m, receivers.shape[2]), F32)
    grad = jnp.zeros((8, width), F32)
    x = jnp.zeros((2, m, width), BF16)
    steps = CHUNKS + stages - 1
    for t in range(steps):
        y, field, factor = stage(t)(where, x, inflow[min(t, CHUNKS - 1)], cells, waves, factor)
        pairs = [(i, i + 1) for i in range(stages - 1) if 0 <= t - i < CHUNKS]
        if pairs:
            x = lax.ppermute(y, "fac", pairs)
        field_all, picked, grad = post(t)(where, field, adjoint, receivers, field_all, picked, grad)
        x, field_all, picked, grad = lax.optimization_barrier((x, field_all, picked, grad))

    picked = picked.astype(BF16)
    step = stages // 2
    while step:
        picked = picked + lax.ppermute(picked, "fac", [(i, i ^ step) for i in range(stages)])
        step //= 2
    residual = (picked.astype(F32) - observed).transpose(0, 2, 1, 3).reshape(sources, 2, -1)
    shards = lax.axis_size(SRC)
    scale = 1.0 / math.sqrt(sources * shards)
    terms = (jnp.sum(grad, axis=0) * scale).reshape(shards, rows)
    terms = lax.all_to_all(terms, SRC, 0, 0, tiled=True)
    gradient = jnp.sum(terms, axis=0)[None]
    wavefield = field_all.transpose(0, 2, 1, 3).reshape(sources, 1, 2, width)
    return wavefield, residual, gradient


def solution(mesh):
    grid = Mesh(mesh.devices.reshape(2, 4, 4, 2, -1), SRC + ("fac",))
    placed = (
        P("fac", SRC, None, None),
        P("fac", SRC, None, None),
        P(SRC),
        P(SRC, None),
        P(SRC, None, None),
        P(SRC, None),
        P(SRC, None, None),
        P(SRC, "fac", None, None),
    )
    return jax.shard_map(
        per_device,
        mesh=grid,
        in_specs=placed,
        out_specs=(P(SRC, "fac", None, None), P(SRC, None, None), P("fac", SRC)),
        check_vma=False,
    )
```

time: 1570 us -> 212 us (0.14)
  waiting for transfers between devices: 1090 us -> 44.7 us
  local copies, waits for them, and re-layouts: 332 us -> 6.51 us
  Pallas kernels: 0 us -> 23.9 us
    unnamed x5 -> x0, waiting for transfers between devices: 597 us -> none
    gather x1 -> x0, local copies, waits for them, and re-layouts: 311 us -> none  [per_device(): values = jnp.take_along_axis(current, index_both, axis=2)]
    all_gather x2 -> x0, waiting for transfers between devices: 263 us -> none  [the longest x1 136 us: per_device(): lax.all_gather(lower_inverse, 'src', axis=1, tiled=True)]
    psum x1 -> x0, waiting for transfers between devices: 153 us -> none  [per_device(): picked = lax.psum(values.astype(jnp.bfloat16), 'fac').astype(jnp.float32)]
    ppermute x8 -> x16, waiting for transfers between devices: 73 us -> 17 us  [the longest x10 7.06 us: per_device(): x = lax.ppermute(y, 'fac', pairs)]
    all_to_all x0 -> x3, starting transfers between devices: none -> 35.5 us  [the longest x1 18.9 us: per_device(): terms = lax.all_to_all(terms, SRC, 0, 0, tiled=True)]
    ppermute x8 -> x16, starting transfers between devices: 124 us -> 94.7 us  [the longest x3 57.8 us: per_device(): lax.ppermute(picked, 'fac', [(i, i ^ step) for i in range(stages)])]
    all_to_all x0 -> x3, waiting for transfers between devices: none -> 27.8 us  [the longest x2 14 us: plane_gather(): return lax.all_to_all(spread, ('y', 'x'), 0, 0, tiled=True)]
  transfers between devices with their start and end apart: 12 -> 19, of which waited for: 12 -> 10; matrix products, arithmetic and copies ran while one was open for 0% -> 2% of each run, Pallas kernels for 0% -> 3%
where the time goes in v1:
time: 212 us; the launch traced here: 208 us
  starting transfers between devices  130 us (61%)
  waiting for transfers between devices  44.7 us (21%)
  Pallas kernels  23.9 us (11%)
  local copies, waits for them, and re-layouts  6.51 us (3%)
    ppermute x3, starting transfers between devices, per_device(): lax.ppermute(picked, 'fac', [(i, i ^ step) for i in range(stages)])  57.8 us
    ppermute x10, starting transfers between devices, per_device(): x = lax.ppermute(y, 'fac', pairs)  19.3 us
    all_to_all x1, starting transfers between devices, per_device(): terms = lax.all_to_all(terms, SRC, 0, 0, tiled=True)  18.9 us
    ppermute x3, starting transfers between devices, swap(): return lax.ppermute(array, axis, [(0, 1), (1, 0)])  17.6 us
    all_to_all x2, starting transfers between devices, plane_gather(): return lax.all_to_all(spread, ('y', 'x'), 0, 0, tiled=True)  16.6 us
    pallas_call x11, Pallas kernels, per_device(): stage(t)(where, x, inflow[min(t, CHUNKS - 1)], cells, waves, factor)  14.1 us
    all_to_all x2, waiting for transfers between devices, plane_gather(): return lax.all_to_all(spread, ('y', 'x'), 0, 0, tiled=True)  14 us
    all_to_all x1, waiting for transfers between devices, per_device(): terms = lax.all_to_all(terms, SRC, 0, 0, tiled=True)  13.7 us
  transfers between devices with their start and end apart: 19, of which 10 were waited for; matrix products, arithmetic and copies ran while one was open for 2% of the time, Pallas kernels for 3%

profile of v1, /device:TPU:6, one launch (start us, length us, event | category | flops | bytes accessed | tf_op | source)
XLA Modules:
  0.0 208.4 jit_solution(10937064855023943283)
XLA Ops:
  0.7 1.0 broadcast_select_fusion
  1.8 1.2 broadcast_in_dim.28
  3.0 9.4 %all-to-all-start = ((bf16[16,2,16,1280]{3,2,1,0:T(8,128)(2,1)}), bf16[16,2,16,1280]{3,2,1,0:T(8,128)(2,1)S(1)}, u32[]{:S(2)}, u32[]{:S(2)}) async-start(bf16[16,2,16,1280]{3,2,1,0:T(8,128)(2,1)} %broadcast_in_dim.28), calls=%async_computation | async-start | bytes 2621440 | tf_op jit(solution)/shard_map/all_to_all | solution.py:120
  12.4 13.8 %collective-permute-start = (bf16[2,16,1280]{2,0,1:T(2,128)(2,1)S(1)}, bf16[2,16,1280]{2,0,1:T(2,128)(2,1)S(1)}, u32[]{:S(2)}, u32[]{:S(2)}) collective-permute-start(bf16[2,16,1280]{2,0,1:T(2,128)(2,1)S(1)} %broadcast_select_fusion), channel_id=1, source_target_pairs={{0,256},{256,0},{1,257},{257,1},{2,258},{258,2},{3,259},{259,3},{4... | collective-permute-start | bytes 245768 | tf_op jit(solution)/shard_map/ppermute | solution.py:114
  26.1 2.7 %collective-permute-done = bf16[2,16,1280]{2,0,1:T(2,128)(2,1)S(1)} collective-permute-done((bf16[2,16,1280]{2,0,1:T(2,128)(2,1)S(1)}, bf16[2,16,1280]{2,0,1:T(2,128)(2,1)S(1)}, u32[]{:S(2)}, u32[]{:S(2)}) %collective-permute-start) | collective-permute-done | bytes 81952 | tf_op jit(solution)/shard_map/ppermute | solution.py:114
  28.9 1.2 broadcast_in_dim.29
  30.1 7.2 %all-to-all-start.1 = ((bf16[16,2,16,1280]{3,2,1,0:T(8,128)(2,1)}), bf16[16,2,16,1280]{3,2,1,0:T(8,128)(2,1)}, u32[]{:S(2)}, u32[]{:S(2)}) async-start(bf16[16,2,16,1280]{3,2,1,0:T(8,128)(2,1)} %broadcast_in_dim.29), calls=%async_computation.1 | async-start | bytes 2621440 | tf_op jit(solution)/shard_map/all_to_all | solution.py:120
  37.3 1.9 collective-permute-start.1
  39.2 14.0 %all-to-all-done.1.far_ref = bf16[16,2,16,1280]{3,2,1,0:T(8,128)(2,1)} async-done(((bf16[16,2,16,1280]{3,2,1,0:T(8,128)(2,1)}), bf16[16,2,16,1280]{3,2,1,0:T(8,128)(2,1)}, u32[]{:S(2)}, u32[]{:S(2)}) %all-to-all-start.1) | async-done | bytes 1310752 | tf_op jit(solution)/shard_map/all_to_all | solution.py:120
  53.2 1.9 collective-permute-start.2
  55.2 0.1 copy.95
  55.3 0.2 reshape_broadcast_in_dim.4.cells_ref
  55.5 0.1 copy.128
  55.7 2.8 %collective-permute-done.2.far_other_ref = bf16[16,2,16,1280]{3,2,1,0:T(8,128)(2,1)} collective-permute-done((bf16[16,2,16,1280]{3,2,1,0:T(8,128)(2,1)}, bf16[16,2,16,1280]{3,2,1,0:T(8,128)(2,1)}, u32[]{:S(2)}, u32[]{:S(2)}) %collective-permute-start.2) | collective-permute-done | bytes 1310752 | tf_op jit(solution)/shard_map/ppermute | solution.py:114
  58.5 2.8 %place.1.w_ref = bf16[2,2,16,2,16,1280]{5,4,3,2,1,0:T(8,128)(2,1)S(1)} custom-call(s32[3]{0:T(128)S(1)} %pad_add_fusion.sc_ref, bf16[16,2,16,1280]{3,2,1,0:T(8,128)(2,1)S(1)} %all-to-all-done.own_ref, bf16[16,2,16,1280]{3,2,1,0:T(8,128)(2,1)} %collective-permute-done.1.own_other_ref, bf16[16,2,16,1280]{3,2,1,0:T(8,128)(2,1)} %all-to-all-done.1.far_ref, ...), custom_call_target="tpu_custom_call" | custom-call | tf_op jit(solution)/shard_map/place/pallas_call | solution.py:131
  61.3 2.4 %stage.11 = (bf16[2,32,1024]{2,1,0:T(8,128)(2,1)S(1)}, f32[2,32,1024]{2,1,0:T(8,128)S(1)}, bf16[2,2,16,2,16,1280]{5,4,3,2,1,0:T(8,128)(2,1)S(1)}) custom-call(s32[3]{0:T(128)S(1)} %pad_add_fusion.sc_ref, bf16[2,32,1024]{2,1,0:T(8,128)(2,1)S(1)} %broadcast_in_dim.27.x_ref, ...), custom_call_target="tpu_custom_call", output_to_operand_aliasing={{2}: (5, {})} | custom-call | flops 335544320 | bytes 5242880 | tf_op jit(solution)/shard_map/stage/pallas_call | solution.py:207
  63.7 2.1 %collective-permute-start.3 = (bf16[2,32,1024]{2,1,0:T(8,128)(2,1)S(1)}, bf16[2,32,1024]{2,1,0:T(8,128)(2,1)S(1)}, u32[]{:S(2)}, u32[]{:S(2)}) collective-permute-start(bf16[2,32,1024]{2,1,0:T(8,128)(2,1)S(1)} %get-tuple-element.114), channel_id=1, source_target_pairs={{0,1},{8,9},{16,17},{24,25},{32,33},{40,41},{48,49},{56,57},{64,65... | collective-permute-start | bytes 393224 | tf_op jit(solution)/shard_map/ppermute | solution.py:210
  65.8 0.1 copy.127
  65.9 0.1 broadcast_in_dim.30._w
  66.1 0.8 post.11
  66.9 1.9 collective-permute-done.3.x_ref
  68.8 2.4 %stage.12 = (bf16[2,32,1024]{2,1,0:T(8,128)(2,1)S(1)}, f32[2,32,1024]{2,1,0:T(8,128)S(1)}, bf16[2,2,16,2,16,1280]{5,4,3,2,1,0:T(8,128)(2,1)S(1)}) custom-call(s32[3]{0:T(128)S(1)} %pad_add_fusion.sc_ref, bf16[2,32,1024]{2,1,0:T(8,128)(2,1)S(1)} %collective-permute-done.3.x_ref, ...), custom_call_target="tpu_custom_call", output_to_operand_aliasing={{2}: (5, {})} | custom-call | flops 335544320 | bytes 5242880 | tf_op jit(solution)/shard_map/stage/pallas_call | solution.py:207
  71.2 4.4 %collective-permute-start.4 = (bf16[2,32,1024]{2,1,0:T(8,128)(2,1)S(1)}, bf16[2,32,1024]{2,1,0:T(8,128)(2,1)S(1)}, u32[]{:S(2)}, u32[]{:S(2)}) collective-permute-start(bf16[2,32,1024]{2,1,0:T(8,128)(2,1)S(1)} %get-tuple-element.121), channel_id=1, source_target_pairs={{0,1},{1,2},{8,9},{9,10},{16,17},{17,18},{24,25},{25,26},{32,33},{... | collective-permute-start | bytes 393224 | tf_op jit(solution)/shard_map/ppermute | solution.py:210
  75.6 0.8 post.12
  76.4 1.7 collective-permute-done.4.x_ref
  78.1 2.4 %stage.13 = (bf16[2,32,1024]{2,1,0:T(8,128)(2,1)S(1)}, f32[2,32,1024]{2,1,0:T(8,128)S(1)}, bf16[2,2,16,2,16,1280]{5,4,3,2,1,0:T(8,128)(2,1)S(1)}) custom-call(s32[3]{0:T(128)S(1)} %pad_add_fusion.sc_ref, bf16[2,32,1024]{2,1,0:T(8,128)(2,1)S(1)} %collective-permute-done.4.x_ref, ...), custom_call_target="tpu_custom_call", output_to_operand_aliasing={{2}: (5, {})} | custom-call | flops 335544320 | bytes 5242880 | tf_op jit(solution)/shard_map/stage/pallas_call | solution.py:207
  80.5 4.4 %collective-permute-start.5 = (bf16[2,32,1024]{2,1,0:T(8,128)(2,1)S(1)}, bf16[2,32,1024]{2,1,0:T(8,128)(2,1)S(1)}, u32[]{:S(2)}, u32[]{:S(2)}) collective-permute-start(bf16[2,32,1024]{2,1,0:T(8,128)(2,1)S(1)} %get-tuple-element.131), channel_id=1, source_target_pairs={{0,1},{1,2},{2,3},{8,9},{9,10},{10,11},{16,17},{17,18},{18,19},{24... | collective-permute-start | bytes 393224 | tf_op jit(solution)/shard_map/ppermute | solution.py:210
  84.8 0.8 post.13
  85.6 1.7 collective-permute-done.5.x_ref
  87.3 2.4 %stage.14 = (bf16[2,32,1024]{2,1,0:T(8,128)(2,1)S(1)}, f32[2,32,1024]{2,1,0:T(8,128)S(1)}, bf16[2,2,16,2,16,1280]{5,4,3,2,1,0:T(8,128)(2,1)S(1)}) custom-call(s32[3]{0:T(128)S(1)} %pad_add_fusion.sc_ref, bf16[2,32,1024]{2,1,0:T(8,128)(2,1)S(1)} %collective-permute-done.5.x_ref, ...), custom_call_target="tpu_custom_call", output_to_operand_aliasing={{2}: (5, {})} | custom-call | flops 335544320 | bytes 5242880 | tf_op jit(solution)/shard_map/stage/pallas_call | solution.py:207
  89.7 4.4 %collective-permute-start.6 = (bf16[2,32,1024]{2,1,0:T(8,128)(2,1)S(1)}, bf16[2,32,1024]{2,1,0:T(8,128)(2,1)S(1)}, u32[]{:S(2)}, u32[]{:S(2)}) collective-permute-start(bf16[2,32,1024]{2,1,0:T(8,128)(2,1)S(1)} %get-tuple-element.141), channel_id=1, source_target_pairs={{0,1},{1,2},{2,3},{3,4},{8,9},{9,10},{10,11},{11,12},{16,17},{17,1... | collective-permute-start | bytes 393224 | tf_op jit(solution)/shard_map/ppermute | solution.py:210
  94.1 0.8 post.14
  94.9 1.7 collective-permute-done.6.x_ref
  96.6 0.5 stage.15
  97.1 0.7 collective-permute-start.7
  97.8 0.6 post.15
  98.4 0.6 stage.16
  98.9 0.7 collective-permute-start.8
  99.6 0.6 post.16
  100.2 0.6 stage.17
  100.7 0.7 collective-permute-start.9
  101.4 0.6 post.17
  102.0 0.6 stage.18
  102.5 0.7 collective-permute-start.10
  103.2 0.6 post.18
  103.8 0.6 stage.19
  104.3 0.7 collective-permute-start.11
  105.0 0.6 post.19
  105.6 0.7 stage.20
  106.3 0.7 collective-permute-start.12
  107.0 0.6 post.20
  107.6 1.2 stage.21
  108.8 0.5 post.21
  109.4 34.2 %collective-permute-start.13 = (bf16[4,2,32,128]{3,2,1,0:T(8,128)(2,1)S(1)}, bf16[4,2,32,128]{3,2,1,0:T(8,128)(2,1)S(1)}, u32[]{:S(2)}, u32[]{:S(2)}) collective-permute-start(bf16[4,2,32,128]{3,2,1,0:T(8,128)(2,1)S(1)} %convert_element_type.10), channel_id=1, source_target_pairs={{0,4},{1,5},{2,6},{3,7},{4,0},{5,1},{6,2},{7,3},{8,12},{9,13},{10,... | collective-permute-start | bytes 196616 | tf_op jit(solution)/shard_map/ppermute | solution.py:217
  143.6 2.2 %collective-permute-done.13 = bf16[4,2,32,128]{3,2,1,0:T(8,128)(2,1)S(1)} collective-permute-done((bf16[4,2,32,128]{3,2,1,0:T(8,128)(2,1)S(1)}, bf16[4,2,32,128]{3,2,1,0:T(8,128)(2,1)S(1)}, u32[]{:S(2)}, u32[]{:S(2)}) %collective-permute-start.13) | collective-permute-done | bytes 65568 | tf_op jit(solution)/shard_map/ppermute | solution.py:217
  145.8 17.2 %collective-permute-start.14 = (bf16[4,2,32,128]{3,2,1,0:T(8,128)(2,1)S(1)}, bf16[4,2,32,128]{3,2,1,0:T(8,128)(2,1)S(1)}, u32[]{:S(2)}, u32[]{:S(2)}) collective-permute-start(bf16[4,2,32,128]{3,2,1,0:T(8,128)(2,1)S(1)} %convert_add_fusion), channel_id=1, source_target_pairs={{0,2},{1,3},{2,0},{3,1},{4,6},{5,7},{6,4},{7,5},{8,10},{9,11},{10,... | collective-permute-start | bytes 196616 | tf_op jit(solution)/shard_map/ppermute | solution.py:217
  163.1 2.2 %collective-permute-done.14 = bf16[4,2,32,128]{3,2,1,0:T(8,128)(2,1)S(1)} collective-permute-done((bf16[4,2,32,128]{3,2,1,0:T(8,128)(2,1)S(1)}, bf16[4,2,32,128]{3,2,1,0:T(8,128)(2,1)S(1)}, u32[]{:S(2)}, u32[]{:S(2)}) %collective-permute-start.14) | collective-permute-done | bytes 65568 | tf_op jit(solution)/shard_map/ppermute | solution.py:217
  165.3 6.4 %collective-permute-start.15 = (bf16[4,2,32,128]{3,2,1,0:T(8,128)(2,1)S(1)}, bf16[4,2,32,128]{3,2,1,0:T(8,128)(2,1)S(1)}, u32[]{:S(2)}, u32[]{:S(2)}) collective-permute-start(bf16[4,2,32,128]{3,2,1,0:T(8,128)(2,1)S(1)} %add.31), channel_id=1, source_target_pairs={{0,1},{1,0},{2,3},{3,2},{4,5},{5,4},{6,7},{7,6},{8,9},{9,8},{10,11... | collective-permute-start | bytes 196616 | tf_op jit(solution)/shard_map/ppermute | solution.py:217
  171.8 0.7 mul.35
  172.4 18.9 %all-to-all-start.2 = ((f32[64,1,16]{2,1,0:T(1,128)}), f32[64,1,16]{2,1,0:T(1,128)S(1)}, u32[]{:S(2)}, u32[]{:S(2)}) async-start(f32[64,1,16]{2,1,0:T(1,128)} %bitcast.23), calls=%async_computation.2 | async-start | bytes 65536 | tf_op jit(solution)/shard_map/all_to_all | solution.py:223
  191.4 1.8 copy.116
  193.2 13.7 %all-to-all-done.2 = f32[64,1,16]{2,1,0:T(1,128)S(1)} async-done(((f32[64,1,16]{2,1,0:T(1,128)}), f32[64,1,16]{2,1,0:T(1,128)S(1)}, u32[]{:S(2)}, u32[]{:S(2)}) %all-to-all-start.2) | async-done | bytes 4128 | tf_op jit(solution)/shard_map/all_to_all | solution.py:223
  207.0 0.6 reduce_sum.19
  207.6 0.8 copy.117
  (37 shorter events, 0.4 us)
Async XLA Ops:
  0.6 54.5 %copy-start.4 = (f32[128,2]{0,1:T(2,128)S(1)}, f32[128,2]{0,1:T(2,128)}, u32[]{:S(2)}) copy-start(f32[128,2]{0,1:T(2,128)} %param.11) | copy-start | bytes 3076
  0.6 54.6 %copy-start.5 = (s32[128]{0:T(128)S(1)}, s32[128]{0:T(128)}, u32[]{:S(2)}) copy-start(s32[128]{0:T(128)} %param.10) | copy-start | bytes 1540
  0.7 54.8 %copy-start.1 = (bf16[128,2,1024]{2,1,0:T(2,128)(2,1)S(1)}, bf16[128,2,1024]{2,1,0:T(2,128)(2,1)}, u32[]{:S(2)}) copy-start(bf16[128,2,1024]{2,1,0:T(2,128)(2,1)} %param.12) | copy-start | bytes 1572868
  3.0 25.8 %all-to-all-start = ((bf16[16,2,16,1280]{3,2,1,0:T(8,128)(2,1)}), bf16[16,2,16,1280]{3,2,1,0:T(8,128)(2,1)S(1)}, u32[]{:S(2)}, u32[]{:S(2)}) async-start(bf16[16,2,16,1280]{3,2,1,0:T(8,128)(2,1)} %broadcast_in_dim.28), calls=%async_computation | async-start | bytes 2621440 | tf_op jit(solution)/shard_map/all_to_all | solution.py:120
  12.4 16.5 %collective-permute-start = (bf16[2,16,1280]{2,0,1:T(2,128)(2,1)S(1)}, bf16[2,16,1280]{2,0,1:T(2,128)(2,1)S(1)}, u32[]{:S(2)}, u32[]{:S(2)}) collective-permute-start(bf16[2,16,1280]{2,0,1:T(2,128)(2,1)S(1)} %broadcast_select_fusion), channel_id=1, source_target_pairs={{0,256},{256,0},{1,257},{257,1},{2,258},{258,2},{3,259},{259,3},{4... | collective-permute-start | bytes 245768 | tf_op jit(solution)/shard_map/ppermute | solution.py:114
  30.1 23.2 %all-to-all-start.1 = ((bf16[16,2,16,1280]{3,2,1,0:T(8,128)(2,1)}), bf16[16,2,16,1280]{3,2,1,0:T(8,128)(2,1)}, u32[]{:S(2)}, u32[]{:S(2)}) async-start(bf16[16,2,16,1280]{3,2,1,0:T(8,128)(2,1)} %broadcast_in_dim.29), calls=%async_computation.1 | async-start | bytes 2621440 | tf_op jit(solution)/shard_map/all_to_all | solution.py:120
  37.3 18.5 %collective-permute-start.1 = (bf16[16,2,16,1280]{3,2,1,0:T(8,128)(2,1)S(1)}, bf16[16,2,16,1280]{3,2,1,0:T(8,128)(2,1)}, u32[]{:S(2)}, u32[]{:S(2)}) collective-permute-start(bf16[16,2,16,1280]{3,2,1,0:T(8,128)(2,1)S(1)} %all-to-all-done.own_ref), channel_id=1, source_target_pairs={{0,8},{8,0},{1,9},{9,1},{2,10},{10,2},{3,11},{11,3},{4,12},{12,4},... | collective-permute-start | bytes 3932168 | tf_op jit(solution)/shard_map/ppermute | solution.py:114
  53.2 5.3 %collective-permute-start.2 = (bf16[16,2,16,1280]{3,2,1,0:T(8,128)(2,1)}, bf16[16,2,16,1280]{3,2,1,0:T(8,128)(2,1)}, u32[]{:S(2)}, u32[]{:S(2)}) collective-permute-start(bf16[16,2,16,1280]{3,2,1,0:T(8,128)(2,1)} %all-to-all-done.1.far_ref), channel_id=1, source_target_pairs={{0,8},{8,0},{1,9},{9,1},{2,10},{10,2},{3,11},{11,3},{4,12},{12,4},... | collective-permute-start | bytes 3932168 | tf_op jit(solution)/shard_map/ppermute | solution.py:114
  61.3 4.5 %copy-start.2 = (bf16[128,1,2,1024]{3,2,1,0:T(2,128)(2,1)S(1)}, bf16[128,1,2,1024]{3,2,1,0:T(2,128)(2,1)}, u32[]{:S(2)}) copy-start(bf16[128,1,2,1024]{3,2,1,0:T(2,128)(2,1)} %param.15) | copy-start | bytes 1572868
  61.3 4.8 %copy-start = (s32[128,128]{1,0:T(8,128)S(1)}, s32[128,128]{1,0:T(8,128)}, u32[]{:S(2)}) copy-start(s32[128,128]{1,0:T(8,128)} %param.13) | copy-start | bytes 196612
  63.7 5.2 %collective-permute-start.3 = (bf16[2,32,1024]{2,1,0:T(8,128)(2,1)S(1)}, bf16[2,32,1024]{2,1,0:T(8,128)(2,1)S(1)}, u32[]{:S(2)}, u32[]{:S(2)}) collective-permute-start(bf16[2,32,1024]{2,1,0:T(8,128)(2,1)S(1)} %get-tuple-element.114), channel_id=1, source_target_pairs={{0,1},{8,9},{16,17},{24,25},{32,33},{40,41},{48,49},{56,57},{64,65... | collective-permute-start | bytes 393224 | tf_op jit(solution)/shard_map/ppermute | solution.py:210
  71.2 6.9 %collective-permute-start.4 = (bf16[2,32,1024]{2,1,0:T(8,128)(2,1)S(1)}, bf16[2,32,1024]{2,1,0:T(8,128)(2,1)S(1)}, u32[]{:S(2)}, u32[]{:S(2)}) collective-permute-start(bf16[2,32,1024]{2,1,0:T(8,128)(2,1)S(1)} %get-tuple-element.121), channel_id=1, source_target_pairs={{0,1},{1,2},{8,9},{9,10},{16,17},{17,18},{24,25},{25,26},{32,33},{... | collective-permute-start | bytes 393224 | tf_op jit(solution)/shard_map/ppermute | solution.py:210
  80.5 6.9 %collective-permute-start.5 = (bf16[2,32,1024]{2,1,0:T(8,128)(2,1)S(1)}, bf16[2,32,1024]{2,1,0:T(8,128)(2,1)S(1)}, u32[]{:S(2)}, u32[]{:S(2)}) collective-permute-start(bf16[2,32,1024]{2,1,0:T(8,128)(2,1)S(1)} %get-tuple-element.131), channel_id=1, source_target_pairs={{0,1},{1,2},{2,3},{8,9},{9,10},{10,11},{16,17},{17,18},{18,19},{24... | collective-permute-start | bytes 393224 | tf_op jit(solution)/shard_map/ppermute | solution.py:210
  89.7 6.9 %collective-permute-start.6 = (bf16[2,32,1024]{2,1,0:T(8,128)(2,1)S(1)}, bf16[2,32,1024]{2,1,0:T(8,128)(2,1)S(1)}, u32[]{:S(2)}, u32[]{:S(2)}) collective-permute-start(bf16[2,32,1024]{2,1,0:T(8,128)(2,1)S(1)} %get-tuple-element.141), channel_id=1, source_target_pairs={{0,1},{1,2},{2,3},{3,4},{8,9},{9,10},{10,11},{11,12},{16,17},{17,1... | collective-permute-start | bytes 393224 | tf_op jit(solution)/shard_map/ppermute | solution.py:210
  97.1 1.2 collective-permute-start.7
  98.9 1.2 collective-permute-start.8
  100.7 1.2 collective-permute-start.9
  102.5 1.2 collective-permute-start.10
  104.3 1.2 collective-permute-start.11
  106.3 1.2 collective-permute-start.12
  107.6 100.0 %copy-start.3 = (f32[128,2,128]{2,1,0:T(2,128)S(1)}, f32[128,2,128]{2,1,0:T(2,128)}, u32[]{:S(2)}) copy-start(f32[128,2,128]{2,1,0:T(2,128)} %param.14) | copy-start | bytes 393220
  109.4 36.4 %collective-permute-start.13 = (bf16[4,2,32,128]{3,2,1,0:T(8,128)(2,1)S(1)}, bf16[4,2,32,128]{3,2,1,0:T(8,128)(2,1)S(1)}, u32[]{:S(2)}, u32[]{:S(2)}) collective-permute-start(bf16[4,2,32,128]{3,2,1,0:T(8,128)(2,1)S(1)} %convert_element_type.10), channel_id=1, source_target_pairs={{0,4},{1,5},{2,6},{3,7},{4,0},{5,1},{6,2},{7,3},{8,12},{9,13},{10,... | collective-permute-start | bytes 196616 | tf_op jit(solution)/shard_map/ppermute | solution.py:217
  145.8 19.5 %collective-permute-start.14 = (bf16[4,2,32,128]{3,2,1,0:T(8,128)(2,1)S(1)}, bf16[4,2,32,128]{3,2,1,0:T(8,128)(2,1)S(1)}, u32[]{:S(2)}, u32[]{:S(2)}) collective-permute-start(bf16[4,2,32,128]{3,2,1,0:T(8,128)(2,1)S(1)} %convert_add_fusion), channel_id=1, source_target_pairs={{0,2},{1,3},{2,0},{3,1},{4,6},{5,7},{6,4},{7,5},{8,10},{9,11},{10,... | collective-permute-start | bytes 196616 | tf_op jit(solution)/shard_map/ppermute | solution.py:217
  165.3 42.3 %collective-permute-start.15 = (bf16[4,2,32,128]{3,2,1,0:T(8,128)(2,1)S(1)}, bf16[4,2,32,128]{3,2,1,0:T(8,128)(2,1)S(1)}, u32[]{:S(2)}, u32[]{:S(2)}) collective-permute-start(bf16[4,2,32,128]{3,2,1,0:T(8,128)(2,1)S(1)} %add.31), channel_id=1, source_target_pairs={{0,1},{1,0},{2,3},{3,2},{4,5},{5,4},{6,7},{7,6},{8,9},{9,8},{10,11... | collective-permute-start | bytes 196616 | tf_op jit(solution)/shard_map/ppermute | solution.py:217
  172.4 34.5 %all-to-all-start.2 = ((f32[64,1,16]{2,1,0:T(1,128)}), f32[64,1,16]{2,1,0:T(1,128)S(1)}, u32[]{:S(2)}, u32[]{:S(2)}) async-start(f32[64,1,16]{2,1,0:T(1,128)} %bitcast.23), calls=%async_computation.2 | async-start | bytes 65536 | tf_op jit(solution)/shard_map/all_to_all | solution.py:223

commit v2 on v1

--- a/solution.py
+++ b/solution.py
@@ -31,21 +31,23 @@
     return jnp.concatenate(tiles, axis=0)
 
 
-def stage_kernel(step, chunks, sc_ref, x_ref, inflow_ref, cells_ref, wave_ref, w_ref, y_ref, field_ref, _w, v_ref):
+def stage_kernel(step, chunks, stages, sc_ref, x_ref, inflow_ref, cells_ref, wave_ref, receivers_ref, w_ref, _p, y_ref, field_ref, _w, picked_ref, v_ref):
     owner = sc_ref[0]
     chunk = step - owner
-    m, width = x_ref.shape[1], x_ref.shape[2]
+    m, width = inflow_ref.shape[1], inflow_ref.shape[2]
     groups = width // GROUP
 
     @pl.when((chunk >= 0) & (chunk < chunks))
     def _():
         @pl.when(owner == 0)
         def _():
-            v_ref[:, 0 : 2 * m] = inflow_ref[...].reshape(1, 2 * m, width)
+            v_ref[...] = inflow_ref[...].reshape(1, 2 * m, width)
+            picked_ref[chunk] = jnp.zeros(picked_ref.shape[1:], BF16)
 
         @pl.when(owner != 0)
         def _():
-            v_ref[:, 0 : 2 * m] = x_ref[...].reshape(1, 2 * m, width)
+            v_ref[...] = x_ref[:, :, :width].reshape(1, 2 * m, width)
+            picked_ref[chunk] = x_ref[:, :, width:]
 
         straight = v_ref[0]
         crossed = jnp.concatenate([-straight[m:], straight[:m]], axis=0)
@@ -69,20 +71,7 @@
             acc = acc.reshape(2, m, GROUP)
             field_ref[:, :, low:high] = acc
             y_ref[:, :, low:high] = acc.astype(BF16)
-
-
-def post_kernel(step, chunks, sc_ref, field_ref, adjoint_ref, cells_ref, _w, _p, _g, wave_out, picked_out, grad_out):
-    owner = sc_ref[0]
-    chunk = step - owner
-    m, width = field_ref.shape[1], field_ref.shape[2]
-
-    @pl.when((chunk >= 0) & (chunk < chunks))
-    def _():
-        field = field_ref[...]
-        wave_out[chunk] = field
-        prod = field * adjoint_ref[chunk].astype(F32)
-        grad_out[...] += jnp.sum(prod.reshape(2 * m // 8, 8, width), axis=0)
-        local = cells_ref[chunk] - owner * width
+        local = receivers_ref[chunk] - owner * width
         tile, lane = local >> 7, local & 127
         for p in range(2):
             got = jnp.zeros((m, 128), F32)
@@ -90,7 +79,27 @@
                 part = field_ref[p, :, 128 * t : 128 * (t + 1)]
                 part = jnp.take_along_axis(part, lane, axis=1, mode="promise_in_bounds")
                 got = jnp.where(tile == t, part, got)
-            picked_out[chunk, p] = got
+            total = picked_ref[chunk, p] + got.astype(BF16)
+            picked_ref[chunk, p] = total
+            y_ref[p, :, width:] = total
+
+    if step == chunks + stages - 2:
+        @pl.when(owner != stages - 1)
+        def _():
+            picked_ref[...] = jnp.zeros_like(picked_ref)
+
+
+def post_kernel(step, chunks, sc_ref, field_ref, adjoint_ref, _w, _g, wave_out, grad_out):
+    owner = sc_ref[0]
+    chunk = step - owner
+    m, width = field_ref.shape[1], field_ref.shape[2]
+
+    @pl.when((chunk >= 0) & (chunk < chunks))
+    def _():
+        field = field_ref[...]
+        wave_out[chunk] = field
+        prod = field * adjoint_ref[chunk].astype(F32)
+        grad_out[...] += jnp.sum(prod.reshape(2 * m // 8, 8, width), axis=0)
 
 
 def place_kernel(sc_ref, own_ref, own_other_ref, far_ref, far_other_ref, out_ref, sems):
@@ -120,11 +129,11 @@
     return lax.all_to_all(spread, ("y", "x"), 0, 0, tiled=True)
 
 
-def gather_factor(packed, where):
+def gather_factor(packed, where, inflow):
     far = swap(packed, "zh")
+    packed, inflow = lax.optimization_barrier((packed, inflow))
     own = plane_gather(packed)
     own_other = swap(own, "c")
-    own, far = lax.optimization_barrier((own, far))
     far = plane_gather(far)
     far_other = swap(far, "c")
     anywhere = pl.BlockSpec(memory_space=pl.ANY)
@@ -136,7 +145,14 @@
         scratch_shapes=[pltpu.SemaphoreType.DMA((4,))],
         compiler_params=pltpu.CompilerParams(vmem_limit_bytes=LIMIT),
         name="place",
-    )(where, own, own_other, far, far_other)
+    )(where, own, own_other, far, far_other), inflow
+
+
+def fan_out(stages):
+    last = stages - 1
+    if stages != 8:
+        return [[[(last, i)] for i in range(last)]]
+    return [[[(7, 3)], [(7, 5)]], [[(3, 1), (5, 4)]], [[(3, 2), (5, 6), (1, 0)]]]
 
 
 def per_device(lower, coupling, source_cell, source_wave, inflow, receiver_cell, observed, adjoint):
@@ -153,12 +169,12 @@
     high = jnp.pad(coupling[0].transpose(1, 0, 2), ((0, 0), (0, 0), (GROUP, 0)))
     packed = jnp.where(lax.broadcasted_iota(jnp.int32, low.shape, 2) < split, low, high)
     where = jnp.stack([owner, lax.axis_index("zh"), lax.axis_index("c")])
-    factor = gather_factor(packed, where)
 
     def by_chunk(array):
         return array.reshape((CHUNKS, m) + array.shape[1:])
 
     inflow = by_chunk(inflow).transpose(0, 2, 1, 3)
+    factor, inflow = gather_factor(packed, where, inflow)
     adjoint = by_chunk(adjoint[:, 0]).transpose(0, 2, 1, 3)
     observed = by_chunk(observed).transpose(0, 2, 1, 3)
     cells, waves, receivers = by_chunk(source_cell[:, None]), by_chunk(source_wave), by_chunk(receiver_cell)
@@ -166,15 +182,16 @@
     vmem = pl.BlockSpec(memory_space=pltpu.VMEM)
     smem = pl.BlockSpec(memory_space=pltpu.SMEM)
     stage = lambda t: pl.pallas_call(
-        functools.partial(stage_kernel, t, CHUNKS),
+        functools.partial(stage_kernel, t, CHUNKS, stages),
         out_shape=(
-            pltpu.VMEM((2, m, width), BF16),
+            pltpu.VMEM((2, m, width + 128), BF16),
             pltpu.VMEM((2, m, width), F32),
             pltpu.VMEM(factor.shape, BF16),
+            pltpu.VMEM((CHUNKS, 2, m, 128), BF16),
         ),
-        in_specs=[smem] + [vmem] * 5,
-        out_specs=(vmem, vmem, vmem),
-        input_output_aliases={5: 2},
+        in_specs=[smem] + [vmem] * 7,
+        out_specs=(vmem, vmem, vmem, vmem),
+        input_output_aliases={6: 2, 7: 3},
         scratch_shapes=[pltpu.VMEM((1, 2 * m, width), BF16)],
         cost_estimate=pl.CostEstimate(
             flops=int(2 * 2 * 2 * m * 2 * width * width * 0.625),
@@ -188,40 +205,41 @@
         functools.partial(post_kernel, t, CHUNKS),
         out_shape=(
             pltpu.VMEM((CHUNKS, 2, m, width), F32),
-            pltpu.VMEM((CHUNKS, 2, m, receivers.shape[2]), F32),
             pltpu.VMEM((8, width), F32),
         ),
-        in_specs=[smem] + [vmem] * 6,
-        out_specs=(vmem, vmem, vmem),
-        input_output_aliases={4: 0, 5: 1, 6: 2},
+        in_specs=[smem] + [vmem] * 4,
+        out_specs=(vmem, vmem),
+        input_output_aliases={3: 0, 4: 1},
         cost_estimate=pl.CostEstimate(flops=8 * m * width, bytes_accessed=24 * m * width, transcendentals=0),
         compiler_params=pltpu.CompilerParams(vmem_limit_bytes=LIMIT),
         name="post",
     )
     field_all = jnp.zeros((CHUNKS, 2, m, width), F32)
-    picked = jnp.zeros((CHUNKS, 2, m, receivers.shape[2]), F32)
+    picked = jnp.zeros((CHUNKS, 2, m, receivers.shape[2]), BF16)
     grad = jnp.zeros((8, width), F32)
-    x = jnp.zeros((2, m, width), BF16)
-    steps = CHUNKS + stages - 1
-    for t in range(steps):
-        y, field, factor = stage(t)(where, x, inflow[min(t, CHUNKS - 1)], cells, waves, factor)
+    x = jnp.zeros((2, m, width + 128), BF16)
+    for t in range(CHUNKS + stages - 1):
+        y, field, factor, picked = stage(t)(
+            where, x, inflow[min(t, CHUNKS - 1)], cells, waves, receivers, factor, picked
+        )
         pairs = [(i, i + 1) for i in range(stages - 1) if 0 <= t - i < CHUNKS]
         if pairs:
             x = lax.ppermute(y, "fac", pairs)
-        field_all, picked, grad = post(t)(where, field, adjoint, receivers, field_all, picked, grad)
-        x, field_all, picked, grad = lax.optimization_barrier((x, field_all, picked, grad))
-
-    picked = picked.astype(BF16)
-    step = stages // 2
-    while step:
-        picked = picked + lax.ppermute(picked, "fac", [(i, i ^ step) for i in range(stages)])
-        step //= 2
-    residual = (picked.astype(F32) - observed).transpose(0, 2, 1, 3).reshape(sources, 2, -1)
+        field_all, grad = post(t)(where, field, adjoint, field_all, grad)
+        x, field_all, grad = lax.optimization_barrier((x, field_all, grad))
+
+    rounds = fan_out(stages)
+    first = [lax.ppermute(picked, "fac", pairs) for pairs in rounds[0]]
     shards = lax.axis_size(SRC)
     scale = 1.0 / math.sqrt(sources * shards)
     terms = (jnp.sum(grad, axis=0) * scale).reshape(shards, rows)
     terms = lax.all_to_all(terms, SRC, 0, 0, tiled=True)
+    first, terms = lax.optimization_barrier((first, terms))
     gradient = jnp.sum(terms, axis=0)[None]
+    picked = functools.reduce(jnp.add, first, picked)
+    for pairs in rounds[1:]:
+        picked = picked + lax.ppermute(picked, "fac", pairs[0])
+    residual = (picked.astype(F32) - observed).transpose(0, 2, 1, 3).reshape(sources, 2, -1)
     wavefield = field_all.transpose(0, 2, 1, 3).reshape(sources, 1, 2, width)
     return wavefield, residual, gradient
 

time: 212 us -> 197 us (0.929)
  the two profiles are of different devices: /device:TPU:6 before, /device:TPU:225 now
where the time goes in v2:
time: 197 us; the launch traced here: 196 us
  waiting for transfers between devices  78 us (40%)
  starting transfers between devices  42.5 us (22%)
  blocking collectives  42.3 us (21%)
  Pallas kernels  23.4 us (12%)
  local copies, waits for them, and re-layouts  6.91 us (4%)
    ppermute x10, waiting for transfers between devices, per_device(): x = lax.ppermute(y, 'fac', pairs)  50.4 us
    all_to_all x1, blocking collectives, per_device(): terms = lax.all_to_all(terms, SRC, 0, 0, tiled=True)  42.3 us
    all_to_all x2, waiting for transfers between devices, plane_gather(): return lax.all_to_all(spread, ('y', 'x'), 0, 0, tiled=True)  19.1 us
    ppermute x3, starting transfers between devices, swap(): return lax.ppermute(array, axis, [(0, 1), (1, 0)])  17.2 us
    pallas_call x11, Pallas kernels, per_device(): stage(t)  14.5 us
    all_to_all x2, starting transfers between devices, plane_gather(): return lax.all_to_all(spread, ('y', 'x'), 0, 0, tiled=True)  12.2 us
    ppermute x10, starting transfers between devices, per_device(): x = lax.ppermute(y, 'fac', pairs)  9.19 us
    ppermute x3, waiting for transfers between devices, swap(): return lax.ppermute(array, axis, [(0, 1), (1, 0)])  8.46 us
  transfers between devices with their start and end apart: 19, of which 8 were waited for; matrix products, arithmetic and copies ran while one was open for 2% of the time, Pallas kernels for 3%

profile of v2, /device:TPU:225, one launch (start us, length us, event | category | flops | bytes accessed | tf_op | source)
XLA Modules:
  0.0 196.1 jit_solution(17029979782862399827)
XLA Ops:
  0.7 1.2 copy.128
  1.9 1.0 broadcast_select_fusion
  2.9 1.2 broadcast_in_dim.28
  4.1 6.8 %all-to-all-start = ((bf16[16,2,16,1280]{3,2,1,0:T(8,128)(2,1)}), bf16[16,2,16,1280]{3,2,1,0:T(8,128)(2,1)S(1)}, u32[]{:S(2)}, u32[]{:S(2)}) async-start(bf16[16,2,16,1280]{3,2,1,0:T(8,128)(2,1)} %broadcast_in_dim.28), calls=%async_computation | async-start | bytes 2621440 | tf_op jit(solution)/shard_map/all_to_all | solution.py:129
  10.9 7.9 %collective-permute-start.1 = (bf16[2,16,1280]{2,0,1:T(2,128)(2,1)S(1)}, bf16[2,16,1280]{2,0,1:T(2,128)(2,1)S(1)}, u32[]{:S(2)}, u32[]{:S(2)}) collective-permute-start(bf16[2,16,1280]{2,0,1:T(2,128)(2,1)S(1)} %broadcast_select_fusion), channel_id=1, source_target_pairs={{0,256},{256,0},{1,257},{257,1},{2,258},{258,2},{3,259},{259,3},{4... | collective-permute-start | bytes 245768 | tf_op jit(solution)/shard_map/ppermute | solution.py:123
  18.8 6.0 %collective-permute-done.1 = bf16[2,16,1280]{2,0,1:T(2,128)(2,1)S(1)} collective-permute-done((bf16[2,16,1280]{2,0,1:T(2,128)(2,1)S(1)}, bf16[2,16,1280]{2,0,1:T(2,128)(2,1)S(1)}, u32[]{:S(2)}, u32[]{:S(2)}) %collective-permute-start.1) | collective-permute-done | bytes 81952 | tf_op jit(solution)/shard_map/ppermute | solution.py:123
  24.8 4.9 %all-to-all-done.own_ref = bf16[16,2,16,1280]{3,2,1,0:T(8,128)(2,1)S(1)} async-done(((bf16[16,2,16,1280]{3,2,1,0:T(8,128)(2,1)}), bf16[16,2,16,1280]{3,2,1,0:T(8,128)(2,1)S(1)}, u32[]{:S(2)}, u32[]{:S(2)}) %all-to-all-start) | async-done | bytes 1310752 | tf_op jit(solution)/shard_map/all_to_all | solution.py:129
  29.7 1.2 broadcast_in_dim.29
  30.8 5.5 %all-to-all-start.1 = ((bf16[16,2,16,1280]{3,2,1,0:T(8,128)(2,1)}), bf16[16,2,16,1280]{3,2,1,0:T(8,128)(2,1)}, u32[]{:S(2)}, u32[]{:S(2)}) async-start(bf16[16,2,16,1280]{3,2,1,0:T(8,128)(2,1)} %broadcast_in_dim.29), calls=%async_computation.1 | async-start | bytes 2621440 | tf_op jit(solution)/shard_map/all_to_all | solution.py:129
  36.3 3.8 %collective-permute-start = (bf16[16,2,16,1280]{3,2,1,0:T(8,128)(2,1)S(1)}, bf16[16,2,16,1280]{3,2,1,0:T(8,128)(2,1)}, u32[]{:S(2)}, u32[]{:S(2)}) collective-permute-start(bf16[16,2,16,1280]{3,2,1,0:T(8,128)(2,1)S(1)} %all-to-all-done.own_ref), channel_id=1, source_target_pairs={{0,8},{8,0},{1,9},{9,1},{2,10},{10,2},{3,11},{11,3},{4,12},{12,4},... | collective-permute-start | bytes 3932168 | tf_op jit(solution)/shard_map/ppermute | solution.py:123
  40.1 14.2 %all-to-all-done.1.far_ref = bf16[16,2,16,1280]{3,2,1,0:T(8,128)(2,1)} async-done(((bf16[16,2,16,1280]{3,2,1,0:T(8,128)(2,1)}), bf16[16,2,16,1280]{3,2,1,0:T(8,128)(2,1)}, u32[]{:S(2)}, u32[]{:S(2)}) %all-to-all-start.1) | async-done | bytes 1310752 | tf_op jit(solution)/shard_map/all_to_all | solution.py:129
  54.3 5.5 %collective-permute-start.2 = (bf16[16,2,16,1280]{3,2,1,0:T(8,128)(2,1)}, bf16[16,2,16,1280]{3,2,1,0:T(8,128)(2,1)}, u32[]{:S(2)}, u32[]{:S(2)}) collective-permute-start(bf16[16,2,16,1280]{3,2,1,0:T(8,128)(2,1)} %all-to-all-done.1.far_ref), channel_id=1, source_target_pairs={{0,8},{8,0},{1,9},{9,1},{2,10},{10,2},{3,11},{11,3},{4,12},{12,4},... | collective-permute-start | bytes 3932168 | tf_op jit(solution)/shard_map/ppermute | solution.py:123
  59.8 0.1 copy.95
  59.9 0.2 reshape_broadcast_in_dim.4.cells_ref
  60.1 0.1 pad_add_fusion.sc_ref
  60.3 2.5 %collective-permute-done.2.far_other_ref = bf16[16,2,16,1280]{3,2,1,0:T(8,128)(2,1)} collective-permute-done((bf16[16,2,16,1280]{3,2,1,0:T(8,128)(2,1)}, bf16[16,2,16,1280]{3,2,1,0:T(8,128)(2,1)}, u32[]{:S(2)}, u32[]{:S(2)}) %collective-permute-start.2) | collective-permute-done | bytes 1310752 | tf_op jit(solution)/shard_map/ppermute | solution.py:123
  62.8 2.8 %place.1.w_ref = bf16[2,2,16,2,16,1280]{5,4,3,2,1,0:T(8,128)(2,1)S(1)} custom-call(s32[3]{0:T(128)S(1)} %pad_add_fusion.sc_ref, bf16[16,2,16,1280]{3,2,1,0:T(8,128)(2,1)S(1)} %all-to-all-done.own_ref, bf16[16,2,16,1280]{3,2,1,0:T(8,128)(2,1)} %collective-permute-done.own_other_ref, bf16[16,2,16,1280]{3,2,1,0:T(8,128)(2,1)} %all-to-all-done.1.far_ref, ...), custom_call_target="tpu_custom_call" | custom-call | tf_op jit(solution)/shard_map/place/pallas_call | solution.py:140
  65.6 0.6 stage.11
  66.2 0.7 collective-permute-start.3
  66.9 0.1 copy.127
  67.0 0.1 broadcast_in_dim.31._w
  67.1 0.6 post.11
  67.7 0.6 stage.12
  68.3 0.7 collective-permute-start.4
  68.9 0.6 post.12
  69.5 0.6 stage.13
  70.1 0.7 collective-permute-start.5
  70.7 0.6 post.13
  71.3 0.6 stage.14
  71.9 0.7 collective-permute-start.6
  72.5 0.6 post.14
  73.1 0.6 stage.15
  73.7 0.7 collective-permute-start.7
  74.4 0.6 post.15
  74.9 0.6 stage.16
  75.5 0.7 collective-permute-start.8
  76.2 0.6 post.16
  76.7 0.6 stage.17
  77.3 1.3 collective-permute-start.9
  78.6 0.6 post.17
  79.2 34.8 %collective-permute-done.9.x_ref = bf16[2,32,1152]{2,1,0:T(8,128)(2,1)S(1)} collective-permute-done((bf16[2,32,1152]{2,1,0:T(8,128)(2,1)S(1)}, bf16[2,32,1152]{2,1,0:T(8,128)(2,1)S(1)}, u32[]{:S(2)}, u32[]{:S(2)}) %collective-permute-start.9) | collective-permute-done | bytes 147488 | tf_op jit(solution)/shard_map/ppermute | solution.py:227
  113.9 2.4 %stage.18 = (bf16[2,32,1152]{2,1,0:T(8,128)(2,1)S(1)}, f32[2,32,1024]{2,1,0:T(8,128)S(1)}, bf16[2,2,16,2,16,1280]{5,4,3,2,1,0:T(8,128)(2,1)S(1)}, bf16[4,2,32,128]{3,2,1,0:T(8,128)(2,1)S(1)}) custom-call(s32[3]{0:T(128)S(1)} %pad_add_fusion.sc_ref, ...), custom_call_target="tpu_custom_call", output_to_operand_aliasing={{2}: (6, {}), {3}: (7, {})} | custom-call | flops 335544320 | bytes 5242880 | tf_op jit(solution)/shard_map/stage/pallas_call | solution.py:222
  116.4 1.3 collective-permute-start.10
  117.7 0.6 post.18
  118.2 5.2 %collective-permute-done.10.x_ref = bf16[2,32,1152]{2,1,0:T(8,128)(2,1)S(1)} collective-permute-done((bf16[2,32,1152]{2,1,0:T(8,128)(2,1)S(1)}, bf16[2,32,1152]{2,1,0:T(8,128)(2,1)S(1)}, u32[]{:S(2)}, u32[]{:S(2)}) %collective-permute-start.10) | collective-permute-done | bytes 147488 | tf_op jit(solution)/shard_map/ppermute | solution.py:227
  123.5 2.4 %stage.19 = (bf16[2,32,1152]{2,1,0:T(8,128)(2,1)S(1)}, f32[2,32,1024]{2,1,0:T(8,128)S(1)}, bf16[2,2,16,2,16,1280]{5,4,3,2,1,0:T(8,128)(2,1)S(1)}, bf16[4,2,32,128]{3,2,1,0:T(8,128)(2,1)S(1)}) custom-call(s32[3]{0:T(128)S(1)} %pad_add_fusion.sc_ref, ...), custom_call_target="tpu_custom_call", output_to_operand_aliasing={{2}: (6, {}), {3}: (7, {})} | custom-call | flops 335544320 | bytes 5242880 | tf_op jit(solution)/shard_map/stage/pallas_call | solution.py:222
  125.9 1.3 collective-permute-start.11
  127.2 0.6 post.19
  127.8 5.2 %collective-permute-done.11.x_ref = bf16[2,32,1152]{2,1,0:T(8,128)(2,1)S(1)} collective-permute-done((bf16[2,32,1152]{2,1,0:T(8,128)(2,1)S(1)}, bf16[2,32,1152]{2,1,0:T(8,128)(2,1)S(1)}, u32[]{:S(2)}, u32[]{:S(2)}) %collective-permute-start.11) | collective-permute-done | bytes 147488 | tf_op jit(solution)/shard_map/ppermute | solution.py:227
  133.0 2.4 %stage.20 = (bf16[2,32,1152]{2,1,0:T(8,128)(2,1)S(1)}, f32[2,32,1024]{2,1,0:T(8,128)S(1)}, bf16[2,2,16,2,16,1280]{5,4,3,2,1,0:T(8,128)(2,1)S(1)}, bf16[4,2,32,128]{3,2,1,0:T(8,128)(2,1)S(1)}) custom-call(s32[3]{0:T(128)S(1)} %pad_add_fusion.sc_ref, ...), custom_call_target="tpu_custom_call", output_to_operand_aliasing={{2}: (6, {}), {3}: (7, {})} | custom-call | flops 335544320 | bytes 5242880 | tf_op jit(solution)/shard_map/stage/pallas_call | solution.py:222
  135.4 1.3 collective-permute-start.12
  136.7 0.6 post.20
  137.3 5.2 %collective-permute-done.12.x_ref = bf16[2,32,1152]{2,1,0:T(8,128)(2,1)S(1)} collective-permute-done((bf16[2,32,1152]{2,1,0:T(8,128)(2,1)S(1)}, bf16[2,32,1152]{2,1,0:T(8,128)(2,1)S(1)}, u32[]{:S(2)}, u32[]{:S(2)}) %collective-permute-start.12) | collective-permute-done | bytes 147488 | tf_op jit(solution)/shard_map/ppermute | solution.py:227
  142.6 3.3 %stage.21 = (bf16[2,32,1152]{2,1,0:T(8,128)(2,1)}, f32[2,32,1024]{2,1,0:T(8,128)S(1)}, bf16[2,2,16,2,16,1280]{5,4,3,2,1,0:T(8,128)(2,1)S(1)}, bf16[4,2,32,128]{3,2,1,0:T(8,128)(2,1)S(1)}) custom-call(s32[3]{0:T(128)S(1)} %pad_add_fusion.sc_ref, bf16[2,32,1152]{2,1,0:T(8,128)(2,1)S(1)} %collective-permute-done.12.x_ref, ...), custom_call_target="tpu_custom_call", output_to_operand_aliasing={{2}: (6, {}), {3}: (7, {})} | custom-call | flops 335544320 | bytes 5242880 | tf_op jit(solution)/shard_map/stage/pallas_call | solution.py:222
  145.9 1.3 collective-permute-start.13
  147.1 1.3 collective-permute-start.14
  148.4 0.6 post.21
  149.1 0.1 mul.35
  149.1 42.3 %all_to_all.19 = f32[64,1,16]{2,1,0:T(1,128)S(1)} all-to-all(f32[64,1,16]{2,1,0:T(1,128)S(1)} %bitcast.81), channel_id=1, replica_groups=mesh['zh'=2,'y'=4,'x'=4,'c'=2,'fac'=8] {'zh','y','x','c'}, dimensions={0} | all-to-all | bytes 8192 | tf_op jit(solution)/shard_map/all_to_all | solution.py:236
  191.5 0.7 collective-permute-start.15
  192.2 0.7 collective-permute-start.16
  192.9 1.8 copy.116
  194.7 0.5 reduce_sum.19
  195.3 0.8 copy.117
  (35 shorter events, 0.3 us)
Async XLA Ops:
  0.6 59.2 %copy-start.3 = (f32[128,2]{0,1:T(2,128)S(1)}, f32[128,2]{0,1:T(2,128)}, u32[]{:S(2)}) copy-start(f32[128,2]{0,1:T(2,128)} %param.11) | copy-start | bytes 3076
  0.6 59.3 %copy-start.4 = (s32[128]{0:T(128)S(1)}, s32[128]{0:T(128)}, u32[]{:S(2)}) copy-start(s32[128]{0:T(128)} %param.10) | copy-start | bytes 1540
  4.1 25.6 %all-to-all-start = ((bf16[16,2,16,1280]{3,2,1,0:T(8,128)(2,1)}), bf16[16,2,16,1280]{3,2,1,0:T(8,128)(2,1)S(1)}, u32[]{:S(2)}, u32[]{:S(2)}) async-start(bf16[16,2,16,1280]{3,2,1,0:T(8,128)(2,1)} %broadcast_in_dim.28), calls=%async_computation | async-start | bytes 2621440 | tf_op jit(solution)/shard_map/all_to_all | solution.py:129
  10.9 13.9 %collective-permute-start.1 = (bf16[2,16,1280]{2,0,1:T(2,128)(2,1)S(1)}, bf16[2,16,1280]{2,0,1:T(2,128)(2,1)S(1)}, u32[]{:S(2)}, u32[]{:S(2)}) collective-permute-start(bf16[2,16,1280]{2,0,1:T(2,128)(2,1)S(1)} %broadcast_select_fusion), channel_id=1, source_target_pairs={{0,256},{256,0},{1,257},{257,1},{2,258},{258,2},{3,259},{259,3},{4... | collective-permute-start | bytes 245768 | tf_op jit(solution)/shard_map/ppermute | solution.py:123
  30.8 23.5 %all-to-all-start.1 = ((bf16[16,2,16,1280]{3,2,1,0:T(8,128)(2,1)}), bf16[16,2,16,1280]{3,2,1,0:T(8,128)(2,1)}, u32[]{:S(2)}, u32[]{:S(2)}) async-start(bf16[16,2,16,1280]{3,2,1,0:T(8,128)(2,1)} %broadcast_in_dim.29), calls=%async_computation.1 | async-start | bytes 2621440 | tf_op jit(solution)/shard_map/all_to_all | solution.py:129
  36.3 23.9 %collective-permute-start = (bf16[16,2,16,1280]{3,2,1,0:T(8,128)(2,1)S(1)}, bf16[16,2,16,1280]{3,2,1,0:T(8,128)(2,1)}, u32[]{:S(2)}, u32[]{:S(2)}) collective-permute-start(bf16[16,2,16,1280]{3,2,1,0:T(8,128)(2,1)S(1)} %all-to-all-done.own_ref), channel_id=1, source_target_pairs={{0,8},{8,0},{1,9},{9,1},{2,10},{10,2},{3,11},{11,3},{4,12},{12,4},... | collective-permute-start | bytes 3932168 | tf_op jit(solution)/shard_map/ppermute | solution.py:123
  54.3 8.5 %collective-permute-start.2 = (bf16[16,2,16,1280]{3,2,1,0:T(8,128)(2,1)}, bf16[16,2,16,1280]{3,2,1,0:T(8,128)(2,1)}, u32[]{:S(2)}, u32[]{:S(2)}) collective-permute-start(bf16[16,2,16,1280]{3,2,1,0:T(8,128)(2,1)} %all-to-all-done.1.far_ref), channel_id=1, source_target_pairs={{0,8},{8,0},{1,9},{9,1},{2,10},{10,2},{3,11},{11,3},{4,12},{12,4},... | collective-permute-start | bytes 3932168 | tf_op jit(solution)/shard_map/ppermute | solution.py:123
  60.2 5.4 %copy-start = (s32[128,128]{1,0:T(8,128)S(1)}, s32[128,128]{1,0:T(8,128)}, u32[]{:S(2)}) copy-start(s32[128,128]{1,0:T(8,128)} %param.13) | copy-start | bytes 196612
  65.6 1.3 copy-start.1
  66.2 1.5 collective-permute-start.3
  68.3 1.2 collective-permute-start.4
  70.1 1.2 collective-permute-start.5
  71.9 1.2 collective-permute-start.6
  73.7 1.2 collective-permute-start.7
  75.5 1.2 collective-permute-start.8
  77.3 36.6 %collective-permute-start.9 = (bf16[2,32,1152]{2,1,0:T(8,128)(2,1)S(1)}, bf16[2,32,1152]{2,1,0:T(8,128)(2,1)S(1)}, u32[]{:S(2)}, u32[]{:S(2)}) collective-permute-start(bf16[2,32,1152]{2,1,0:T(8,128)(2,1)S(1)} %get-tuple-element.158), channel_id=1, source_target_pairs={{3,4},{4,5},{5,6},{6,7},{11,12},{12,13},{13,14},{14,15},{19,20},{2... | collective-permute-start | bytes 442376 | tf_op jit(solution)/shard_map/ppermute | solution.py:227
  116.4 7.1 %collective-permute-start.10 = (bf16[2,32,1152]{2,1,0:T(8,128)(2,1)S(1)}, bf16[2,32,1152]{2,1,0:T(8,128)(2,1)S(1)}, u32[]{:S(2)}, u32[]{:S(2)}) collective-permute-start(bf16[2,32,1152]{2,1,0:T(8,128)(2,1)S(1)} %get-tuple-element.167), channel_id=1, source_target_pairs={{4,5},{5,6},{6,7},{12,13},{13,14},{14,15},{20,21},{21,22},{22,23},... | collective-permute-start | bytes 442376 | tf_op jit(solution)/shard_map/ppermute | solution.py:227
  125.9 7.1 %collective-permute-start.11 = (bf16[2,32,1152]{2,1,0:T(8,128)(2,1)S(1)}, bf16[2,32,1152]{2,1,0:T(8,128)(2,1)S(1)}, u32[]{:S(2)}, u32[]{:S(2)}) collective-permute-start(bf16[2,32,1152]{2,1,0:T(8,128)(2,1)S(1)} %get-tuple-element.176), channel_id=1, source_target_pairs={{5,6},{6,7},{13,14},{14,15},{21,22},{22,23},{29,30},{30,31},{37,38... | collective-permute-start | bytes 442376 | tf_op jit(solution)/shard_map/ppermute | solution.py:227
  135.4 7.1 %collective-permute-start.12 = (bf16[2,32,1152]{2,1,0:T(8,128)(2,1)S(1)}, bf16[2,32,1152]{2,1,0:T(8,128)(2,1)S(1)}, u32[]{:S(2)}, u32[]{:S(2)}) collective-permute-start(bf16[2,32,1152]{2,1,0:T(8,128)(2,1)S(1)} %get-tuple-element.185), channel_id=1, source_target_pairs={{6,7},{14,15},{22,23},{30,31},{38,39},{46,47},{54,55},{62,63},{70,... | collective-permute-start | bytes 442376 | tf_op jit(solution)/shard_map/ppermute | solution.py:227
  142.6 52.7 %copy-start.2 = (f32[128,2,128]{2,1,0:T(2,128)S(1)}, f32[128,2,128]{2,1,0:T(2,128)}, u32[]{:S(2)}) copy-start(f32[128,2,128]{2,1,0:T(2,128)} %param.14) | copy-start | bytes 393220
  145.9 45.6 %collective-permute-start.13 = (bf16[4,2,32,128]{3,2,1,0:T(8,128)(2,1)S(1)}, bf16[4,2,32,128]{3,2,1,0:T(8,128)(2,1)S(1)}, u32[]{:S(2)}, u32[]{:S(2)}) collective-permute-start(bf16[4,2,32,128]{3,2,1,0:T(8,128)(2,1)S(1)} %get-tuple-element.200), channel_id=1, source_target_pairs={{7,3},{15,11},{23,19},{31,27},{39,35},{47,43},{55,51},{63,59},{71,... | collective-permute-start | bytes 196616 | tf_op jit(solution)/shard_map/ppermute | solution.py:232
  147.1 44.3 %collective-permute-start.14 = (bf16[4,2,32,128]{3,2,1,0:T(8,128)(2,1)S(1)}, bf16[4,2,32,128]{3,2,1,0:T(8,128)(2,1)S(1)}, u32[]{:S(2)}, u32[]{:S(2)}) collective-permute-start(bf16[4,2,32,128]{3,2,1,0:T(8,128)(2,1)S(1)} %get-tuple-element.200), channel_id=1, source_target_pairs={{7,5},{15,13},{23,21},{31,29},{39,37},{47,45},{55,53},{63,61},{71,... | collective-permute-start | bytes 196616 | tf_op jit(solution)/shard_map/ppermute | solution.py:232
  191.5 0.7 collective-permute-start.15
  192.2 3.1 %collective-permute-start.16 = (bf16[4,2,32,128]{3,2,1,0:T(8,128)(2,1)S(1)}, bf16[4,2,32,128]{3,2,1,0:T(8,128)(2,1)S(1)}, u32[]{:S(2)}, u32[]{:S(2)}) collective-permute-start(bf16[4,2,32,128]{3,2,1,0:T(8,128)(2,1)S(1)} %add.35), channel_id=1, source_target_pairs={{3,2},{5,6},{1,0},{11,10},{13,14},{9,8},{19,18},{21,22},{17,16},{2... | collective-permute-start | bytes 196616 | tf_op jit(solution)/shard_map/ppermute | solution.py:241

commit v3 on v2

--- a/solution.py
+++ b/solution.py
@@ -12,6 +12,7 @@
 CHUNKS = 4
 GROUP = 256
 LIMIT = 16 << 20
+SPLIT = 4
 F32, BF16 = jnp.float32, jnp.bfloat16
 NT = (((1,), (1,)), ((), ()))
 
@@ -31,7 +32,9 @@
     return jnp.concatenate(tiles, axis=0)
 
 
-def stage_kernel(step, chunks, stages, sc_ref, x_ref, inflow_ref, cells_ref, wave_ref, receivers_ref, w_ref, _p, y_ref, field_ref, _w, picked_ref, v_ref):
+def stage_kernel(step, chunks, stages, sc_ref, x_ref, inflow_ref, cells_ref, wave_ref, receivers_ref, w_ref, _p, field_ref, _w, picked_ref, *rest):
+    v_ref = rest[-1]
+    last = step == chunks + stages - 2
     owner = sc_ref[0]
     chunk = step - owner
     m, width = inflow_ref.shape[1], inflow_ref.shape[2]
@@ -70,7 +73,8 @@
             acc += dot_nt(crossed[:, :high], group_block(w_ref, g, 1, 0, high))
             acc = acc.reshape(2, m, GROUP)
             field_ref[:, :, low:high] = acc
-            y_ref[:, :, low:high] = acc.astype(BF16)
+            if not last:
+                rest[0][:, :, low:high] = acc.astype(BF16)
         local = receivers_ref[chunk] - owner * width
         tile, lane = local >> 7, local & 127
         for p in range(2):
@@ -81,25 +85,34 @@
                 got = jnp.where(tile == t, part, got)
             total = picked_ref[chunk, p] + got.astype(BF16)
             picked_ref[chunk, p] = total
-            y_ref[p, :, width:] = total
-
-    if step == chunks + stages - 2:
+            if not last:
+                rest[0][p, :, width:] = total
+
+    if last:
         @pl.when(owner != stages - 1)
         def _():
             picked_ref[...] = jnp.zeros_like(picked_ref)
 
 
-def post_kernel(step, chunks, sc_ref, field_ref, adjoint_ref, _w, _g, wave_out, grad_out):
+def post_kernel(step, chunks, sc_ref, field_ref, adjoint_ref, *refs):
+    wave_out, grad_out, rows_ref, sem = refs[-4:]
     owner = sc_ref[0]
     chunk = step - owner
     m, width = field_ref.shape[1], field_ref.shape[2]
 
+    if step == 0:
+        grad_out[...] = jnp.zeros_like(grad_out)
+
     @pl.when((chunk >= 0) & (chunk < chunks))
     def _():
         field = field_ref[...]
-        wave_out[chunk] = field
+        for p in range(2):
+            rows_ref[:, p, :] = field[p]
+        store = pltpu.make_async_copy(rows_ref, wave_out.at[pl.ds(chunk * m, m)], sem)
+        store.start()
         prod = field * adjoint_ref[chunk].astype(F32)
         grad_out[...] += jnp.sum(prod.reshape(2 * m // 8, 8, width), axis=0)
+        store.wait()
 
 
 def place_kernel(sc_ref, own_ref, own_other_ref, far_ref, far_other_ref, out_ref, sems):
@@ -110,8 +123,13 @@
         (far_ref, core, 1 - half),
         (far_other_ref, 1 - core, 1 - half),
     )
+    part = own_ref.shape[0] // SPLIT
     copies = [
-        pltpu.make_async_copy(ref, out_ref.at[c, h], sems.at[i]) for i, (ref, c, h) in enumerate(pieces)
+        pltpu.make_async_copy(
+            ref.at[pl.ds(part * k, part)], out_ref.at[c, h, pl.ds(part * k, part)], sems.at[i, k]
+        )
+        for i, (ref, c, h) in enumerate(pieces)
+        for k in range(SPLIT)
     ]
     for copy in copies:
         copy.start()
@@ -129,10 +147,13 @@
     return lax.all_to_all(spread, ("y", "x"), 0, 0, tiled=True)
 
 
-def gather_factor(packed, where, inflow):
+def empty_plane(piece):
+    return jnp.zeros((lax.axis_size(("y", "x")),) + piece.shape, piece.dtype)
+
+
+def gather_factor(packed, where):
     far = swap(packed, "zh")
-    packed, inflow = lax.optimization_barrier((packed, inflow))
-    own = plane_gather(packed)
+    own = lax.cond(where[0] < lax.axis_size("fac"), plane_gather, empty_plane, packed)
     own_other = swap(own, "c")
     far = plane_gather(far)
     far_other = swap(far, "c")
@@ -142,17 +163,17 @@
         out_shape=pltpu.VMEM((2, 2) + own.shape, own.dtype),
         in_specs=[pl.BlockSpec(memory_space=pltpu.SMEM)] + [anywhere] * 4,
         out_specs=pl.BlockSpec(memory_space=pltpu.VMEM),
-        scratch_shapes=[pltpu.SemaphoreType.DMA((4,))],
+        scratch_shapes=[pltpu.SemaphoreType.DMA((4, SPLIT))],
         compiler_params=pltpu.CompilerParams(vmem_limit_bytes=LIMIT),
         name="place",
-    )(where, own, own_other, far, far_other), inflow
+    )(where, own, own_other, far, far_other)
 
 
 def fan_out(stages):
     last = stages - 1
     if stages != 8:
         return [[[(last, i)] for i in range(last)]]
-    return [[[(7, 3)], [(7, 5)]], [[(3, 1), (5, 4)]], [[(3, 2), (5, 6), (1, 0)]]]
+    return [[[(7, 3)]], [[(3, 1)], [(3, 5)]], [[(3, 2), (5, 6), (1, 0)], [(3, 4)]]]
 
 
 def per_device(lower, coupling, source_cell, source_wave, inflow, receiver_cell, observed, adjoint):
@@ -174,24 +195,25 @@
         return array.reshape((CHUNKS, m) + array.shape[1:])
 
     inflow = by_chunk(inflow).transpose(0, 2, 1, 3)
-    factor, inflow = gather_factor(packed, where, inflow)
+    factor = gather_factor(packed, where)
     adjoint = by_chunk(adjoint[:, 0]).transpose(0, 2, 1, 3)
     observed = by_chunk(observed).transpose(0, 2, 1, 3)
     cells, waves, receivers = by_chunk(source_cell[:, None]), by_chunk(source_wave), by_chunk(receiver_cell)
 
+    steps = CHUNKS + stages - 1
     vmem = pl.BlockSpec(memory_space=pltpu.VMEM)
     smem = pl.BlockSpec(memory_space=pltpu.SMEM)
     stage = lambda t: pl.pallas_call(
         functools.partial(stage_kernel, t, CHUNKS, stages),
         out_shape=(
-            pltpu.VMEM((2, m, width + 128), BF16),
             pltpu.VMEM((2, m, width), F32),
             pltpu.VMEM(factor.shape, BF16),
             pltpu.VMEM((CHUNKS, 2, m, 128), BF16),
-        ),
+        )
+        + ((pltpu.VMEM((2, m, width + 128), BF16),) if t < steps - 1 else ()),
         in_specs=[smem] + [vmem] * 7,
-        out_specs=(vmem, vmem, vmem, vmem),
-        input_output_aliases={6: 2, 7: 3},
+        out_specs=(vmem,) * (4 if t < steps - 1 else 3),
+        input_output_aliases={6: 1, 7: 2},
         scratch_shapes=[pltpu.VMEM((1, 2 * m, width), BF16)],
         cost_estimate=pl.CostEstimate(
             flops=int(2 * 2 * 2 * m * 2 * width * width * 0.625),
@@ -204,29 +226,30 @@
     post = lambda t: pl.pallas_call(
         functools.partial(post_kernel, t, CHUNKS),
         out_shape=(
-            pltpu.VMEM((CHUNKS, 2, m, width), F32),
+            jax.ShapeDtypeStruct((sources, 2, width), F32),
             pltpu.VMEM((8, width), F32),
         ),
-        in_specs=[smem] + [vmem] * 4,
-        out_specs=(vmem, vmem),
-        input_output_aliases={3: 0, 4: 1},
+        in_specs=[smem, vmem, vmem] + ([pl.BlockSpec(memory_space=pl.ANY), vmem] if t else []),
+        out_specs=(pl.BlockSpec(memory_space=pl.ANY), vmem),
+        scratch_shapes=[pltpu.VMEM((m, 2, width), F32), pltpu.SemaphoreType.DMA(())],
+        input_output_aliases={3: 0, 4: 1} if t else {},
+        compiler_params=pltpu.CompilerParams(vmem_limit_bytes=LIMIT),
         cost_estimate=pl.CostEstimate(flops=8 * m * width, bytes_accessed=24 * m * width, transcendentals=0),
-        compiler_params=pltpu.CompilerParams(vmem_limit_bytes=LIMIT),
         name="post",
     )
-    field_all = jnp.zeros((CHUNKS, 2, m, width), F32)
     picked = jnp.zeros((CHUNKS, 2, m, receivers.shape[2]), BF16)
-    grad = jnp.zeros((8, width), F32)
+    done = ()
     x = jnp.zeros((2, m, width + 128), BF16)
-    for t in range(CHUNKS + stages - 1):
-        y, field, factor, picked = stage(t)(
+    for t in range(steps):
+        field, factor, picked, *y = stage(t)(
             where, x, inflow[min(t, CHUNKS - 1)], cells, waves, receivers, factor, picked
         )
         pairs = [(i, i + 1) for i in range(stages - 1) if 0 <= t - i < CHUNKS]
         if pairs:
-            x = lax.ppermute(y, "fac", pairs)
-        field_all, grad = post(t)(where, field, adjoint, field_all, grad)
-        x, field_all, grad = lax.optimization_barrier((x, field_all, grad))
+            x = lax.ppermute(y[0], "fac", pairs)
+        done = post(t)(where, field, adjoint, *done)
+        x, done = lax.optimization_barrier((x, done))
+    wavefield, grad = done
 
     rounds = fan_out(stages)
     first = [lax.ppermute(picked, "fac", pairs) for pairs in rounds[0]]
@@ -238,10 +261,9 @@
     gradient = jnp.sum(terms, axis=0)[None]
     picked = functools.reduce(jnp.add, first, picked)
     for pairs in rounds[1:]:
-        picked = picked + lax.ppermute(picked, "fac", pairs[0])
+        picked = functools.reduce(jnp.add, [lax.ppermute(picked, "fac", p) for p in pairs], picked)
     residual = (picked.astype(F32) - observed).transpose(0, 2, 1, 3).reshape(sources, 2, -1)
-    wavefield = field_all.transpose(0, 2, 1, 3).reshape(sources, 1, 2, width)
-    return wavefield, residual, gradient
+    return wavefield[:, None], residual, gradient
 
 
 def solution(mesh):

time: 197 us -> 199 us (1.010)
  the two profiles are of different devices: /device:TPU:225 before, /device:TPU:6 now
where the time goes in v3:
time: 199 us; the launch traced here: 198 us
  waiting for transfers between devices  70.3 us (35%)
  starting transfers between devices  48.1 us (24%)
  blocking collectives  46.2 us (23%)
  Pallas kernels  25.9 us (13%)
  local copies, waits for them, and re-layouts  4.91 us (2%)
    ppermute x4, waiting for transfers between devices, per_device(): lax.ppermute(picked, 'fac', p)  47.1 us
    all_to_all x1, blocking collectives, plane_gather(): return lax.all_to_all(spread, ('y', 'x'), 0, 0, tiled=True)  24.5 us
    all_to_all x1, blocking collectives, per_device(): terms = lax.all_to_all(terms, SRC, 0, 0, tiled=True)  21.7 us
    ppermute x3, starting transfers between devices, swap(): return lax.ppermute(array, axis, [(0, 1), (1, 0)])  19.5 us
    ppermute x10, starting transfers between devices, per_device(): x = lax.ppermute(y[0], 'fac', pairs)  18.6 us
    all_to_all x1, waiting for transfers between devices, plane_gather(): return lax.all_to_all(spread, ('y', 'x'), 0, 0, tiled=True)  14.3 us
    pallas_call x11, Pallas kernels, per_device(): stage(t)  13.8 us
    pallas_call x11, Pallas kernels, per_device(): done = post(t)(where, field, adjoint, *done)  9.22 us
  transfers between devices with their start and end apart: 19, of which 7 were waited for; matrix products, arithmetic and copies ran while one was open for 1% of the time, Pallas kernels for 4%

profile of v3, /device:TPU:6, one launch (start us, length us, event | category | flops | bytes accessed | tf_op | source)
XLA Modules:
  0.0 198.0 jit_solution(2628523951067508140)
XLA Ops:
  0.7 1.0 copy_bitcast_fusion.2
  1.7 0.7 pad_select_fusion
  2.3 15.7 %collective-permute-start.1 = (bf16[2,16,1280]{2,1,0:T(8,128)(2,1)}, bf16[2,16,1280]{2,1,0:T(8,128)(2,1)S(1)}, u32[]{:S(2)}, u32[]{:S(2)}) collective-permute-start(bf16[2,16,1280]{2,1,0:T(8,128)(2,1)} %pad_select_fusion), channel_id=1, source_target_pairs={{0,256},{256,0},{1,257},{257,1},{2,258},{258,2},{3,259},{259,3},{4... | collective-permute-start | bytes 245768 | tf_op jit(solution)/shard_map/ppermute | solution.py:141
  18.0 25.5 %conditional.1 = (bf16[16,2,16,1280]{3,2,1,0:T(8,128)(2,1)S(1)}) conditional(s32[]{:T(128)} %convert_element_type.10, () %tuple.26, bf16[2,16,1280]{2,1,0:T(8,128)(2,1)} %pad_select_fusion), branch_computations={%region_0.1_spmd, %region_1.2_spmd} | conditional | bytes 4014088 | solution.py:156
  18.0 1.0 broadcast_in_dim.4
  19.1 24.5 %all_to_all.18 = bf16[16,2,16,1280]{3,2,1,0:T(8,128)(2,1)S(1)} all-to-all(bf16[16,2,16,1280]{3,2,1,0:T(8,128)(2,1)S(1)} %broadcast_in_dim.4), channel_id=1, replica_groups=mesh['zh'=2,'y'=4,'x'=4,'c'=2,'fac'=8] {'y','x'}, dimensions={0} | all-to-all | bytes 2621440 | tf_op jit(solution)/shard_map/cond/branch_1_fun/all_to_all | solution.py:147
  43.6 1.3 broadcast_in_dim.25
  44.9 0.1 copy-done.1
  45.0 6.0 %all-to-all-start.1 = ((bf16[16,2,16,1280]{3,2,1,0:T(8,128)(2,1)}), bf16[16,2,16,1280]{3,2,1,0:T(8,128)(2,1)S(1)}, u32[]{:S(2)}, u32[]{:S(2)}) async-start(bf16[16,2,16,1280]{3,2,1,0:T(8,128)(2,1)} %broadcast_in_dim.25), calls=%async_computation.1 | async-start | bytes 2621440 | tf_op jit(solution)/shard_map/all_to_all | solution.py:147
  51.0 1.9 collective-permute-start
  52.9 14.3 %all-to-all-done.1.far_ref = bf16[16,2,16,1280]{3,2,1,0:T(8,128)(2,1)S(1)} async-done(((bf16[16,2,16,1280]{3,2,1,0:T(8,128)(2,1)}), bf16[16,2,16,1280]{3,2,1,0:T(8,128)(2,1)S(1)}, u32[]{:S(2)}, u32[]{:S(2)}) %all-to-all-start.1) | async-done | bytes 1310752 | tf_op jit(solution)/shard_map/all_to_all | solution.py:147
  67.3 1.9 collective-permute-start.2
  69.2 0.2 reshape_broadcast_in_dim.4.cells_ref
  69.4 0.1 copy.93
  69.5 0.1 copy.127
  69.6 0.1 pad_add_fusion.sc_ref
  69.8 2.5 %collective-permute-done.2.far_other_ref = bf16[16,2,16,1280]{3,2,1,0:T(8,128)(2,1)} collective-permute-done((bf16[16,2,16,1280]{3,2,1,0:T(8,128)(2,1)S(1)}, bf16[16,2,16,1280]{3,2,1,0:T(8,128)(2,1)}, u32[]{:S(2)}, u32[]{:S(2)}) %collective-permute-start.2) | collective-permute-done | bytes 1310752 | tf_op jit(solution)/shard_map/ppermute | solution.py:141
  72.3 2.9 %place.1.w_ref = bf16[2,2,16,2,16,1280]{5,4,3,2,1,0:T(8,128)(2,1)S(1)} custom-call(s32[3]{0:T(128)S(1)} %pad_add_fusion.sc_ref, bf16[16,2,16,1280]{3,2,1,0:T(8,128)(2,1)} %copy-done.1, bf16[16,2,16,1280]{3,2,1,0:T(8,128)(2,1)S(1)} %collective-permute-done.own_other_ref, bf16[16,2,16,1280]{3,2,1,0:T(8,128)(2,1)S(1)} %all-to-all-done.1.far_ref, ...), custom_call_target="tpu_custom_call" | custom-call | tf_op jit(solution)/shard_map/place/pallas_call | solution.py:161
  75.3 2.4 %stage.11 = (f32[2,32,1024]{2,1,0:T(8,128)S(1)}, bf16[2,2,16,2,16,1280]{5,4,3,2,1,0:T(8,128)(2,1)S(1)}, bf16[4,2,32,128]{3,2,1,0:T(8,128)(2,1)S(1)}, bf16[2,32,1152]{2,1,0:T(8,128)(2,1)S(1)}) custom-call(s32[3]{0:T(128)S(1)} %pad_add_fusion.sc_ref, bf16[2,32,1152]{2,1,0:T(8,128)(2,1)S(1)} %broadcast_in_dim.24.x_ref, ...), custom_call_target="tpu_custom_call", output_to_operand_aliasing={{1}: (6, {}), {2}: (7, {})} | custom-call | flops 335544320 | bytes 5242880 | tf_op jit(solution)/shard_map/stage/pallas_call | solution.py:244
  77.7 1.3 collective-permute-start.3
  79.0 0.1 copy.126
  79.1 1.3 post.11
  80.5 2.2 %collective-permute-done.3.x_ref = bf16[2,32,1152]{2,1,0:T(8,128)(2,1)S(1)} collective-permute-done((bf16[2,32,1152]{2,1,0:T(8,128)(2,1)S(1)}, bf16[2,32,1152]{2,1,0:T(8,128)(2,1)S(1)}, u32[]{:S(2)}, u32[]{:S(2)}) %collective-permute-start.3) | collective-permute-done | bytes 147488 | tf_op jit(solution)/shard_map/ppermute | solution.py:249
  82.7 2.4 %stage.12 = (f32[2,32,1024]{2,1,0:T(8,128)S(1)}, bf16[2,2,16,2,16,1280]{5,4,3,2,1,0:T(8,128)(2,1)S(1)}, bf16[4,2,32,128]{3,2,1,0:T(8,128)(2,1)S(1)}, bf16[2,32,1152]{2,1,0:T(8,128)(2,1)S(1)}) custom-call(s32[3]{0:T(128)S(1)} %pad_add_fusion.sc_ref, ...), custom_call_target="tpu_custom_call", output_to_operand_aliasing={{1}: (6, {}), {2}: (7, {})} | custom-call | flops 335544320 | bytes 5242880 | tf_op jit(solution)/shard_map/stage/pallas_call | solution.py:244
  85.1 4.4 %collective-permute-start.4 = (bf16[2,32,1152]{2,1,0:T(8,128)(2,1)S(1)}, bf16[2,32,1152]{2,1,0:T(8,128)(2,1)S(1)}, u32[]{:S(2)}, u32[]{:S(2)}) collective-permute-start(bf16[2,32,1152]{2,1,0:T(8,128)(2,1)S(1)} %get-tuple-element.112), channel_id=1, source_target_pairs={{0,1},{1,2},{8,9},{9,10},{16,17},{17,18},{24,25},{25,26},{32,33},{... | collective-permute-start | bytes 442376 | tf_op jit(solution)/shard_map/ppermute | solution.py:249
  89.5 1.3 post.12
  90.8 1.5 collective-permute-done.4.x_ref
  92.4 2.4 %stage.13 = (f32[2,32,1024]{2,1,0:T(8,128)S(1)}, bf16[2,2,16,2,16,1280]{5,4,3,2,1,0:T(8,128)(2,1)S(1)}, bf16[4,2,32,128]{3,2,1,0:T(8,128)(2,1)S(1)}, bf16[2,32,1152]{2,1,0:T(8,128)(2,1)S(1)}) custom-call(s32[3]{0:T(128)S(1)} %pad_add_fusion.sc_ref, ...), custom_call_target="tpu_custom_call", output_to_operand_aliasing={{1}: (6, {}), {2}: (7, {})} | custom-call | flops 335544320 | bytes 5242880 | tf_op jit(solution)/shard_map/stage/pallas_call | solution.py:244
  94.8 4.4 %collective-permute-start.5 = (bf16[2,32,1152]{2,1,0:T(8,128)(2,1)S(1)}, bf16[2,32,1152]{2,1,0:T(8,128)(2,1)S(1)}, u32[]{:S(2)}, u32[]{:S(2)}) collective-permute-start(bf16[2,32,1152]{2,1,0:T(8,128)(2,1)S(1)} %get-tuple-element.121), channel_id=1, source_target_pairs={{0,1},{1,2},{2,3},{8,9},{9,10},{10,11},{16,17},{17,18},{18,19},{24... | collective-permute-start | bytes 442376 | tf_op jit(solution)/shard_map/ppermute | solution.py:249
  99.2 1.3 post.13
  100.6 1.3 collective-permute-done.5.x_ref
  101.9 2.4 %stage.14 = (f32[2,32,1024]{2,1,0:T(8,128)S(1)}, bf16[2,2,16,2,16,1280]{5,4,3,2,1,0:T(8,128)(2,1)S(1)}, bf16[4,2,32,128]{3,2,1,0:T(8,128)(2,1)S(1)}, bf16[2,32,1152]{2,1,0:T(8,128)(2,1)S(1)}) custom-call(s32[3]{0:T(128)S(1)} %pad_add_fusion.sc_ref, ...), custom_call_target="tpu_custom_call", output_to_operand_aliasing={{1}: (6, {}), {2}: (7, {})} | custom-call | flops 335544320 | bytes 5242880 | tf_op jit(solution)/shard_map/stage/pallas_call | solution.py:244
  104.3 4.4 %collective-permute-start.6 = (bf16[2,32,1152]{2,1,0:T(8,128)(2,1)S(1)}, bf16[2,32,1152]{2,1,0:T(8,128)(2,1)S(1)}, u32[]{:S(2)}, u32[]{:S(2)}) collective-permute-start(bf16[2,32,1152]{2,1,0:T(8,128)(2,1)S(1)} %get-tuple-element.130), channel_id=1, source_target_pairs={{0,1},{1,2},{2,3},{3,4},{8,9},{9,10},{10,11},{11,12},{16,17},{17,1... | collective-permute-start | bytes 442376 | tf_op jit(solution)/shard_map/ppermute | solution.py:249
  108.7 1.3 post.14
  110.0 1.3 collective-permute-done.6.x_ref
  111.4 0.5 stage.15
  111.9 0.7 collective-permute-start.7
  112.6 0.6 post.15
  113.2 0.6 stage.16
  113.7 0.7 collective-permute-start.8
  114.4 0.6 post.16
  115.0 0.6 stage.17
  115.6 0.7 collective-permute-start.9
  116.2 0.6 post.17
  116.8 0.6 stage.18
  117.4 0.7 collective-permute-start.10
  118.1 0.6 post.18
  118.6 0.6 stage.19
  119.2 0.7 collective-permute-start.11
  119.9 0.6 post.19
  120.5 0.7 stage.20
  121.2 0.8 collective-permute-start.12
  122.0 0.6 post.20
  122.6 0.6 stage.21
  123.2 0.6 post.21
  123.7 0.7 collective-permute-start.13
  124.5 21.7 %all_to_all.19 = f32[64,1,16]{2,1,0:T(1,128)S(1)} all-to-all(f32[64,1,16]{2,1,0:T(1,128)S(1)} %bitcast.83), channel_id=1, replica_groups=mesh['zh'=2,'y'=4,'x'=4,'c'=2,'fac'=8] {'zh','y','x','c'}, dimensions={0} | all-to-all | bytes 8192 | tf_op jit(solution)/shard_map/all_to_all | solution.py:259
  146.2 0.7 collective-permute-start.15
  146.9 0.7 collective-permute-start.14
  147.6 0.7 collective-permute-start.17
  148.3 1.3 collective-permute-start.16
  149.6 0.5 reduce_sum.19
  150.1 47.0 %collective-permute-done.16 = bf16[4,2,32,128]{3,2,1,0:T(8,128)(2,1)S(1)} collective-permute-done((bf16[4,2,32,128]{3,2,1,0:T(8,128)(2,1)S(1)}, bf16[4,2,32,128]{3,2,1,0:T(8,128)(2,1)S(1)}, u32[]{:S(2)}, u32[]{:S(2)}) %collective-permute-start.16) | collective-permute-done | bytes 65568 | tf_op jit(solution)/shard_map/ppermute | solution.py:264
  197.2 0.8 copy.114
  (36 shorter events, 0.3 us)
Async XLA Ops:
  0.6 68.5 %copy-start.6 = (s32[128]{0:T(128)S(1)}, s32[128]{0:T(128)}, u32[]{:S(2)}) copy-start(s32[128]{0:T(128)} %param.12) | copy-start | bytes 1540
  0.6 68.8 %copy-start.5 = (f32[128,2]{0,1:T(2,128)S(1)}, f32[128,2]{0,1:T(2,128)}, u32[]{:S(2)}) copy-start(f32[128,2]{0,1:T(2,128)} %param.13) | copy-start | bytes 3076
  0.7 68.9 %copy-start.2 = (bf16[128,2,1024]{2,1,0:T(2,128)(2,1)S(1)}, bf16[128,2,1024]{2,1,0:T(2,128)(2,1)}, u32[]{:S(2)}) copy-start(bf16[128,2,1024]{2,1,0:T(2,128)(2,1)} %param.14) | copy-start | bytes 1572868
  2.3 41.3 %collective-permute-start.1 = (bf16[2,16,1280]{2,1,0:T(8,128)(2,1)}, bf16[2,16,1280]{2,1,0:T(8,128)(2,1)S(1)}, u32[]{:S(2)}, u32[]{:S(2)}) collective-permute-start(bf16[2,16,1280]{2,1,0:T(8,128)(2,1)} %pad_select_fusion), channel_id=1, source_target_pairs={{0,256},{256,0},{1,257},{257,1},{2,258},{258,2},{3,259},{259,3},{4... | collective-permute-start | bytes 245768 | tf_op jit(solution)/shard_map/ppermute | solution.py:141
  43.6 1.5 copy-start.1
  45.0 22.2 %all-to-all-start.1 = ((bf16[16,2,16,1280]{3,2,1,0:T(8,128)(2,1)}), bf16[16,2,16,1280]{3,2,1,0:T(8,128)(2,1)S(1)}, u32[]{:S(2)}, u32[]{:S(2)}) async-start(bf16[16,2,16,1280]{3,2,1,0:T(8,128)(2,1)} %broadcast_in_dim.25), calls=%async_computation.1 | async-start | bytes 2621440 | tf_op jit(solution)/shard_map/all_to_all | solution.py:147
  51.0 18.8 %collective-permute-start = (bf16[16,2,16,1280]{3,2,1,0:T(8,128)(2,1)}, bf16[16,2,16,1280]{3,2,1,0:T(8,128)(2,1)S(1)}, u32[]{:S(2)}, u32[]{:S(2)}) collective-permute-start(bf16[16,2,16,1280]{3,2,1,0:T(8,128)(2,1)} %copy-done.1), channel_id=1, source_target_pairs={{0,8},{8,0},{1,9},{9,1},{2,10},{10,2},{3,11},{11,3},{4,12},{12,4},... | collective-permute-start | bytes 3932168 | tf_op jit(solution)/shard_map/ppermute | solution.py:141
  67.3 5.0 %collective-permute-start.2 = (bf16[16,2,16,1280]{3,2,1,0:T(8,128)(2,1)S(1)}, bf16[16,2,16,1280]{3,2,1,0:T(8,128)(2,1)}, u32[]{:S(2)}, u32[]{:S(2)}) collective-permute-start(bf16[16,2,16,1280]{3,2,1,0:T(8,128)(2,1)S(1)} %all-to-all-done.1.far_ref), channel_id=1, source_target_pairs={{0,8},{8,0},{1,9},{9,1},{2,10},{10,2},{3,11},{11,3},{4,12},{12,4},... | collective-permute-start | bytes 3932168 | tf_op jit(solution)/shard_map/ppermute | solution.py:141
  69.8 5.5 %copy-start = (s32[128,128]{1,0:T(8,128)S(1)}, s32[128,128]{1,0:T(8,128)}, u32[]{:S(2)}) copy-start(s32[128,128]{1,0:T(8,128)} %param.15) | copy-start | bytes 196612
  75.2 3.8 %copy-start.3 = (bf16[128,1,2,1024]{3,2,1,0:T(2,128)(2,1)S(1)}, bf16[128,1,2,1024]{3,2,1,0:T(2,128)(2,1)}, u32[]{:S(2)}) copy-start(bf16[128,1,2,1024]{3,2,1,0:T(2,128)(2,1)} %param.17) | copy-start | bytes 1572868
  77.7 5.0 %collective-permute-start.3 = (bf16[2,32,1152]{2,1,0:T(8,128)(2,1)S(1)}, bf16[2,32,1152]{2,1,0:T(8,128)(2,1)S(1)}, u32[]{:S(2)}, u32[]{:S(2)}) collective-permute-start(bf16[2,32,1152]{2,1,0:T(8,128)(2,1)S(1)} %get-tuple-element.105), channel_id=1, source_target_pairs={{0,1},{8,9},{16,17},{24,25},{32,33},{40,41},{48,49},{56,57},{64,65... | collective-permute-start | bytes 442376 | tf_op jit(solution)/shard_map/ppermute | solution.py:249
  85.1 7.3 %collective-permute-start.4 = (bf16[2,32,1152]{2,1,0:T(8,128)(2,1)S(1)}, bf16[2,32,1152]{2,1,0:T(8,128)(2,1)S(1)}, u32[]{:S(2)}, u32[]{:S(2)}) collective-permute-start(bf16[2,32,1152]{2,1,0:T(8,128)(2,1)S(1)} %get-tuple-element.112), channel_id=1, source_target_pairs={{0,1},{1,2},{8,9},{9,10},{16,17},{17,18},{24,25},{25,26},{32,33},{... | collective-permute-start | bytes 442376 | tf_op jit(solution)/shard_map/ppermute | solution.py:249
  94.8 7.1 %collective-permute-start.5 = (bf16[2,32,1152]{2,1,0:T(8,128)(2,1)S(1)}, bf16[2,32,1152]{2,1,0:T(8,128)(2,1)S(1)}, u32[]{:S(2)}, u32[]{:S(2)}) collective-permute-start(bf16[2,32,1152]{2,1,0:T(8,128)(2,1)S(1)} %get-tuple-element.121), channel_id=1, source_target_pairs={{0,1},{1,2},{2,3},{8,9},{9,10},{10,11},{16,17},{17,18},{18,19},{24... | collective-permute-start | bytes 442376 | tf_op jit(solution)/shard_map/ppermute | solution.py:249
  104.3 7.0 %collective-permute-start.6 = (bf16[2,32,1152]{2,1,0:T(8,128)(2,1)S(1)}, bf16[2,32,1152]{2,1,0:T(8,128)(2,1)S(1)}, u32[]{:S(2)}, u32[]{:S(2)}) collective-permute-start(bf16[2,32,1152]{2,1,0:T(8,128)(2,1)S(1)} %get-tuple-element.130), channel_id=1, source_target_pairs={{0,1},{1,2},{2,3},{3,4},{8,9},{9,10},{10,11},{11,12},{16,17},{17,1... | collective-permute-start | bytes 442376 | tf_op jit(solution)/shard_map/ppermute | solution.py:249
  111.9 1.3 collective-permute-start.7
  113.7 1.3 collective-permute-start.8
  115.6 1.3 collective-permute-start.9
  117.4 1.3 collective-permute-start.10
  119.2 1.3 collective-permute-start.11
  121.2 76.0 %copy-start.4 = (f32[128,2,128]{2,1,0:T(2,128)S(1)}, f32[128,2,128]{2,1,0:T(2,128)}, u32[]{:S(2)}) copy-start(f32[128,2,128]{2,1,0:T(2,128)} %param.16) | copy-start | bytes 393220
  121.2 1.4 collective-permute-start.12
  123.7 22.4 %collective-permute-start.13 = (bf16[4,2,32,128]{3,2,1,0:T(8,128)(2,1)S(1)}, bf16[4,2,32,128]{3,2,1,0:T(8,128)(2,1)S(1)}, u32[]{:S(2)}, u32[]{:S(2)}) collective-permute-start(bf16[4,2,32,128]{3,2,1,0:T(8,128)(2,1)S(1)} %get-tuple-element.199), channel_id=1, source_target_pairs={{7,3},{15,11},{23,19},{31,27},{39,35},{47,43},{55,51},{63,59},{71,... | collective-permute-start | bytes 196616 | tf_op jit(solution)/shard_map/ppermute | solution.py:255
  146.2 1.3 collective-permute-start.15
  146.9 0.7 collective-permute-start.14
  147.6 2.5 %collective-permute-start.17 = (bf16[4,2,32,128]{3,2,1,0:T(8,128)(2,1)S(1)}, bf16[4,2,32,128]{3,2,1,0:T(8,128)(2,1)S(1)}, u32[]{:S(2)}, u32[]{:S(2)}) collective-permute-start(bf16[4,2,32,128]{3,2,1,0:T(8,128)(2,1)S(1)} %add_add_fusion), channel_id=1, source_target_pairs={{3,4},{11,12},{19,20},{27,28},{35,36},{43,44},{51,52},{59,60},{67,... | collective-permute-start | bytes 196616 | tf_op jit(solution)/shard_map/ppermute | solution.py:264
  148.3 48.9 %collective-permute-start.16 = (bf16[4,2,32,128]{3,2,1,0:T(8,128)(2,1)S(1)}, bf16[4,2,32,128]{3,2,1,0:T(8,128)(2,1)S(1)}, u32[]{:S(2)}, u32[]{:S(2)}) collective-permute-start(bf16[4,2,32,128]{3,2,1,0:T(8,128)(2,1)S(1)} %add_add_fusion), channel_id=1, source_target_pairs={{3,2},{5,6},{1,0},{11,10},{13,14},{9,8},{19,18},{21,22},{17,16},{2... | collective-permute-start | bytes 196616 | tf_op jit(solution)/shard_map/ppermute | solution.py:264

commit v4 on v3

--- a/solution.py
+++ b/solution.py
@@ -10,29 +10,27 @@
 
 SRC = ("zh", "y", "x", "c")
 CHUNKS = 4
-GROUP = 256
+GROUP = 128
 LIMIT = 16 << 20
 SPLIT = 4
 F32, BF16 = jnp.float32, jnp.bfloat16
 NT = (((1,), (1,)), ((), ()))
-
-
-def dot_nt(rows, block):
-    return lax.dot_general(rows, block, NT, preferred_element_type=F32)
+NN = (((1,), (0,)), ((), ()))
+
+
+def multiply(block, columns, dims):
+    return lax.dot_general(block, columns, dims, preferred_element_type=F32)
 
 
 def group_block(w_ref, group, part, low, high):
-    half = group // 2
-    tiles = [
-        w_ref[c, half, 4 * y + x, part, :, low:high]
-        for y in (2 * (group % 2), 2 * (group % 2) + 1)
-        for x in range(4)
-        for c in range(2)
-    ]
+    tiles = [w_ref[c, group // 4, 4 * (group % 4) + x, part, :, low:high] for x in range(4) for c in range(2)]
     return jnp.concatenate(tiles, axis=0)
 
 
-def stage_kernel(step, chunks, stages, sc_ref, x_ref, inflow_ref, cells_ref, wave_ref, receivers_ref, w_ref, _p, field_ref, _w, picked_ref, *rest):
+def stage_kernel(
+    step, chunks, stages, sc_ref, x_ref, inflow_ref, cells_ref, wave_ref, receivers_ref, w_ref, _p,
+    field_ref, _w, picked_ref, *rest
+):
     v_ref = rest[-1]
     last = step == chunks + stages - 2
     owner = sc_ref[0]
@@ -56,22 +54,21 @@
         crossed = jnp.concatenate([-straight[m:], straight[:m]], axis=0)
         cells = cells_ref[chunk] - owner * width
         waves = wave_ref[chunk]
-        lanes = lax.broadcasted_iota(jnp.int32, (m, GROUP), 1)
-        reduced = []
+        rows = lax.broadcasted_iota(jnp.int32, (GROUP, 2 * m), 0)
+        reduced, turned = [], []
         for g in range(groups):
             low = GROUP * g
-            acc = dot_nt(straight[:, low:], group_block(w_ref, g, 0, low + GROUP, width + GROUP))
-            acc += dot_nt(crossed[:, low:], group_block(w_ref, g, 1, low + GROUP, width + GROUP))
-            hit = lanes + low == cells
-            term = jnp.concatenate([jnp.where(hit, waves[:, p : p + 1], 0.0) for p in range(2)], axis=0)
-            reduced.append((term - acc).astype(BF16))
-        straight = jnp.concatenate(reduced, axis=1)
-        crossed = jnp.concatenate([-straight[m:], straight[:m]], axis=0)
+            acc = multiply(group_block(w_ref, g, 0, low + GROUP, width + GROUP), straight[:, low:], NT)
+            acc += multiply(group_block(w_ref, g, 1, low + GROUP, width + GROUP), crossed[:, low:], NT)
+            value = jnp.where(rows + low == cells, waves, 0.0) - acc
+            reduced.append(value.astype(BF16))
+            turned.append(jnp.concatenate([-value[:, m:], value[:, :m]], axis=1).astype(BF16))
+        reduced, turned = jnp.concatenate(reduced, axis=0), jnp.concatenate(turned, axis=0)
         for g in range(groups):
             low, high = GROUP * g, GROUP * (g + 1)
-            acc = dot_nt(straight[:, :high], group_block(w_ref, g, 0, 0, high))
-            acc += dot_nt(crossed[:, :high], group_block(w_ref, g, 1, 0, high))
-            acc = acc.reshape(2, m, GROUP)
+            acc = multiply(group_block(w_ref, g, 0, 0, high), reduced[:high], NN)
+            acc += multiply(group_block(w_ref, g, 1, 0, high), turned[:high], NN)
+            acc = acc.T.reshape(2, m, GROUP)
             field_ref[:, :, low:high] = acc
             if not last:
                 rest[0][:, :, low:high] = acc.astype(BF16)
@@ -147,13 +144,9 @@
     return lax.all_to_all(spread, ("y", "x"), 0, 0, tiled=True)
 
 
-def empty_plane(piece):
-    return jnp.zeros((lax.axis_size(("y", "x")),) + piece.shape, piece.dtype)
-
-
 def gather_factor(packed, where):
     far = swap(packed, "zh")
-    own = lax.cond(where[0] < lax.axis_size("fac"), plane_gather, empty_plane, packed)
+    own = plane_gather(packed)
     own_other = swap(own, "c")
     far = plane_gather(far)
     far_other = swap(far, "c")
@@ -198,7 +191,9 @@
     factor = gather_factor(packed, where)
     adjoint = by_chunk(adjoint[:, 0]).transpose(0, 2, 1, 3)
     observed = by_chunk(observed).transpose(0, 2, 1, 3)
-    cells, waves, receivers = by_chunk(source_cell[:, None]), by_chunk(source_wave), by_chunk(receiver_cell)
+    cells = jnp.tile(by_chunk(source_cell)[:, None], (1, 1, 2))
+    waves = by_chunk(source_wave).transpose(0, 2, 1).reshape(CHUNKS, 1, 2 * m)
+    receivers = by_chunk(receiver_cell)
 
     steps = CHUNKS + stages - 1
     vmem = pl.BlockSpec(memory_space=pltpu.VMEM)

time: 199 us -> 192 us (0.965)
  blocking collectives: 46.2 us -> 33.1 us
  starting transfers between devices: 48.1 us -> 56.6 us
    all_to_all x1 -> x0, blocking collectives: 24.5 us -> none  [plane_gather(): return lax.all_to_all(spread, ('y', 'x'), 0, 0, tiled=True)]
    all_to_all x1, blocking collectives: 21.7 us -> 33.1 us  [per_device(): terms = lax.all_to_all(terms, SRC, 0, 0, tiled=True)]
    all_to_all x1 -> x2, starting transfers between devices: 5.98 us -> 16.6 us  [plane_gather(): return lax.all_to_all(spread, ('y', 'x'), 0, 0, tiled=True)]
    all_to_all x1 -> x2, waiting for transfers between devices: 14.3 us -> 10.8 us  [plane_gather(): return lax.all_to_all(spread, ('y', 'x'), 0, 0, tiled=True)]
    ppermute x3, waiting for transfers between devices: 2.52 us -> 5.52 us  [swap(): return lax.ppermute(array, axis, [(0, 1), (1, 0)])]
  transfers between devices with their start and end apart: 19 -> 20, of which waited for: 7 -> 8; matrix products, arithmetic and copies ran while one was open for 1% -> 1% of each run, Pallas kernels for 4% -> 5%
where the time goes in v4:
time: 192 us; the launch traced here: 191 us
  waiting for transfers between devices  69 us (36%)
  starting transfers between devices  56.6 us (29%)
  blocking collectives  33.1 us (17%)
  Pallas kernels  24.3 us (13%)
  local copies, waits for them, and re-layouts  4.82 us (3%)
    ppermute x4, waiting for transfers between devices, per_device(): lax.ppermute(picked, 'fac', p)  46.3 us
    all_to_all x1, blocking collectives, per_device(): terms = lax.all_to_all(terms, SRC, 0, 0, tiled=True)  33.1 us
    ppermute x10, starting transfers between devices, per_device(): x = lax.ppermute(y[0], 'fac', pairs)  18.5 us
    ppermute x3, starting transfers between devices, swap(): return lax.ppermute(array, axis, [(0, 1), (1, 0)])  17.6 us
    all_to_all x2, starting transfers between devices, plane_gather(): return lax.all_to_all(spread, ('y', 'x'), 0, 0, tiled=True)  16.6 us
    pallas_call x11, Pallas kernels, per_device(): stage(t)  12.4 us
    all_to_all x2, waiting for transfers between devices, plane_gather(): return lax.all_to_all(spread, ('y', 'x'), 0, 0, tiled=True)  10.8 us
    pallas_call x11, Pallas kernels, per_device(): done = post(t)(where, field, adjoint, *done)  9.23 us
  transfers between devices with their start and end apart: 20, of which 8 were waited for; matrix products, arithmetic and copies ran while one was open for 1% of the time, Pallas kernels for 5%

profile of v4, /device:TPU:6, one launch (start us, length us, event | category | flops | bytes accessed | tf_op | source)
XLA Modules:
  0.0 190.8 jit_solution(14011058695006785690)
XLA Ops:
  0.7 1.0 broadcast_select_fusion
  1.7 1.1 broadcast_in_dim.25
  2.8 9.4 %all-to-all-start = ((bf16[16,2,16,1152]{3,2,1,0:T(8,128)(2,1)}), bf16[16,2,16,1152]{3,2,1,0:T(8,128)(2,1)S(1)}, u32[]{:S(2)}, u32[]{:S(2)}) async-start(bf16[16,2,16,1152]{3,2,1,0:T(8,128)(2,1)} %broadcast_in_dim.25), calls=%async_computation | async-start | bytes 2359296 | tf_op jit(solution)/shard_map/all_to_all | solution.py:144
  12.2 13.8 %collective-permute-start.1 = (bf16[2,16,1152]{2,0,1:T(2,128)(2,1)S(1)}, bf16[2,16,1152]{2,0,1:T(2,128)(2,1)S(1)}, u32[]{:S(2)}, u32[]{:S(2)}) collective-permute-start(bf16[2,16,1152]{2,0,1:T(2,128)(2,1)S(1)} %broadcast_select_fusion), channel_id=1, source_target_pairs={{0,256},{256,0},{1,257},{257,1},{2,258},{258,2},{3,259},{259,3},{4... | collective-permute-start | bytes 221192 | tf_op jit(solution)/shard_map/ppermute | solution.py:138
  26.0 4.2 %collective-permute-done.1 = bf16[2,16,1152]{2,0,1:T(2,128)(2,1)S(1)} collective-permute-done((bf16[2,16,1152]{2,0,1:T(2,128)(2,1)S(1)}, bf16[2,16,1152]{2,0,1:T(2,128)(2,1)S(1)}, u32[]{:S(2)}, u32[]{:S(2)}) %collective-permute-start.1) | collective-permute-done | bytes 73760 | tf_op jit(solution)/shard_map/ppermute | solution.py:138
  30.2 1.1 broadcast_in_dim.26
  31.4 7.2 %all-to-all-start.1 = ((bf16[16,2,16,1152]{3,2,1,0:T(8,128)(2,1)}), bf16[16,2,16,1152]{3,2,1,0:T(8,128)(2,1)S(1)}, u32[]{:S(2)}, u32[]{:S(2)}) async-start(bf16[16,2,16,1152]{3,2,1,0:T(8,128)(2,1)} %broadcast_in_dim.26), calls=%async_computation.1 | async-start | bytes 2359296 | tf_op jit(solution)/shard_map/all_to_all | solution.py:144
  38.6 1.9 %collective-permute-start = (bf16[16,2,16,1152]{3,2,1,0:T(8,128)(2,1)S(1)}, bf16[16,2,16,1152]{3,2,1,0:T(8,128)(2,1)S(1)}, u32[]{:S(2)}, u32[]{:S(2)}) collective-permute-start(bf16[16,2,16,1152]{3,2,1,0:T(8,128)(2,1)S(1)} %all-to-all-done.own_ref), channel_id=1, source_target_pairs={{0,8},{8,0},{1,9},{9,1},{2,10},{10,2},{3,11},{11,3},{4,12},{12,4},... | collective-permute-start | bytes 3538952 | tf_op jit(solution)/shard_map/ppermute | solution.py:138
  40.5 10.8 %all-to-all-done.1.far_ref = bf16[16,2,16,1152]{3,2,1,0:T(8,128)(2,1)S(1)} async-done(((bf16[16,2,16,1152]{3,2,1,0:T(8,128)(2,1)}), bf16[16,2,16,1152]{3,2,1,0:T(8,128)(2,1)S(1)}, u32[]{:S(2)}, u32[]{:S(2)}) %all-to-all-start.1) | async-done | bytes 1179680 | tf_op jit(solution)/shard_map/all_to_all | solution.py:144
  51.3 1.9 %collective-permute-start.2 = (bf16[16,2,16,1152]{3,2,1,0:T(8,128)(2,1)S(1)}, bf16[16,2,16,1152]{3,2,1,0:T(8,128)(2,1)}, u32[]{:S(2)}, u32[]{:S(2)}) collective-permute-start(bf16[16,2,16,1152]{3,2,1,0:T(8,128)(2,1)S(1)} %all-to-all-done.1.far_ref), channel_id=1, source_target_pairs={{0,8},{8,0},{1,9},{9,1},{2,10},{10,2},{3,11},{11,3},{4,12},{12,4},... | collective-permute-start | bytes 3538952 | tf_op jit(solution)/shard_map/ppermute | solution.py:138
  53.2 0.1 tile.10
  53.3 0.1 tile.12.cells_ref
  53.4 0.1 reshape.49
  53.5 0.1 reshape.50.wave_ref
  53.6 1.2 copy.93
  54.7 0.1 pad_add_fusion.sc_ref
  54.9 1.3 collective-permute-done.2.far_other_ref
  56.2 2.6 %place.1.w_ref = bf16[2,2,16,2,16,1152]{5,4,3,2,1,0:T(8,128)(2,1)S(1)} custom-call(s32[3]{0:T(128)S(1)} %pad_add_fusion.sc_ref, bf16[16,2,16,1152]{3,2,1,0:T(8,128)(2,1)S(1)} %all-to-all-done.own_ref, bf16[16,2,16,1152]{3,2,1,0:T(8,128)(2,1)S(1)} %collective-permute-done.own_other_ref, bf16[16,2,16,1152]{3,2,1,0:T(8,128)(2,1)S(1)} %all-to-all-done.1.far_ref, ...), custom_call_target="tpu_custom_call" | custom-call | tf_op jit(solution)/shard_map/place/pallas_call | solution.py:154
  58.9 2.1 %stage.11 = (f32[2,32,1024]{2,1,0:T(8,128)S(1)}, bf16[2,2,16,2,16,1152]{5,4,3,2,1,0:T(8,128)(2,1)S(1)}, bf16[4,2,32,128]{3,2,1,0:T(8,128)(2,1)S(1)}, bf16[2,32,1152]{2,1,0:T(8,128)(2,1)S(1)}) custom-call(s32[3]{0:T(128)S(1)} %pad_add_fusion.sc_ref, bf16[2,32,1152]{2,1,0:T(8,128)(2,1)S(1)} %broadcast_in_dim.24.x_ref, ...), custom_call_target="tpu_custom_call", output_to_operand_aliasing={{1}: (6, {}), {2}: (7, {})} | custom-call | flops 335544320 | bytes 4718592 | tf_op jit(solution)/shard_map/stage/pallas_call | solution.py:239
  61.0 1.3 collective-permute-start.3
  62.3 0.1 copy.92
  62.4 1.3 post.11
  63.7 2.2 %collective-permute-done.3.x_ref = bf16[2,32,1152]{2,1,0:T(8,128)(2,1)S(1)} collective-permute-done((bf16[2,32,1152]{2,1,0:T(8,128)(2,1)S(1)}, bf16[2,32,1152]{2,1,0:T(8,128)(2,1)S(1)}, u32[]{:S(2)}, u32[]{:S(2)}) %collective-permute-start.3) | collective-permute-done | bytes 147488 | tf_op jit(solution)/shard_map/ppermute | solution.py:244
  65.9 2.1 %stage.12 = (f32[2,32,1024]{2,1,0:T(8,128)S(1)}, bf16[2,2,16,2,16,1152]{5,4,3,2,1,0:T(8,128)(2,1)S(1)}, bf16[4,2,32,128]{3,2,1,0:T(8,128)(2,1)S(1)}, bf16[2,32,1152]{2,1,0:T(8,128)(2,1)S(1)}) custom-call(s32[3]{0:T(128)S(1)} %pad_add_fusion.sc_ref, ...), custom_call_target="tpu_custom_call", output_to_operand_aliasing={{1}: (6, {}), {2}: (7, {})} | custom-call | flops 335544320 | bytes 4718592 | tf_op jit(solution)/shard_map/stage/pallas_call | solution.py:239
  68.0 4.4 %collective-permute-start.4 = (bf16[2,32,1152]{2,1,0:T(8,128)(2,1)S(1)}, bf16[2,32,1152]{2,1,0:T(8,128)(2,1)S(1)}, u32[]{:S(2)}, u32[]{:S(2)}) collective-permute-start(bf16[2,32,1152]{2,1,0:T(8,128)(2,1)S(1)} %get-tuple-element.108), channel_id=1, source_target_pairs={{0,1},{1,2},{8,9},{9,10},{16,17},{17,18},{24,25},{25,26},{32,33},{... | collective-permute-start | bytes 442376 | tf_op jit(solution)/shard_map/ppermute | solution.py:244
  72.5 1.3 post.12
  73.8 1.5 collective-permute-done.4.x_ref
  75.3 2.1 %stage.13 = (f32[2,32,1024]{2,1,0:T(8,128)S(1)}, bf16[2,2,16,2,16,1152]{5,4,3,2,1,0:T(8,128)(2,1)S(1)}, bf16[4,2,32,128]{3,2,1,0:T(8,128)(2,1)S(1)}, bf16[2,32,1152]{2,1,0:T(8,128)(2,1)S(1)}) custom-call(s32[3]{0:T(128)S(1)} %pad_add_fusion.sc_ref, ...), custom_call_target="tpu_custom_call", output_to_operand_aliasing={{1}: (6, {}), {2}: (7, {})} | custom-call | flops 335544320 | bytes 4718592 | tf_op jit(solution)/shard_map/stage/pallas_call | solution.py:239
  77.4 4.4 %collective-permute-start.5 = (bf16[2,32,1152]{2,1,0:T(8,128)(2,1)S(1)}, bf16[2,32,1152]{2,1,0:T(8,128)(2,1)S(1)}, u32[]{:S(2)}, u32[]{:S(2)}) collective-permute-start(bf16[2,32,1152]{2,1,0:T(8,128)(2,1)S(1)} %get-tuple-element.117), channel_id=1, source_target_pairs={{0,1},{1,2},{2,3},{8,9},{9,10},{10,11},{16,17},{17,18},{18,19},{24... | collective-permute-start | bytes 442376 | tf_op jit(solution)/shard_map/ppermute | solution.py:244
  81.8 1.3 post.13
  83.2 1.3 collective-permute-done.5.x_ref
  84.5 2.1 %stage.14 = (f32[2,32,1024]{2,1,0:T(8,128)S(1)}, bf16[2,2,16,2,16,1152]{5,4,3,2,1,0:T(8,128)(2,1)S(1)}, bf16[4,2,32,128]{3,2,1,0:T(8,128)(2,1)S(1)}, bf16[2,32,1152]{2,1,0:T(8,128)(2,1)S(1)}) custom-call(s32[3]{0:T(128)S(1)} %pad_add_fusion.sc_ref, ...), custom_call_target="tpu_custom_call", output_to_operand_aliasing={{1}: (6, {}), {2}: (7, {})} | custom-call | flops 335544320 | bytes 4718592 | tf_op jit(solution)/shard_map/stage/pallas_call | solution.py:239
  86.6 4.4 %collective-permute-start.6 = (bf16[2,32,1152]{2,1,0:T(8,128)(2,1)S(1)}, bf16[2,32,1152]{2,1,0:T(8,128)(2,1)S(1)}, u32[]{:S(2)}, u32[]{:S(2)}) collective-permute-start(bf16[2,32,1152]{2,1,0:T(8,128)(2,1)S(1)} %get-tuple-element.126), channel_id=1, source_target_pairs={{0,1},{1,2},{2,3},{3,4},{8,9},{9,10},{10,11},{11,12},{16,17},{17,1... | collective-permute-start | bytes 442376 | tf_op jit(solution)/shard_map/ppermute | solution.py:244
  91.0 1.3 post.14
  92.3 1.3 collective-permute-done.6.x_ref
  93.6 0.5 stage.15
  94.2 0.7 collective-permute-start.7
  94.8 0.6 post.15
  95.4 0.6 stage.16
  96.0 0.7 collective-permute-start.8
  96.7 0.6 post.16
  97.3 0.7 stage.17
  98.0 0.7 collective-permute-start.9
  98.7 0.6 post.17
  99.3 0.6 stage.18
  99.8 0.7 collective-permute-start.10
  100.5 0.6 post.18
  101.1 0.6 stage.19
  101.6 0.7 collective-permute-start.11
  102.3 0.6 post.19
  102.9 0.6 stage.20
  103.5 0.7 collective-permute-start.12
  104.1 0.6 post.20
  104.7 0.6 stage.21
  105.3 0.6 post.21
  105.9 0.7 collective-permute-start.13
  106.6 33.1 %all_to_all.19 = f32[64,1,16]{2,1,0:T(1,128)S(1)} all-to-all(f32[64,1,16]{2,1,0:T(1,128)S(1)} %bitcast.74), channel_id=1, replica_groups=mesh['zh'=2,'y'=4,'x'=4,'c'=2,'fac'=8] {'zh','y','x','c'}, dimensions={0} | all-to-all | bytes 8192 | tf_op jit(solution)/shard_map/all_to_all | solution.py:254
  139.8 0.7 collective-permute-start.15
  140.4 0.7 collective-permute-start.14
  141.2 0.7 collective-permute-start.17
  141.8 1.3 collective-permute-start.16
  143.1 0.5 reduce_sum.19
  143.7 46.3 %collective-permute-done.16 = bf16[4,2,32,128]{3,2,1,0:T(8,128)(2,1)S(1)} collective-permute-done((bf16[4,2,32,128]{3,2,1,0:T(8,128)(2,1)S(1)}, bf16[4,2,32,128]{3,2,1,0:T(8,128)(2,1)S(1)}, u32[]{:S(2)}, u32[]{:S(2)}) %collective-permute-start.16) | collective-permute-done | bytes 65568 | tf_op jit(solution)/shard_map/ppermute | solution.py:259
  190.0 0.8 copy.81
  (37 shorter events, 0.3 us)
Async XLA Ops:
  0.6 52.6 %copy-start.4 = (s32[128]{0:T(128)S(1)}, s32[128]{0:T(128)}, u32[]{:S(2)}) copy-start(s32[128]{0:T(128)} %param.10) | copy-start | bytes 1540
  0.6 52.8 %copy-start.3 = (f32[128,2]{0,1:T(2,128)S(1)}, f32[128,2]{0,1:T(2,128)}, u32[]{:S(2)}) copy-start(f32[128,2]{0,1:T(2,128)} %param.11) | copy-start | bytes 3076
  2.8 27.4 %all-to-all-start = ((bf16[16,2,16,1152]{3,2,1,0:T(8,128)(2,1)}), bf16[16,2,16,1152]{3,2,1,0:T(8,128)(2,1)S(1)}, u32[]{:S(2)}, u32[]{:S(2)}) async-start(bf16[16,2,16,1152]{3,2,1,0:T(8,128)(2,1)} %broadcast_in_dim.25), calls=%async_computation | async-start | bytes 2359296 | tf_op jit(solution)/shard_map/all_to_all | solution.py:144
  12.2 18.0 %collective-permute-start.1 = (bf16[2,16,1152]{2,0,1:T(2,128)(2,1)S(1)}, bf16[2,16,1152]{2,0,1:T(2,128)(2,1)S(1)}, u32[]{:S(2)}, u32[]{:S(2)}) collective-permute-start(bf16[2,16,1152]{2,0,1:T(2,128)(2,1)S(1)} %broadcast_select_fusion), channel_id=1, source_target_pairs={{0,256},{256,0},{1,257},{257,1},{2,258},{258,2},{3,259},{259,3},{4... | collective-permute-start | bytes 221192 | tf_op jit(solution)/shard_map/ppermute | solution.py:138
  31.4 19.9 %all-to-all-start.1 = ((bf16[16,2,16,1152]{3,2,1,0:T(8,128)(2,1)}), bf16[16,2,16,1152]{3,2,1,0:T(8,128)(2,1)S(1)}, u32[]{:S(2)}, u32[]{:S(2)}) async-start(bf16[16,2,16,1152]{3,2,1,0:T(8,128)(2,1)} %broadcast_in_dim.26), calls=%async_computation.1 | async-start | bytes 2359296 | tf_op jit(solution)/shard_map/all_to_all | solution.py:144
  38.6 16.3 %collective-permute-start = (bf16[16,2,16,1152]{3,2,1,0:T(8,128)(2,1)S(1)}, bf16[16,2,16,1152]{3,2,1,0:T(8,128)(2,1)S(1)}, u32[]{:S(2)}, u32[]{:S(2)}) collective-permute-start(bf16[16,2,16,1152]{3,2,1,0:T(8,128)(2,1)S(1)} %all-to-all-done.own_ref), channel_id=1, source_target_pairs={{0,8},{8,0},{1,9},{9,1},{2,10},{10,2},{3,11},{11,3},{4,12},{12,4},... | collective-permute-start | bytes 3538952 | tf_op jit(solution)/shard_map/ppermute | solution.py:138
  51.3 4.9 %collective-permute-start.2 = (bf16[16,2,16,1152]{3,2,1,0:T(8,128)(2,1)S(1)}, bf16[16,2,16,1152]{3,2,1,0:T(8,128)(2,1)}, u32[]{:S(2)}, u32[]{:S(2)}) collective-permute-start(bf16[16,2,16,1152]{3,2,1,0:T(8,128)(2,1)S(1)} %all-to-all-done.1.far_ref), channel_id=1, source_target_pairs={{0,8},{8,0},{1,9},{9,1},{2,10},{10,2},{3,11},{11,3},{4,12},{12,4},... | collective-permute-start | bytes 3538952 | tf_op jit(solution)/shard_map/ppermute | solution.py:138
  54.9 4.0 %copy-start = (s32[128,128]{1,0:T(8,128)S(1)}, s32[128,128]{1,0:T(8,128)}, u32[]{:S(2)}) copy-start(s32[128,128]{1,0:T(8,128)} %param.13) | copy-start | bytes 196612
  58.8 3.5 %copy-start.1 = (bf16[128,1,2,1024]{3,2,1,0:T(2,128)(2,1)S(1)}, bf16[128,1,2,1024]{3,2,1,0:T(2,128)(2,1)}, u32[]{:S(2)}) copy-start(bf16[128,1,2,1024]{3,2,1,0:T(2,128)(2,1)} %param.15) | copy-start | bytes 1572868
  61.0 5.0 %collective-permute-start.3 = (bf16[2,32,1152]{2,1,0:T(8,128)(2,1)S(1)}, bf16[2,32,1152]{2,1,0:T(8,128)(2,1)S(1)}, u32[]{:S(2)}, u32[]{:S(2)}) collective-permute-start(bf16[2,32,1152]{2,1,0:T(8,128)(2,1)S(1)} %get-tuple-element.101), channel_id=1, source_target_pairs={{0,1},{8,9},{16,17},{24,25},{32,33},{40,41},{48,49},{56,57},{64,65... | collective-permute-start | bytes 442376 | tf_op jit(solution)/shard_map/ppermute | solution.py:244
  68.0 7.3 %collective-permute-start.4 = (bf16[2,32,1152]{2,1,0:T(8,128)(2,1)S(1)}, bf16[2,32,1152]{2,1,0:T(8,128)(2,1)S(1)}, u32[]{:S(2)}, u32[]{:S(2)}) collective-permute-start(bf16[2,32,1152]{2,1,0:T(8,128)(2,1)S(1)} %get-tuple-element.108), channel_id=1, source_target_pairs={{0,1},{1,2},{8,9},{9,10},{16,17},{17,18},{24,25},{25,26},{32,33},{... | collective-permute-start | bytes 442376 | tf_op jit(solution)/shard_map/ppermute | solution.py:244
  77.4 7.1 %collective-permute-start.5 = (bf16[2,32,1152]{2,1,0:T(8,128)(2,1)S(1)}, bf16[2,32,1152]{2,1,0:T(8,128)(2,1)S(1)}, u32[]{:S(2)}, u32[]{:S(2)}) collective-permute-start(bf16[2,32,1152]{2,1,0:T(8,128)(2,1)S(1)} %get-tuple-element.117), channel_id=1, source_target_pairs={{0,1},{1,2},{2,3},{8,9},{9,10},{10,11},{16,17},{17,18},{18,19},{24... | collective-permute-start | bytes 442376 | tf_op jit(solution)/shard_map/ppermute | solution.py:244
  86.6 7.0 %collective-permute-start.6 = (bf16[2,32,1152]{2,1,0:T(8,128)(2,1)S(1)}, bf16[2,32,1152]{2,1,0:T(8,128)(2,1)S(1)}, u32[]{:S(2)}, u32[]{:S(2)}) collective-permute-start(bf16[2,32,1152]{2,1,0:T(8,128)(2,1)S(1)} %get-tuple-element.126), channel_id=1, source_target_pairs={{0,1},{1,2},{2,3},{3,4},{8,9},{9,10},{10,11},{11,12},{16,17},{17,1... | collective-permute-start | bytes 442376 | tf_op jit(solution)/shard_map/ppermute | solution.py:244
  94.2 1.3 collective-permute-start.7
  96.0 1.3 collective-permute-start.8
  98.0 1.3 collective-permute-start.9
  99.8 1.3 collective-permute-start.10
  101.6 1.3 collective-permute-start.11
  103.5 1.3 collective-permute-start.12
  104.1 85.8 %copy-start.2 = (f32[128,2,128]{2,1,0:T(2,128)S(1)}, f32[128,2,128]{2,1,0:T(2,128)}, u32[]{:S(2)}) copy-start(f32[128,2,128]{2,1,0:T(2,128)} %param.14) | copy-start | bytes 393220
  105.9 33.9 %collective-permute-start.13 = (bf16[4,2,32,128]{3,2,1,0:T(8,128)(2,1)S(1)}, bf16[4,2,32,128]{3,2,1,0:T(8,128)(2,1)S(1)}, u32[]{:S(2)}, u32[]{:S(2)}) collective-permute-start(bf16[4,2,32,128]{3,2,1,0:T(8,128)(2,1)S(1)} %get-tuple-element.195), channel_id=1, source_target_pairs={{7,3},{15,11},{23,19},{31,27},{39,35},{47,43},{55,51},{63,59},{71,... | collective-permute-start | bytes 196616 | tf_op jit(solution)/shard_map/ppermute | solution.py:250
  139.8 1.3 collective-permute-start.15
  140.4 0.7 collective-permute-start.14
  141.2 2.5 %collective-permute-start.17 = (bf16[4,2,32,128]{3,2,1,0:T(8,128)(2,1)S(1)}, bf16[4,2,32,128]{3,2,1,0:T(8,128)(2,1)S(1)}, u32[]{:S(2)}, u32[]{:S(2)}) collective-permute-start(bf16[4,2,32,128]{3,2,1,0:T(8,128)(2,1)S(1)} %add_add_fusion), channel_id=1, source_target_pairs={{3,4},{11,12},{19,20},{27,28},{35,36},{43,44},{51,52},{59,60},{67,... | collective-permute-start | bytes 196616 | tf_op jit(solution)/shard_map/ppermute | solution.py:259
  141.8 48.1 %collective-permute-start.16 = (bf16[4,2,32,128]{3,2,1,0:T(8,128)(2,1)S(1)}, bf16[4,2,32,128]{3,2,1,0:T(8,128)(2,1)S(1)}, u32[]{:S(2)}, u32[]{:S(2)}) collective-permute-start(bf16[4,2,32,128]{3,2,1,0:T(8,128)(2,1)S(1)} %add_add_fusion), channel_id=1, source_target_pairs={{3,2},{5,6},{1,0},{11,10},{13,14},{9,8},{19,18},{21,22},{17,16},{2... | collective-permute-start | bytes 196616 | tf_op jit(solution)/shard_map/ppermute | solution.py:259

commit v5 on v4

--- a/solution.py
+++ b/solution.py
@@ -9,7 +9,7 @@
 from jax.sharding import Mesh, PartitionSpec as P
 
 SRC = ("zh", "y", "x", "c")
-CHUNKS = 4
+CHUNK = 48
 GROUP = 128
 LIMIT = 16 << 20
 SPLIT = 4
@@ -25,6 +25,10 @@
 def group_block(w_ref, group, part, low, high):
     tiles = [w_ref[c, group // 4, 4 * (group % 4) + x, part, :, low:high] for x in range(4) for c in range(2)]
     return jnp.concatenate(tiles, axis=0)
+
+
+def first_row(chunk, m, sources):
+    return pl.multiple_of(jnp.minimum(chunk * m, sources - m), 16)
 
 
 def stage_kernel(
@@ -40,15 +44,17 @@
 
     @pl.when((chunk >= 0) & (chunk < chunks))
     def _():
+        held = pl.ds(first_row(chunk, m, receivers_ref.shape[0]), m)
+
         @pl.when(owner == 0)
         def _():
             v_ref[...] = inflow_ref[...].reshape(1, 2 * m, width)
-            picked_ref[chunk] = jnp.zeros(picked_ref.shape[1:], BF16)
+            picked_ref[:, held] = jnp.zeros((2, m, 128), BF16)
 
         @pl.when(owner != 0)
         def _():
             v_ref[...] = x_ref[:, :, :width].reshape(1, 2 * m, width)
-            picked_ref[chunk] = x_ref[:, :, width:]
+            picked_ref[:, held] = x_ref[:, :, width:]
 
         straight = v_ref[0]
         crossed = jnp.concatenate([-straight[m:], straight[:m]], axis=0)
@@ -72,7 +78,7 @@
             field_ref[:, :, low:high] = acc
             if not last:
                 rest[0][:, :, low:high] = acc.astype(BF16)
-        local = receivers_ref[chunk] - owner * width
+        local = receivers_ref[held, :] - owner * width
         tile, lane = local >> 7, local & 127
         for p in range(2):
             got = jnp.zeros((m, 128), F32)
@@ -80,8 +86,8 @@
                 part = field_ref[p, :, 128 * t : 128 * (t + 1)]
                 part = jnp.take_along_axis(part, lane, axis=1, mode="promise_in_bounds")
                 got = jnp.where(tile == t, part, got)
-            total = picked_ref[chunk, p] + got.astype(BF16)
-            picked_ref[chunk, p] = total
+            total = picked_ref[p, held] + got.astype(BF16)
+            picked_ref[p, held] = total
             if not last:
                 rest[0][p, :, width:] = total
 
@@ -102,12 +108,15 @@
 
     @pl.when((chunk >= 0) & (chunk < chunks))
     def _():
+        start = first_row(chunk, m, wave_out.shape[0])
         field = field_ref[...]
         for p in range(2):
             rows_ref[:, p, :] = field[p]
-        store = pltpu.make_async_copy(rows_ref, wave_out.at[pl.ds(chunk * m, m)], sem)
+        store = pltpu.make_async_copy(rows_ref, wave_out.at[pl.ds(start, m)], sem)
         store.start()
-        prod = field * adjoint_ref[chunk].astype(F32)
+        prod = field * adjoint_ref[:, pl.ds(start, m), :].astype(F32)
+        fresh = lax.broadcasted_iota(jnp.int32, prod.shape, 1) >= chunk * m - start
+        prod = jnp.where(fresh, prod, 0.0)
         grad_out[...] += jnp.sum(prod.reshape(2 * m // 8, 8, width), axis=0)
         store.wait()
 
@@ -144,11 +153,12 @@
     return lax.all_to_all(spread, ("y", "x"), 0, 0, tiled=True)
 
 
-def gather_factor(packed, where):
+def gather_factor(packed, where, others):
     far = swap(packed, "zh")
     own = plane_gather(packed)
     own_other = swap(own, "c")
     far = plane_gather(far)
+    far, others = lax.optimization_barrier((far, others))
     far_other = swap(far, "c")
     anywhere = pl.BlockSpec(memory_space=pl.ANY)
     return pl.pallas_call(
@@ -159,14 +169,14 @@
         scratch_shapes=[pltpu.SemaphoreType.DMA((4, SPLIT))],
         compiler_params=pltpu.CompilerParams(vmem_limit_bytes=LIMIT),
         name="place",
-    )(where, own, own_other, far, far_other)
+    )(where, own, own_other, far, far_other), *others
 
 
 def fan_out(stages):
     last = stages - 1
     if stages != 8:
         return [[[(last, i)] for i in range(last)]]
-    return [[[(7, 3)]], [[(3, 1)], [(3, 5)]], [[(3, 2), (5, 6), (1, 0)], [(3, 4)]]]
+    return [[[(7, 1)], [(7, 4)], [(7, 5)], [(7, 6)]], [[(1, 0), (4, 3), (5, 2)]]]
 
 
 def per_device(lower, coupling, source_cell, source_wave, inflow, receiver_cell, observed, adjoint):
@@ -176,7 +186,8 @@
     width = lower.shape[3]
     rows = lower.shape[1]
     sources = source_cell.shape[0]
-    m = sources // CHUNKS
+    m = min(CHUNK, sources)
+    chunks = -(-sources // m)
 
     split = (src // (GROUP // rows) + 1) * GROUP
     low = jnp.pad(lower[0].transpose(1, 0, 2), ((0, 0), (0, 0), (0, GROUP)))
@@ -184,26 +195,22 @@
     packed = jnp.where(lax.broadcasted_iota(jnp.int32, low.shape, 2) < split, low, high)
     where = jnp.stack([owner, lax.axis_index("zh"), lax.axis_index("c")])
 
-    def by_chunk(array):
-        return array.reshape((CHUNKS, m) + array.shape[1:])
-
-    inflow = by_chunk(inflow).transpose(0, 2, 1, 3)
-    factor = gather_factor(packed, where)
-    adjoint = by_chunk(adjoint[:, 0]).transpose(0, 2, 1, 3)
-    observed = by_chunk(observed).transpose(0, 2, 1, 3)
-    cells = jnp.tile(by_chunk(source_cell)[:, None], (1, 1, 2))
-    waves = by_chunk(source_wave).transpose(0, 2, 1).reshape(CHUNKS, 1, 2 * m)
-    receivers = by_chunk(receiver_cell)
-
-    steps = CHUNKS + stages - 1
+    starts = [min(m * i, sources - m) for i in range(chunks)]
+    inflow = inflow.transpose(1, 0, 2)
+    adjoint = adjoint[:, 0].transpose(1, 0, 2)
+    cells = jnp.stack([jnp.tile(source_cell[i : i + m], 2)[None] for i in starts])
+    waves = jnp.stack([source_wave[i : i + m].T.reshape(1, 2 * m) for i in starts])
+    factor, inflow, adjoint, cells, waves = gather_factor(packed, where, (inflow, adjoint, cells, waves))
+
+    steps = chunks + stages - 1
     vmem = pl.BlockSpec(memory_space=pltpu.VMEM)
     smem = pl.BlockSpec(memory_space=pltpu.SMEM)
     stage = lambda t: pl.pallas_call(
-        functools.partial(stage_kernel, t, CHUNKS, stages),
+        functools.partial(stage_kernel, t, chunks, stages),
         out_shape=(
             pltpu.VMEM((2, m, width), F32),
             pltpu.VMEM(factor.shape, BF16),
-            pltpu.VMEM((CHUNKS, 2, m, 128), BF16),
+            pltpu.VMEM((2,) + receiver_cell.shape, BF16),
         )
         + ((pltpu.VMEM((2, m, width + 128), BF16),) if t < steps - 1 else ()),
         in_specs=[smem] + [vmem] * 7,
@@ -219,7 +226,7 @@
         name="stage",
     )
     post = lambda t: pl.pallas_call(
-        functools.partial(post_kernel, t, CHUNKS),
+        functools.partial(post_kernel, t, chunks),
         out_shape=(
             jax.ShapeDtypeStruct((sources, 2, width), F32),
             pltpu.VMEM((8, width), F32),
@@ -232,14 +239,15 @@
         cost_estimate=pl.CostEstimate(flops=8 * m * width, bytes_accessed=24 * m * width, transcendentals=0),
         name="post",
     )
-    picked = jnp.zeros((CHUNKS, 2, m, receivers.shape[2]), BF16)
+    picked = jnp.zeros((2,) + receiver_cell.shape, BF16)
     done = ()
     x = jnp.zeros((2, m, width + 128), BF16)
     for t in range(steps):
+        at = min(t, chunks - 1)
         field, factor, picked, *y = stage(t)(
-            where, x, inflow[min(t, CHUNKS - 1)], cells, waves, receivers, factor, picked
+            where, x, inflow[:, starts[at] : starts[at] + m], cells, waves, receiver_cell, factor, picked
         )
-        pairs = [(i, i + 1) for i in range(stages - 1) if 0 <= t - i < CHUNKS]
+        pairs = [(i, i + 1) for i in range(stages - 1) if 0 <= t - i < chunks]
         if pairs:
             x = lax.ppermute(y[0], "fac", pairs)
         done = post(t)(where, field, adjoint, *done)
@@ -257,7 +265,7 @@
     picked = functools.reduce(jnp.add, first, picked)
     for pairs in rounds[1:]:
         picked = functools.reduce(jnp.add, [lax.ppermute(picked, "fac", p) for p in pairs], picked)
-    residual = (picked.astype(F32) - observed).transpose(0, 2, 1, 3).reshape(sources, 2, -1)
+    residual = picked.transpose(1, 0, 2).astype(F32) - observed
     return wavefield[:, None], residual, gradient
 
 

time: 192 us -> 187 us (0.974)
  the two profiles are of different devices: /device:TPU:6 before, /device:TPU:225 now
where the time goes in v5:
time: 187 us; the launch traced here: 186 us
  waiting for transfers between devices  76.1 us (41%)
  starting transfers between devices  42.1 us (23%)
  blocking collectives  38.6 us (21%)
  Pallas kernels  21.2 us (11%)
  local copies, waits for them, and re-layouts  5.09 us (3%)
    ppermute x9, waiting for transfers between devices, per_device(): x = lax.ppermute(y[0], 'fac', pairs)  52.7 us
    all_to_all x1, blocking collectives, per_device(): terms = lax.all_to_all(terms, SRC, 0, 0, tiled=True)  38.6 us
    ppermute x3, starting transfers between devices, swap(): return lax.ppermute(array, axis, [(0, 1), (1, 0)])  16.4 us
    all_to_all x2, waiting for transfers between devices, plane_gather(): return lax.all_to_all(spread, ('y', 'x'), 0, 0, tiled=True)  15.1 us
    all_to_all x2, starting transfers between devices, plane_gather(): return lax.all_to_all(spread, ('y', 'x'), 0, 0, tiled=True)  11.8 us
    pallas_call x10, Pallas kernels, per_device(): stage(t)  10.4 us
    ppermute x3, waiting for transfers between devices, swap(): return lax.ppermute(array, axis, [(0, 1), (1, 0)])  8.29 us
    pallas_call x10, Pallas kernels, per_device(): done = post(t)(where, field, adjoint, *done)  8.16 us
  transfers between devices with their start and end apart: 19, of which 7 were waited for; matrix products, arithmetic and copies ran while one was open for 1% of the time, Pallas kernels for 4%

profile of v5, /device:TPU:225, one launch (start us, length us, event | category | flops | bytes accessed | tf_op | source)
XLA Modules:
  0.0 186.0 jit_solution(3545368412650548114)
XLA Ops:
  0.7 1.0 broadcast_select_fusion
  1.8 1.1 broadcast_in_dim.26
  2.9 6.8 %all-to-all-start.1 = ((bf16[16,2,16,1152]{3,2,1,0:T(8,128)(2,1)}), bf16[16,2,16,1152]{3,2,1,0:T(8,128)(2,1)S(1)}, u32[]{:S(2)}, u32[]{:S(2)}) async-start(bf16[16,2,16,1152]{3,2,1,0:T(8,128)(2,1)} %broadcast_in_dim.26), calls=%async_computation.1 | async-start | bytes 2359296 | tf_op jit(solution)/shard_map/all_to_all | solution.py:153
  9.6 7.9 %collective-permute-start = (bf16[2,16,1152]{2,0,1:T(2,128)(2,1)S(1)}, bf16[2,16,1152]{2,0,1:T(2,128)(2,1)S(1)}, u32[]{:S(2)}, u32[]{:S(2)}) collective-permute-start(bf16[2,16,1152]{2,0,1:T(2,128)(2,1)S(1)} %broadcast_select_fusion), channel_id=1, source_target_pairs={{0,256},{256,0},{1,257},{257,1},{2,258},{258,2},{3,259},{259,3},{4... | collective-permute-start | bytes 221192 | tf_op jit(solution)/shard_map/ppermute | solution.py:147
  17.6 5.9 %collective-permute-done = bf16[2,16,1152]{2,0,1:T(2,128)(2,1)S(1)} collective-permute-done((bf16[2,16,1152]{2,0,1:T(2,128)(2,1)S(1)}, bf16[2,16,1152]{2,0,1:T(2,128)(2,1)S(1)}, u32[]{:S(2)}, u32[]{:S(2)}) %collective-permute-start) | collective-permute-done | bytes 73760 | tf_op jit(solution)/shard_map/ppermute | solution.py:147
  23.5 3.6 %all-to-all-done.1.own_ref = bf16[16,2,16,1152]{3,2,1,0:T(8,128)(2,1)S(1)} async-done(((bf16[16,2,16,1152]{3,2,1,0:T(8,128)(2,1)}), bf16[16,2,16,1152]{3,2,1,0:T(8,128)(2,1)S(1)}, u32[]{:S(2)}, u32[]{:S(2)}) %all-to-all-start.1) | async-done | bytes 1179680 | tf_op jit(solution)/shard_map/all_to_all | solution.py:153
  27.0 1.1 broadcast_in_dim.25
  28.1 5.0 %all-to-all-start = ((bf16[16,2,16,1152]{3,2,1,0:T(8,128)(2,1)}), bf16[16,2,16,1152]{3,2,1,0:T(8,128)(2,1)S(1)}, u32[]{:S(2)}, u32[]{:S(2)}) async-start(bf16[16,2,16,1152]{3,2,1,0:T(8,128)(2,1)} %broadcast_in_dim.25), calls=%async_computation | async-start | bytes 2359296 | tf_op jit(solution)/shard_map/all_to_all | solution.py:153
  33.2 0.1 fusion.1
  33.2 0.1 stack_broadcast_in_dim_tile.9
  33.3 0.1 stack_broadcast_in_dim_tile.11
  33.4 0.1 stack_broadcast_in_dim_tile.10
  33.6 0.1 stack_reshape.9
  33.6 0.1 stack_reshape.11
  33.7 0.1 stack_reshape.10
  33.8 0.1 copy.75
  33.9 1.2 copy.74
  35.1 3.4 %collective-permute-start.1 = (bf16[16,2,16,1152]{3,2,1,0:T(8,128)(2,1)S(1)}, bf16[16,2,16,1152]{3,2,1,0:T(8,128)(2,1)}, u32[]{:S(2)}, u32[]{:S(2)}) collective-permute-start(bf16[16,2,16,1152]{3,2,1,0:T(8,128)(2,1)S(1)} %all-to-all-done.1.own_ref), channel_id=1, source_target_pairs={{0,8},{8,0},{1,9},{9,1},{2,10},{10,2},{3,11},{11,3},{4,12},{12,4},... | collective-permute-start | bytes 3538952 | tf_op jit(solution)/shard_map/ppermute | solution.py:147
  38.5 11.5 %all-to-all-done.far_ref = bf16[16,2,16,1152]{3,2,1,0:T(8,128)(2,1)S(1)} async-done(((bf16[16,2,16,1152]{3,2,1,0:T(8,128)(2,1)}), bf16[16,2,16,1152]{3,2,1,0:T(8,128)(2,1)S(1)}, u32[]{:S(2)}, u32[]{:S(2)}) %all-to-all-start) | async-done | bytes 1179680 | tf_op jit(solution)/shard_map/all_to_all | solution.py:153
  50.0 5.1 %collective-permute-start.2 = (bf16[16,2,16,1152]{3,2,1,0:T(8,128)(2,1)S(1)}, bf16[16,2,16,1152]{3,2,1,0:T(8,128)(2,1)}, u32[]{:S(2)}, u32[]{:S(2)}) collective-permute-start(bf16[16,2,16,1152]{3,2,1,0:T(8,128)(2,1)S(1)} %all-to-all-done.far_ref), channel_id=1, source_target_pairs={{0,8},{8,0},{1,9},{9,1},{2,10},{10,2},{3,11},{11,3},{4,12},{12,4},... | collective-permute-start | bytes 3538952 | tf_op jit(solution)/shard_map/ppermute | solution.py:147
  55.1 0.1 pad_add_fusion.1.sc_ref
  55.3 2.4 %collective-permute-done.2.far_other_ref = bf16[16,2,16,1152]{3,2,1,0:T(8,128)(2,1)} collective-permute-done((bf16[16,2,16,1152]{3,2,1,0:T(8,128)(2,1)S(1)}, bf16[16,2,16,1152]{3,2,1,0:T(8,128)(2,1)}, u32[]{:S(2)}, u32[]{:S(2)}) %collective-permute-start.2) | collective-permute-done | bytes 1179680 | tf_op jit(solution)/shard_map/ppermute | solution.py:147
  57.7 2.6 %place.1.w_ref = bf16[2,2,16,2,16,1152]{5,4,3,2,1,0:T(8,128)(2,1)S(1)} custom-call(s32[3]{0:T(128)S(1)} %pad_add_fusion.1.sc_ref, bf16[16,2,16,1152]{3,2,1,0:T(8,128)(2,1)S(1)} %all-to-all-done.1.own_ref, bf16[16,2,16,1152]{3,2,1,0:T(8,128)(2,1)} %collective-permute-done.1.own_other_ref, bf16[16,2,16,1152]{3,2,1,0:T(8,128)(2,1)S(1)} %all-to-all-done.far_ref, ...), custom_call_target="tpu_custom_call" | custom-call | tf_op jit(solution)/shard_map/place/pallas_call | solution.py:164
  60.4 0.6 stage.10
  60.9 0.7 collective-permute-start.3
  61.6 0.6 post.10
  62.2 0.6 stage.11
  62.7 0.7 collective-permute-start.4
  63.4 0.6 post.11
  64.0 0.6 stage.12
  64.6 0.7 collective-permute-start.5
  65.2 0.6 post.12
  65.8 0.6 stage.13
  66.4 0.7 collective-permute-start.6
  67.1 0.6 post.13
  67.7 0.6 stage.14
  68.2 0.7 collective-permute-start.7
  68.9 0.6 post.14
  69.5 0.6 stage.15
  70.0 0.9 collective-permute-start.8
  70.9 0.6 post.15
  71.5 0.6 stage.16
  72.0 1.3 collective-permute-start.9
  73.3 0.6 post.16
  73.9 43.2 %collective-permute-done.9.x_ref = bf16[2,48,1152]{2,1,0:T(8,128)(2,1)S(1)} collective-permute-done((bf16[2,48,1152]{2,1,0:T(8,128)(2,1)S(1)}, bf16[2,48,1152]{2,1,0:T(8,128)(2,1)S(1)}, u32[]{:S(2)}, u32[]{:S(2)}) %collective-permute-start.9) | collective-permute-done | bytes 221216 | tf_op jit(solution)/shard_map/ppermute | solution.py:252
  117.1 2.2 %stage.17 = (f32[2,48,1024]{2,1,0:T(8,128)S(1)}, bf16[2,2,16,2,16,1152]{5,4,3,2,1,0:T(8,128)(2,1)S(1)}, bf16[2,128,128]{2,1,0:T(8,128)(2,1)S(1)}, bf16[2,48,1152]{2,1,0:T(8,128)(2,1)S(1)}) custom-call(s32[3]{0:T(128)S(1)} %pad_add_fusion.1.sc_ref, ...), custom_call_target="tpu_custom_call", output_to_operand_aliasing={{1}: (6, {}), {2}: (7, {})} | custom-call | flops 503316480 | bytes 4718592 | tf_op jit(solution)/shard_map/stage/pallas_call | solution.py:247
  119.3 1.3 collective-permute-start.10
  120.6 1.4 post.17
  122.0 5.2 %collective-permute-done.10.x_ref = bf16[2,48,1152]{2,1,0:T(8,128)(2,1)S(1)} collective-permute-done((bf16[2,48,1152]{2,1,0:T(8,128)(2,1)S(1)}, bf16[2,48,1152]{2,1,0:T(8,128)(2,1)S(1)}, u32[]{:S(2)}, u32[]{:S(2)}) %collective-permute-start.10) | collective-permute-done | bytes 221216 | tf_op jit(solution)/shard_map/ppermute | solution.py:252
  127.2 2.2 %stage.18 = (f32[2,48,1024]{2,1,0:T(8,128)S(1)}, bf16[2,2,16,2,16,1152]{5,4,3,2,1,0:T(8,128)(2,1)S(1)}, bf16[2,128,128]{2,1,0:T(8,128)(2,1)S(1)}, bf16[2,48,1152]{2,1,0:T(8,128)(2,1)S(1)}) custom-call(s32[3]{0:T(128)S(1)} %pad_add_fusion.1.sc_ref, ...), custom_call_target="tpu_custom_call", output_to_operand_aliasing={{1}: (6, {}), {2}: (7, {})} | custom-call | flops 503316480 | bytes 4718592 | tf_op jit(solution)/shard_map/stage/pallas_call | solution.py:247
  129.4 1.3 collective-permute-start.11
  130.7 1.4 post.18
  132.1 4.3 %collective-permute-done.11.x_ref = bf16[2,48,1152]{2,1,0:T(8,128)(2,1)S(1)} collective-permute-done((bf16[2,48,1152]{2,1,0:T(8,128)(2,1)S(1)}, bf16[2,48,1152]{2,1,0:T(8,128)(2,1)S(1)}, u32[]{:S(2)}, u32[]{:S(2)}) %collective-permute-start.11) | collective-permute-done | bytes 221216 | tf_op jit(solution)/shard_map/ppermute | solution.py:252
  136.4 2.2 %stage.19 = (f32[2,48,1024]{2,1,0:T(8,128)S(1)}, bf16[2,2,16,2,16,1152]{5,4,3,2,1,0:T(8,128)(2,1)S(1)}, bf16[2,128,128]{2,1,0:T(8,128)(2,1)S(1)}) custom-call(s32[3]{0:T(128)S(1)} %pad_add_fusion.1.sc_ref, bf16[2,48,1152]{2,1,0:T(8,128)(2,1)S(1)} %collective-permute-done.11.x_ref, ...), custom_call_target="tpu_custom_call", output_to_operand_aliasing={{1}: (6, {}), {2}: (7, {})} | custom-call | flops 503316480 | bytes 4718592 | tf_op jit(solution)/shard_map/stage/pallas_call | solution.py:247
  138.6 1.3 collective-permute-start.15
  139.9 1.3 collective-permute-start.14
  141.2 1.3 collective-permute-start.13
  142.5 1.3 collective-permute-start.12
  143.8 1.4 post.19
  145.3 0.1 mul.35
  145.4 38.6 %all_to_all.19 = f32[64,1,16]{2,1,0:T(1,128)S(1)} all-to-all(f32[64,1,16]{2,1,0:T(1,128)S(1)} %bitcast.44), channel_id=1, replica_groups=mesh['zh'=2,'y'=4,'x'=4,'c'=2,'fac'=8] {'zh','y','x','c'}, dimensions={0} | all-to-all | bytes 8192 | tf_op jit(solution)/shard_map/all_to_all | solution.py:262
  184.0 0.7 collective-permute-start.16
  184.7 0.5 reduce_sum.19
  185.3 0.8 copy.70
  (38 shorter events, 0.3 us)
Async XLA Ops:
  0.6 32.5 %copy-start.4 = (s32[128]{0:T(128)S(1)}, s32[128]{0:T(128)}, u32[]{:S(2)}) copy-start(s32[128]{0:T(128)} %param.10) | copy-start | bytes 1540
  0.6 32.9 %copy-start.3 = (f32[128,2]{0,1:T(2,128)S(1)}, f32[128,2]{0,1:T(2,128)}, u32[]{:S(2)}) copy-start(f32[128,2]{0,1:T(2,128)} %param.11) | copy-start | bytes 3076
  0.7 33.2 %copy-start.1 = (bf16[128,2,1024]{2,1,0:T(2,128)(2,1)S(1)}, bf16[128,2,1024]{2,1,0:T(2,128)(2,1)}, u32[]{:S(2)}) copy-start(bf16[128,2,1024]{2,1,0:T(2,128)(2,1)} %param.12) | copy-start | bytes 1572868
  2.9 24.2 %all-to-all-start.1 = ((bf16[16,2,16,1152]{3,2,1,0:T(8,128)(2,1)}), bf16[16,2,16,1152]{3,2,1,0:T(8,128)(2,1)S(1)}, u32[]{:S(2)}, u32[]{:S(2)}) async-start(bf16[16,2,16,1152]{3,2,1,0:T(8,128)(2,1)} %broadcast_in_dim.26), calls=%async_computation.1 | async-start | bytes 2359296 | tf_op jit(solution)/shard_map/all_to_all | solution.py:153
  9.6 13.8 %collective-permute-start = (bf16[2,16,1152]{2,0,1:T(2,128)(2,1)S(1)}, bf16[2,16,1152]{2,0,1:T(2,128)(2,1)S(1)}, u32[]{:S(2)}, u32[]{:S(2)}) collective-permute-start(bf16[2,16,1152]{2,0,1:T(2,128)(2,1)S(1)} %broadcast_select_fusion), channel_id=1, source_target_pairs={{0,256},{256,0},{1,257},{257,1},{2,258},{258,2},{3,259},{259,3},{4... | collective-permute-start | bytes 221192 | tf_op jit(solution)/shard_map/ppermute | solution.py:147
  28.1 21.9 %all-to-all-start = ((bf16[16,2,16,1152]{3,2,1,0:T(8,128)(2,1)}), bf16[16,2,16,1152]{3,2,1,0:T(8,128)(2,1)S(1)}, u32[]{:S(2)}, u32[]{:S(2)}) async-start(bf16[16,2,16,1152]{3,2,1,0:T(8,128)(2,1)} %broadcast_in_dim.25), calls=%async_computation | async-start | bytes 2359296 | tf_op jit(solution)/shard_map/all_to_all | solution.py:153
  35.1 20.2 %collective-permute-start.1 = (bf16[16,2,16,1152]{3,2,1,0:T(8,128)(2,1)S(1)}, bf16[16,2,16,1152]{3,2,1,0:T(8,128)(2,1)}, u32[]{:S(2)}, u32[]{:S(2)}) collective-permute-start(bf16[16,2,16,1152]{3,2,1,0:T(8,128)(2,1)S(1)} %all-to-all-done.1.own_ref), channel_id=1, source_target_pairs={{0,8},{8,0},{1,9},{9,1},{2,10},{10,2},{3,11},{11,3},{4,12},{12,4},... | collective-permute-start | bytes 3538952 | tf_op jit(solution)/shard_map/ppermute | solution.py:147
  50.0 7.7 %collective-permute-start.2 = (bf16[16,2,16,1152]{3,2,1,0:T(8,128)(2,1)S(1)}, bf16[16,2,16,1152]{3,2,1,0:T(8,128)(2,1)}, u32[]{:S(2)}, u32[]{:S(2)}) collective-permute-start(bf16[16,2,16,1152]{3,2,1,0:T(8,128)(2,1)S(1)} %all-to-all-done.far_ref), channel_id=1, source_target_pairs={{0,8},{8,0},{1,9},{9,1},{2,10},{10,2},{3,11},{11,3},{4,12},{12,4},... | collective-permute-start | bytes 3538952 | tf_op jit(solution)/shard_map/ppermute | solution.py:147
  55.3 5.1 %copy-start = (s32[128,128]{1,0:T(8,128)S(1)}, s32[128,128]{1,0:T(8,128)}, u32[]{:S(2)}) copy-start(s32[128,128]{1,0:T(8,128)} %receivers_ref.19) | copy-start | bytes 196612
  60.9 1.3 collective-permute-start.3
  62.7 1.3 collective-permute-start.4
  64.6 1.3 collective-permute-start.5
  66.4 1.3 collective-permute-start.6
  68.2 1.3 collective-permute-start.7
  70.0 1.4 collective-permute-start.8
  72.0 45.1 %collective-permute-start.9 = (bf16[2,48,1152]{2,1,0:T(8,128)(2,1)S(1)}, bf16[2,48,1152]{2,1,0:T(8,128)(2,1)S(1)}, u32[]{:S(2)}, u32[]{:S(2)}) collective-permute-start(bf16[2,48,1152]{2,1,0:T(8,128)(2,1)S(1)} %get-tuple-element.157), channel_id=1, source_target_pairs={{4,5},{5,6},{6,7},{12,13},{13,14},{14,15},{20,21},{21,22},{22,23},... | collective-permute-start | bytes 663560 | tf_op jit(solution)/shard_map/ppermute | solution.py:252
  119.3 7.9 %collective-permute-start.10 = (bf16[2,48,1152]{2,1,0:T(8,128)(2,1)S(1)}, bf16[2,48,1152]{2,1,0:T(8,128)(2,1)S(1)}, u32[]{:S(2)}, u32[]{:S(2)}) collective-permute-start(bf16[2,48,1152]{2,1,0:T(8,128)(2,1)S(1)} %get-tuple-element.166), channel_id=1, source_target_pairs={{5,6},{6,7},{13,14},{14,15},{21,22},{22,23},{29,30},{30,31},{37,38... | collective-permute-start | bytes 663560 | tf_op jit(solution)/shard_map/ppermute | solution.py:252
  129.4 7.0 %collective-permute-start.11 = (bf16[2,48,1152]{2,1,0:T(8,128)(2,1)S(1)}, bf16[2,48,1152]{2,1,0:T(8,128)(2,1)S(1)}, u32[]{:S(2)}, u32[]{:S(2)}) collective-permute-start(bf16[2,48,1152]{2,1,0:T(8,128)(2,1)S(1)} %get-tuple-element.175), channel_id=1, source_target_pairs={{6,7},{14,15},{22,23},{30,31},{38,39},{46,47},{54,55},{62,63},{70,... | collective-permute-start | bytes 663560 | tf_op jit(solution)/shard_map/ppermute | solution.py:252
  130.7 54.5 %copy-start.2 = (f32[128,2,128]{2,1,0:T(2,128)S(1)}, f32[128,2,128]{2,1,0:T(2,128)}, u32[]{:S(2)}) copy-start(f32[128,2,128]{2,1,0:T(2,128)} %param.14) | copy-start | bytes 393220
  138.6 45.3 %collective-permute-start.15 = (bf16[2,128,128]{2,1,0:T(8,128)(2,1)S(1)}, bf16[2,128,128]{2,1,0:T(8,128)(2,1)S(1)}, u32[]{:S(2)}, u32[]{:S(2)}) collective-permute-start(bf16[2,128,128]{2,1,0:T(8,128)(2,1)S(1)} %get-tuple-element.190), channel_id=1, source_target_pairs={{7,6},{15,14},{23,22},{31,30},{39,38},{47,46},{55,54},{63,62},{71,... | collective-permute-start | bytes 196616 | tf_op jit(solution)/shard_map/ppermute | solution.py:258
  139.9 44.0 %collective-permute-start.14 = (bf16[2,128,128]{2,1,0:T(8,128)(2,1)S(1)}, bf16[2,128,128]{2,1,0:T(8,128)(2,1)S(1)}, u32[]{:S(2)}, u32[]{:S(2)}) collective-permute-start(bf16[2,128,128]{2,1,0:T(8,128)(2,1)S(1)} %get-tuple-element.190), channel_id=1, source_target_pairs={{7,5},{15,13},{23,21},{31,29},{39,37},{47,45},{55,53},{63,61},{71,... | collective-permute-start | bytes 196616 | tf_op jit(solution)/shard_map/ppermute | solution.py:258
  141.2 42.7 %collective-permute-start.13 = (bf16[2,128,128]{2,1,0:T(8,128)(2,1)S(1)}, bf16[2,128,128]{2,1,0:T(8,128)(2,1)S(1)}, u32[]{:S(2)}, u32[]{:S(2)}) collective-permute-start(bf16[2,128,128]{2,1,0:T(8,128)(2,1)S(1)} %get-tuple-element.190), channel_id=1, source_target_pairs={{7,4},{15,12},{23,20},{31,28},{39,36},{47,44},{55,52},{63,60},{71,... | collective-permute-start | bytes 196616 | tf_op jit(solution)/shard_map/ppermute | solution.py:258
  142.5 41.4 %collective-permute-start.12 = (bf16[2,128,128]{2,1,0:T(8,128)(2,1)S(1)}, bf16[2,128,128]{2,1,0:T(8,128)(2,1)S(1)}, u32[]{:S(2)}, u32[]{:S(2)}) collective-permute-start(bf16[2,128,128]{2,1,0:T(8,128)(2,1)S(1)} %get-tuple-element.190), channel_id=1, source_target_pairs={{7,1},{15,9},{23,17},{31,25},{39,33},{47,41},{55,49},{63,57},{71,6... | collective-permute-start | bytes 196616 | tf_op jit(solution)/shard_map/ppermute | solution.py:258
  184.0 1.2 collective-permute-start.16

commit v6 on v5

--- a/solution.py
+++ b/solution.py
@@ -9,7 +9,7 @@
 from jax.sharding import Mesh, PartitionSpec as P
 
 SRC = ("zh", "y", "x", "c")
-CHUNK = 48
+CHUNK = 64
 GROUP = 128
 LIMIT = 16 << 20
 SPLIT = 4
@@ -176,7 +176,7 @@
     last = stages - 1
     if stages != 8:
         return [[[(last, i)] for i in range(last)]]
-    return [[[(7, 1)], [(7, 4)], [(7, 5)], [(7, 6)]], [[(1, 0), (4, 3), (5, 2)]]]
+    return [[[(7, 5)], [(7, 2)]], [[(5, 4), (2, 0)]], [[(5, 6), (2, 1), (0, 3)]]]
 
 
 def per_device(lower, coupling, source_cell, source_wave, inflow, receiver_cell, observed, adjoint):

time: 187 us -> 184 us (0.984)
  the two profiles are of different devices: /device:TPU:225 before, /device:TPU:192 now
where the time goes in v6:
time: 184 us
  waiting for transfers between devices  88.8 us (48%)
  starting transfers between devices  37.9 us (21%)
  blocking collectives  31 us (17%)
  Pallas kernels  18 us (10%)
  local copies, waits for them, and re-layouts  4.91 us (3%)
    ppermute x8, waiting for transfers between devices, per_device(): x = lax.ppermute(y[0], 'fac', pairs)  56 us
    all_to_all x1, blocking collectives, per_device(): terms = lax.all_to_all(terms, SRC, 0, 0, tiled=True)  31 us
    all_to_all x2, waiting for transfers between devices, plane_gather(): return lax.all_to_all(spread, ('y', 'x'), 0, 0, tiled=True)  16.5 us
    all_to_all x2, starting transfers between devices, plane_gather(): return lax.all_to_all(spread, ('y', 'x'), 0, 0, tiled=True)  13 us
    ppermute x3, starting transfers between devices, swap(): return lax.ppermute(array, axis, [(0, 1), (1, 0)])  12.9 us
    ppermute x3, waiting for transfers between devices, swap(): return lax.ppermute(array, axis, [(0, 1), (1, 0)])  11.9 us
    ppermute x8, starting transfers between devices, per_device(): x = lax.ppermute(y[0], 'fac', pairs)  8.64 us
    pallas_call x9, Pallas kernels, per_device(): stage(t)  8.53 us
  transfers between devices with their start and end apart: 17, of which 8 were waited for; matrix products, arithmetic and copies ran while one was open for 1% of the time, Pallas kernels for 4%

profile of v6, /device:TPU:192, one launch (start us, length us, event | category | flops | bytes accessed | tf_op | source)
XLA Modules:
  0.0 183.6 jit_solution(14420278757544839458)
XLA Ops:
  0.7 1.0 broadcast_select_fusion
  1.8 1.1 broadcast_in_dim.26
  2.9 7.0 %all-to-all-start.1 = ((bf16[16,2,16,1152]{3,2,1,0:T(8,128)(2,1)}), bf16[16,2,16,1152]{3,2,1,0:T(8,128)(2,1)S(1)}, u32[]{:S(2)}, u32[]{:S(2)}) async-start(bf16[16,2,16,1152]{3,2,1,0:T(8,128)(2,1)} %broadcast_in_dim.26), calls=%async_computation.1 | async-start | bytes 2359296 | tf_op jit(solution)/shard_map/all_to_all | solution.py:153
  9.9 9.1 %collective-permute-start = (bf16[2,16,1152]{2,0,1:T(2,128)(2,1)S(1)}, bf16[2,16,1152]{2,0,1:T(2,128)(2,1)S(1)}, u32[]{:S(2)}, u32[]{:S(2)}) collective-permute-start(bf16[2,16,1152]{2,0,1:T(2,128)(2,1)S(1)} %broadcast_select_fusion), channel_id=1, source_target_pairs={{0,256},{256,0},{1,257},{257,1},{2,258},{258,2},{3,259},{259,3},{4... | collective-permute-start | bytes 221192 | tf_op jit(solution)/shard_map/ppermute | solution.py:147
  19.1 9.1 %collective-permute-done = bf16[2,16,1152]{2,0,1:T(2,128)(2,1)S(1)} collective-permute-done((bf16[2,16,1152]{2,0,1:T(2,128)(2,1)S(1)}, bf16[2,16,1152]{2,0,1:T(2,128)(2,1)S(1)}, u32[]{:S(2)}, u32[]{:S(2)}) %collective-permute-start) | collective-permute-done | bytes 73760 | tf_op jit(solution)/shard_map/ppermute | solution.py:147
  28.2 0.9 all-to-all-done.1.own_ref
  29.2 1.1 broadcast_in_dim.25
  30.3 6.0 %all-to-all-start = ((bf16[16,2,16,1152]{3,2,1,0:T(8,128)(2,1)}), bf16[16,2,16,1152]{3,2,1,0:T(8,128)(2,1)S(1)}, u32[]{:S(2)}, u32[]{:S(2)}) async-start(bf16[16,2,16,1152]{3,2,1,0:T(8,128)(2,1)} %broadcast_in_dim.25), calls=%async_computation | async-start | bytes 2359296 | tf_op jit(solution)/shard_map/all_to_all | solution.py:153
  36.3 0.1 fusion.1
  36.3 0.1 stack_broadcast_in_dim_tile.6
  36.4 0.1 stack_broadcast_in_dim_tile.7
  36.5 0.1 slice_bitcast_fusion.1
  36.6 0.1 stack_reshape.6
  36.7 0.1 stack_reshape.7
  36.8 0.1 copy.71
  36.9 1.2 copy.70
  38.1 1.9 %collective-permute-start.1 = (bf16[16,2,16,1152]{3,2,1,0:T(8,128)(2,1)S(1)}, bf16[16,2,16,1152]{3,2,1,0:T(8,128)(2,1)}, u32[]{:S(2)}, u32[]{:S(2)}) collective-permute-start(bf16[16,2,16,1152]{3,2,1,0:T(8,128)(2,1)S(1)} %all-to-all-done.1.own_ref), channel_id=1, source_target_pairs={{0,8},{8,0},{1,9},{9,1},{2,10},{10,2},{3,11},{11,3},{4,12},{12,4},... | collective-permute-start | bytes 3538952 | tf_op jit(solution)/shard_map/ppermute | solution.py:147
  40.0 15.6 %all-to-all-done.far_ref = bf16[16,2,16,1152]{3,2,1,0:T(8,128)(2,1)S(1)} async-done(((bf16[16,2,16,1152]{3,2,1,0:T(8,128)(2,1)}), bf16[16,2,16,1152]{3,2,1,0:T(8,128)(2,1)S(1)}, u32[]{:S(2)}, u32[]{:S(2)}) %all-to-all-start) | async-done | bytes 1179680 | tf_op jit(solution)/shard_map/all_to_all | solution.py:153
  55.6 1.9 %collective-permute-start.2 = (bf16[16,2,16,1152]{3,2,1,0:T(8,128)(2,1)S(1)}, bf16[16,2,16,1152]{3,2,1,0:T(8,128)(2,1)}, u32[]{:S(2)}, u32[]{:S(2)}) collective-permute-start(bf16[16,2,16,1152]{3,2,1,0:T(8,128)(2,1)S(1)} %all-to-all-done.far_ref), channel_id=1, source_target_pairs={{0,8},{8,0},{1,9},{9,1},{2,10},{10,2},{3,11},{11,3},{4,12},{12,4},... | collective-permute-start | bytes 3538952 | tf_op jit(solution)/shard_map/ppermute | solution.py:147
  57.5 0.1 pad_add_fusion.1.sc_ref
  57.6 0.0 copy-start
  57.6 2.8 %collective-permute-done.2.far_other_ref = bf16[16,2,16,1152]{3,2,1,0:T(8,128)(2,1)} collective-permute-done((bf16[16,2,16,1152]{3,2,1,0:T(8,128)(2,1)S(1)}, bf16[16,2,16,1152]{3,2,1,0:T(8,128)(2,1)}, u32[]{:S(2)}, u32[]{:S(2)}) %collective-permute-start.2) | collective-permute-done | bytes 1179680 | tf_op jit(solution)/shard_map/ppermute | solution.py:147
  60.4 2.6 %place.1.w_ref = bf16[2,2,16,2,16,1152]{5,4,3,2,1,0:T(8,128)(2,1)S(1)} custom-call(s32[3]{0:T(128)S(1)} %pad_add_fusion.1.sc_ref, bf16[16,2,16,1152]{3,2,1,0:T(8,128)(2,1)S(1)} %all-to-all-done.1.own_ref, bf16[16,2,16,1152]{3,2,1,0:T(8,128)(2,1)} %collective-permute-done.1.own_other_ref, bf16[16,2,16,1152]{3,2,1,0:T(8,128)(2,1)S(1)} %all-to-all-done.far_ref, ...), custom_call_target="tpu_custom_call" | custom-call | tf_op jit(solution)/shard_map/place/pallas_call | solution.py:164
  63.1 0.6 stage.9
  63.6 0.7 collective-permute-start.3
  64.3 0.6 post.9
  64.9 0.0 collective-permute-done.3.x_ref
  64.9 0.6 stage.10
  65.5 0.7 collective-permute-start.4
  66.1 0.6 post.10
  66.7 0.6 stage.11
  67.3 0.7 collective-permute-start.5
  68.0 0.6 post.11
  68.5 0.0 collective-permute-done.5.x_ref
  68.6 0.6 stage.12
  69.1 0.7 collective-permute-start.6
  69.8 0.6 post.12
  70.4 0.6 stage.13
  70.9 0.7 collective-permute-start.7
  71.6 0.6 post.13
  72.2 0.7 stage.14
  73.0 1.3 collective-permute-start.8
  74.3 0.6 post.14
  74.8 47.8 %collective-permute-done.8.x_ref = bf16[2,64,1152]{2,1,0:T(8,128)(2,1)S(1)} collective-permute-done((bf16[2,64,1152]{2,1,0:T(8,128)(2,1)S(1)}, bf16[2,64,1152]{2,1,0:T(8,128)(2,1)S(1)}, u32[]{:S(2)}, u32[]{:S(2)}) %collective-permute-start.8) | collective-permute-done | bytes 294944 | tf_op jit(solution)/shard_map/ppermute | solution.py:252
  122.7 2.2 %stage.15 = (f32[2,64,1024]{2,1,0:T(8,128)S(1)}, bf16[2,2,16,2,16,1152]{5,4,3,2,1,0:T(8,128)(2,1)S(1)}, bf16[2,128,128]{2,1,0:T(8,128)(2,1)S(1)}, bf16[2,64,1152]{2,1,0:T(8,128)(2,1)S(1)}) custom-call(s32[3]{0:T(128)S(1)} %pad_add_fusion.1.sc_ref, ...), custom_call_target="tpu_custom_call", output_to_operand_aliasing={{1}: (6, {}), {2}: (7, {})} | custom-call | flops 671088640 | bytes 4718592 | tf_op jit(solution)/shard_map/stage/pallas_call | solution.py:247
  124.9 1.9 %collective-permute-start.9 = (bf16[2,64,1152]{2,1,0:T(8,128)(2,1)S(1)}, bf16[2,64,1152]{2,1,0:T(8,128)(2,1)S(1)}, u32[]{:S(2)}, u32[]{:S(2)}) collective-permute-start(bf16[2,64,1152]{2,1,0:T(8,128)(2,1)S(1)} %get-tuple-element.146), channel_id=1, source_target_pairs={{5,6},{6,7},{13,14},{14,15},{21,22},{22,23},{29,30},{30,31},{37,38... | collective-permute-start | bytes 884744 | tf_op jit(solution)/shard_map/ppermute | solution.py:252
  126.8 1.5 post.15
  128.3 5.5 %collective-permute-done.9.x_ref = bf16[2,64,1152]{2,1,0:T(8,128)(2,1)S(1)} collective-permute-done((bf16[2,64,1152]{2,1,0:T(8,128)(2,1)S(1)}, bf16[2,64,1152]{2,1,0:T(8,128)(2,1)S(1)}, u32[]{:S(2)}, u32[]{:S(2)}) %collective-permute-start.9) | collective-permute-done | bytes 294944 | tf_op jit(solution)/shard_map/ppermute | solution.py:252
  133.8 2.2 %stage.16 = (f32[2,64,1024]{2,1,0:T(8,128)S(1)}, bf16[2,2,16,2,16,1152]{5,4,3,2,1,0:T(8,128)(2,1)S(1)}, bf16[2,128,128]{2,1,0:T(8,128)(2,1)S(1)}, bf16[2,64,1152]{2,1,0:T(8,128)(2,1)S(1)}) custom-call(s32[3]{0:T(128)S(1)} %pad_add_fusion.1.sc_ref, ...), custom_call_target="tpu_custom_call", output_to_operand_aliasing={{1}: (6, {}), {2}: (7, {})} | custom-call | flops 671088640 | bytes 4718592 | tf_op jit(solution)/shard_map/stage/pallas_call | solution.py:247
  136.0 2.0 %collective-permute-start.10 = (bf16[2,64,1152]{2,1,0:T(8,128)(2,1)S(1)}, bf16[2,64,1152]{2,1,0:T(8,128)(2,1)S(1)}, u32[]{:S(2)}, u32[]{:S(2)}) collective-permute-start(bf16[2,64,1152]{2,1,0:T(8,128)(2,1)S(1)} %get-tuple-element.155), channel_id=1, source_target_pairs={{6,7},{14,15},{22,23},{30,31},{38,39},{46,47},{54,55},{62,63},{70,... | collective-permute-start | bytes 884744 | tf_op jit(solution)/shard_map/ppermute | solution.py:252
  138.1 0.0 copy-start.2
  138.1 1.5 post.16
  139.6 2.7 %collective-permute-done.10.x_ref = bf16[2,64,1152]{2,1,0:T(8,128)(2,1)S(1)} collective-permute-done((bf16[2,64,1152]{2,1,0:T(8,128)(2,1)S(1)}, bf16[2,64,1152]{2,1,0:T(8,128)(2,1)S(1)}, u32[]{:S(2)}, u32[]{:S(2)}) %collective-permute-start.10) | collective-permute-done | bytes 294944 | tf_op jit(solution)/shard_map/ppermute | solution.py:252
  142.3 0.6 stage.17
  142.8 0.7 collective-permute-start.12
  143.5 0.7 collective-permute-start.11
  144.2 0.6 post.17
  144.8 0.1 mul.35
  144.9 31.0 %all_to_all.19 = f32[64,1,16]{2,1,0:T(1,128)S(1)} all-to-all(f32[64,1,16]{2,1,0:T(1,128)S(1)} %bitcast.41), channel_id=1, replica_groups=mesh['zh'=2,'y'=4,'x'=4,'c'=2,'fac'=8] {'zh','y','x','c'}, dimensions={0} | all-to-all | bytes 8192 | tf_op jit(solution)/shard_map/all_to_all | solution.py:262
  175.9 0.7 collective-permute-start.13
  176.6 1.3 collective-permute-start.14
  177.9 0.5 reduce_sum.19
  178.5 4.3 %collective-permute-done.14 = bf16[2,128,128]{2,1,0:T(8,128)(2,1)S(1)} collective-permute-done((bf16[2,128,128]{2,1,0:T(8,128)(2,1)S(1)}, bf16[2,128,128]{2,1,0:T(8,128)(2,1)S(1)}, u32[]{:S(2)}, u32[]{:S(2)}) %collective-permute-start.14) | collective-permute-done | bytes 65568 | tf_op jit(solution)/shard_map/ppermute | solution.py:267
  182.8 0.8 copy.66
  (30 shorter events, 0.2 us)
Async XLA Ops:
  0.6 35.6 %copy-start.4 = (s32[128]{0:T(128)S(1)}, s32[128]{0:T(128)}, u32[]{:S(2)}) copy-start(s32[128]{0:T(128)} %param.10) | copy-start | bytes 1540
  0.6 35.9 %copy-start.3 = (f32[128,2]{0,1:T(2,128)S(1)}, f32[128,2]{0,1:T(2,128)}, u32[]{:S(2)}) copy-start(f32[128,2]{0,1:T(2,128)} %param.11) | copy-start | bytes 3076
  0.7 36.1 %copy-start.1 = (bf16[128,2,1024]{2,1,0:T(2,128)(2,1)S(1)}, bf16[128,2,1024]{2,1,0:T(2,128)(2,1)}, u32[]{:S(2)}) copy-start(bf16[128,2,1024]{2,1,0:T(2,128)(2,1)} %param.12) | copy-start | bytes 1572868
  2.9 26.3 %all-to-all-start.1 = ((bf16[16,2,16,1152]{3,2,1,0:T(8,128)(2,1)}), bf16[16,2,16,1152]{3,2,1,0:T(8,128)(2,1)S(1)}, u32[]{:S(2)}, u32[]{:S(2)}) async-start(bf16[16,2,16,1152]{3,2,1,0:T(8,128)(2,1)} %broadcast_in_dim.26), calls=%async_computation.1 | async-start | bytes 2359296 | tf_op jit(solution)/shard_map/all_to_all | solution.py:153
  9.9 18.3 %collective-permute-start = (bf16[2,16,1152]{2,0,1:T(2,128)(2,1)S(1)}, bf16[2,16,1152]{2,0,1:T(2,128)(2,1)S(1)}, u32[]{:S(2)}, u32[]{:S(2)}) collective-permute-start(bf16[2,16,1152]{2,0,1:T(2,128)(2,1)S(1)} %broadcast_select_fusion), channel_id=1, source_target_pairs={{0,256},{256,0},{1,257},{257,1},{2,258},{258,2},{3,259},{259,3},{4... | collective-permute-start | bytes 221192 | tf_op jit(solution)/shard_map/ppermute | solution.py:147
  30.3 25.3 %all-to-all-start = ((bf16[16,2,16,1152]{3,2,1,0:T(8,128)(2,1)}), bf16[16,2,16,1152]{3,2,1,0:T(8,128)(2,1)S(1)}, u32[]{:S(2)}, u32[]{:S(2)}) async-start(bf16[16,2,16,1152]{3,2,1,0:T(8,128)(2,1)} %broadcast_in_dim.25), calls=%async_computation | async-start | bytes 2359296 | tf_op jit(solution)/shard_map/all_to_all | solution.py:153
  38.1 19.6 %collective-permute-start.1 = (bf16[16,2,16,1152]{3,2,1,0:T(8,128)(2,1)S(1)}, bf16[16,2,16,1152]{3,2,1,0:T(8,128)(2,1)}, u32[]{:S(2)}, u32[]{:S(2)}) collective-permute-start(bf16[16,2,16,1152]{3,2,1,0:T(8,128)(2,1)S(1)} %all-to-all-done.1.own_ref), channel_id=1, source_target_pairs={{0,8},{8,0},{1,9},{9,1},{2,10},{10,2},{3,11},{11,3},{4,12},{12,4},... | collective-permute-start | bytes 3538952 | tf_op jit(solution)/shard_map/ppermute | solution.py:147
  55.6 4.9 %collective-permute-start.2 = (bf16[16,2,16,1152]{3,2,1,0:T(8,128)(2,1)S(1)}, bf16[16,2,16,1152]{3,2,1,0:T(8,128)(2,1)}, u32[]{:S(2)}, u32[]{:S(2)}) collective-permute-start(bf16[16,2,16,1152]{3,2,1,0:T(8,128)(2,1)S(1)} %all-to-all-done.far_ref), channel_id=1, source_target_pairs={{0,8},{8,0},{1,9},{9,1},{2,10},{10,2},{3,11},{11,3},{4,12},{12,4},... | collective-permute-start | bytes 3538952 | tf_op jit(solution)/shard_map/ppermute | solution.py:147
  57.6 5.5 %copy-start = (s32[128,128]{1,0:T(8,128)S(1)}, s32[128,128]{1,0:T(8,128)}, u32[]{:S(2)}) copy-start(s32[128,128]{1,0:T(8,128)} %receivers_ref.17) | copy-start | bytes 196612
  63.6 1.3 collective-permute-start.3
  65.5 1.3 collective-permute-start.4
  67.3 1.3 collective-permute-start.5
  69.1 1.3 collective-permute-start.6
  70.9 1.3 collective-permute-start.7
  73.0 49.7 %collective-permute-start.8 = (bf16[2,64,1152]{2,1,0:T(8,128)(2,1)S(1)}, bf16[2,64,1152]{2,1,0:T(8,128)(2,1)S(1)}, u32[]{:S(2)}, u32[]{:S(2)}) collective-permute-start(bf16[2,64,1152]{2,1,0:T(8,128)(2,1)S(1)} %get-tuple-element.137), channel_id=1, source_target_pairs={{4,5},{5,6},{12,13},{13,14},{20,21},{21,22},{28,29},{29,30},{36,37... | collective-permute-start | bytes 884744 | tf_op jit(solution)/shard_map/ppermute | solution.py:252
  124.9 8.9 %collective-permute-start.9 = (bf16[2,64,1152]{2,1,0:T(8,128)(2,1)S(1)}, bf16[2,64,1152]{2,1,0:T(8,128)(2,1)S(1)}, u32[]{:S(2)}, u32[]{:S(2)}) collective-permute-start(bf16[2,64,1152]{2,1,0:T(8,128)(2,1)S(1)} %get-tuple-element.146), channel_id=1, source_target_pairs={{5,6},{6,7},{13,14},{14,15},{21,22},{22,23},{29,30},{30,31},{37,38... | collective-permute-start | bytes 884744 | tf_op jit(solution)/shard_map/ppermute | solution.py:252
  136.0 6.2 %collective-permute-start.10 = (bf16[2,64,1152]{2,1,0:T(8,128)(2,1)S(1)}, bf16[2,64,1152]{2,1,0:T(8,128)(2,1)S(1)}, u32[]{:S(2)}, u32[]{:S(2)}) collective-permute-start(bf16[2,64,1152]{2,1,0:T(8,128)(2,1)S(1)} %get-tuple-element.155), channel_id=1, source_target_pairs={{6,7},{14,15},{22,23},{30,31},{38,39},{46,47},{54,55},{62,63},{70,... | collective-permute-start | bytes 884744 | tf_op jit(solution)/shard_map/ppermute | solution.py:252
  138.1 44.7 %copy-start.2 = (f32[128,2,128]{2,1,0:T(2,128)S(1)}, f32[128,2,128]{2,1,0:T(2,128)}, u32[]{:S(2)}) copy-start(f32[128,2,128]{2,1,0:T(2,128)} %param.14) | copy-start | bytes 393220
  142.8 33.1 %collective-permute-start.12 = (bf16[2,128,128]{2,1,0:T(8,128)(2,1)S(1)}, bf16[2,128,128]{2,1,0:T(8,128)(2,1)S(1)}, u32[]{:S(2)}, u32[]{:S(2)}) collective-permute-start(bf16[2,128,128]{2,1,0:T(8,128)(2,1)S(1)} %get-tuple-element.170), channel_id=1, source_target_pairs={{7,2},{15,10},{23,18},{31,26},{39,34},{47,42},{55,50},{63,58},{71,... | collective-permute-start | bytes 196616 | tf_op jit(solution)/shard_map/ppermute | solution.py:258
  143.5 32.4 %collective-permute-start.11 = (bf16[2,128,128]{2,1,0:T(8,128)(2,1)S(1)}, bf16[2,128,128]{2,1,0:T(8,128)(2,1)S(1)}, u32[]{:S(2)}, u32[]{:S(2)}) collective-permute-start(bf16[2,128,128]{2,1,0:T(8,128)(2,1)S(1)} %get-tuple-element.170), channel_id=1, source_target_pairs={{7,5},{15,13},{23,21},{31,29},{39,37},{47,45},{55,53},{63,61},{71,... | collective-permute-start | bytes 196616 | tf_op jit(solution)/shard_map/ppermute | solution.py:258
  175.9 0.7 collective-permute-start.13
  176.6 6.2 %collective-permute-start.14 = (bf16[2,128,128]{2,1,0:T(8,128)(2,1)S(1)}, bf16[2,128,128]{2,1,0:T(8,128)(2,1)S(1)}, u32[]{:S(2)}, u32[]{:S(2)}) collective-permute-start(bf16[2,128,128]{2,1,0:T(8,128)(2,1)S(1)} %add.35), channel_id=1, source_target_pairs={{5,6},{2,1},{0,3},{13,14},{10,9},{8,11},{21,22},{18,17},{16,19},{2... | collective-permute-start | bytes 196616 | tf_op jit(solution)/shard_map/ppermute | solution.py:267

commit v7 on v6

--- a/solution.py
+++ b/solution.py
@@ -97,28 +97,54 @@
             picked_ref[...] = jnp.zeros_like(picked_ref)
 
 
+def store_rows(field_ref, wave_out, rows_ref, sem, start):
+    for p in range(2):
+        rows_ref[:, p, :] = field_ref[p]
+    store = pltpu.make_async_copy(rows_ref, wave_out.at[pl.ds(start, rows_ref.shape[0])], sem)
+    store.start()
+    return store
+
+
+def add_gradient(field_ref, adjoint_ref, grad_out, chunk, start):
+    m, width = field_ref.shape[1], field_ref.shape[2]
+    prod = field_ref[...] * adjoint_ref[:, pl.ds(start, m), :].astype(F32)
+    if adjoint_ref.shape[1] % m:
+        fresh = lax.broadcasted_iota(jnp.int32, prod.shape, 1) >= chunk * m - start
+        prod = jnp.where(fresh, prod, 0.0)
+    grad_out[...] += jnp.sum(prod.reshape(2 * m // 8, 8, width), axis=0)
+
+
 def post_kernel(step, chunks, sc_ref, field_ref, adjoint_ref, *refs):
     wave_out, grad_out, rows_ref, sem = refs[-4:]
-    owner = sc_ref[0]
-    chunk = step - owner
-    m, width = field_ref.shape[1], field_ref.shape[2]
+    chunk = step - sc_ref[0]
 
     if step == 0:
         grad_out[...] = jnp.zeros_like(grad_out)
 
     @pl.when((chunk >= 0) & (chunk < chunks))
     def _():
-        start = first_row(chunk, m, wave_out.shape[0])
-        field = field_ref[...]
-        for p in range(2):
-            rows_ref[:, p, :] = field[p]
-        store = pltpu.make_async_copy(rows_ref, wave_out.at[pl.ds(start, m)], sem)
-        store.start()
-        prod = field * adjoint_ref[:, pl.ds(start, m), :].astype(F32)
-        fresh = lax.broadcasted_iota(jnp.int32, prod.shape, 1) >= chunk * m - start
-        prod = jnp.where(fresh, prod, 0.0)
-        grad_out[...] += jnp.sum(prod.reshape(2 * m // 8, 8, width), axis=0)
+        start = first_row(chunk, field_ref.shape[1], wave_out.shape[0])
+        store = store_rows(field_ref, wave_out, rows_ref, sem, start)
+        add_gradient(field_ref, adjoint_ref, grad_out, chunk, start)
         store.wait()
+
+
+def last_gradient_kernel(step, chunks, sc_ref, field_ref, adjoint_ref, _g, grad_out):
+    chunk = step - sc_ref[0]
+
+    @pl.when((chunk >= 0) & (chunk < chunks))
+    def _():
+        start = first_row(chunk, field_ref.shape[1], adjoint_ref.shape[1])
+        add_gradient(field_ref, adjoint_ref, grad_out, chunk, start)
+
+
+def last_store_kernel(step, chunks, sc_ref, field_ref, _w, wave_out, rows_ref, sem):
+    chunk = step - sc_ref[0]
+
+    @pl.when((chunk >= 0) & (chunk < chunks))
+    def _():
+        start = first_row(chunk, field_ref.shape[1], wave_out.shape[0])
+        store_rows(field_ref, wave_out, rows_ref, sem, start).wait()
 
 
 def place_kernel(sc_ref, own_ref, own_other_ref, far_ref, far_other_ref, out_ref, sems):
@@ -239,6 +265,27 @@
         cost_estimate=pl.CostEstimate(flops=8 * m * width, bytes_accessed=24 * m * width, transcendentals=0),
         name="post",
     )
+    last_gradient = pl.pallas_call(
+        functools.partial(last_gradient_kernel, steps - 1, chunks),
+        out_shape=pltpu.VMEM((8, width), F32),
+        in_specs=[smem] + [vmem] * 3,
+        out_specs=vmem,
+        input_output_aliases={3: 0},
+        compiler_params=pltpu.CompilerParams(vmem_limit_bytes=LIMIT),
+        cost_estimate=pl.CostEstimate(flops=8 * m * width, bytes_accessed=12 * m * width, transcendentals=0),
+        name="last_gradient",
+    )
+    last_store = pl.pallas_call(
+        functools.partial(last_store_kernel, steps - 1, chunks),
+        out_shape=jax.ShapeDtypeStruct((sources, 2, width), F32),
+        in_specs=[smem, vmem, pl.BlockSpec(memory_space=pl.ANY)],
+        out_specs=pl.BlockSpec(memory_space=pl.ANY),
+        scratch_shapes=[pltpu.VMEM((m, 2, width), F32), pltpu.SemaphoreType.DMA(())],
+        input_output_aliases={2: 0},
+        compiler_params=pltpu.CompilerParams(vmem_limit_bytes=LIMIT),
+        cost_estimate=pl.CostEstimate(flops=0, bytes_accessed=16 * m * width, transcendentals=0),
+        name="last_store",
+    )
     picked = jnp.zeros((2,) + receiver_cell.shape, BF16)
     done = ()
     x = jnp.zeros((2, m, width + 128), BF16)
@@ -250,9 +297,11 @@
         pairs = [(i, i + 1) for i in range(stages - 1) if 0 <= t - i < chunks]
         if pairs:
             x = lax.ppermute(y[0], "fac", pairs)
-        done = post(t)(where, field, adjoint, *done)
-        x, done = lax.optimization_barrier((x, done))
-    wavefield, grad = done
+        if t < steps - 1:
+            done = post(t)(where, field, adjoint, *done)
+            x, done = lax.optimization_barrier((x, done))
+    wavefield = last_store(where, field, done[0])
+    grad = last_gradient(where, field, adjoint, done[1])
 
     rounds = fan_out(stages)
     first = [lax.ppermute(picked, "fac", pairs) for pairs in rounds[0]]
@@ -260,7 +309,7 @@
     scale = 1.0 / math.sqrt(sources * shards)
     terms = (jnp.sum(grad, axis=0) * scale).reshape(shards, rows)
     terms = lax.all_to_all(terms, SRC, 0, 0, tiled=True)
-    first, terms = lax.optimization_barrier((first, terms))
+    first, terms, wavefield = lax.optimization_barrier((first, terms, wavefield))
     gradient = jnp.sum(terms, axis=0)[None]
     picked = functools.reduce(jnp.add, first, picked)
     for pairs in rounds[1:]:

time: 184 us -> 185 us (level)
  blocking collectives: 31 us -> 0 us
  waiting for transfers between devices: 88.8 us -> 105 us
  starting transfers between devices: 37.9 us -> 52.4 us
    all_to_all x1 -> x0, blocking collectives: 31 us -> none  [per_device(): terms = lax.all_to_all(terms, SRC, 0, 0, tiled=True)]
    all_to_all x0 -> x1, waiting for transfers between devices: none -> 16.1 us  [per_device(): terms = lax.all_to_all(terms, SRC, 0, 0, tiled=True)]
    all_to_all x0 -> x1, starting transfers between devices: none -> 14.7 us  [per_device(): terms = lax.all_to_all(terms, SRC, 0, 0, tiled=True)]
    pallas_call x9 -> x8, Pallas kernels: 6.93 us -> 6.26 us  [per_device(): done = post(t)(where, field, adjoint, *done)]
  transfers between devices with their start and end apart: 17 -> 18, of which waited for: 8 -> 9; matrix products, arithmetic and copies ran while one was open for 1% -> 2% of each run, Pallas kernels for 4% -> 4%
where the time goes in v7:
time: 185 us; the launch traced here: 184 us
  waiting for transfers between devices  105 us (57%)
  starting transfers between devices  52.4 us (28%)
  Pallas kernels  18.4 us (10%)
  local copies, waits for them, and re-layouts  5.54 us (3%)
    ppermute x8, waiting for transfers between devices, per_device(): x = lax.ppermute(y[0], 'fac', pairs)  55.9 us
    all_to_all x2, waiting for transfers between devices, plane_gather(): return lax.all_to_all(spread, ('y', 'x'), 0, 0, tiled=True)  16.5 us
    all_to_all x1, waiting for transfers between devices, per_device(): terms = lax.all_to_all(terms, SRC, 0, 0, tiled=True)  16.1 us
    all_to_all x1, starting transfers between devices, per_device(): terms = lax.all_to_all(terms, SRC, 0, 0, tiled=True)  14.7 us
    all_to_all x2, starting transfers between devices, plane_gather(): return lax.all_to_all(spread, ('y', 'x'), 0, 0, tiled=True)  13 us
    ppermute x3, starting transfers between devices, swap(): return lax.ppermute(array, axis, [(0, 1), (1, 0)])  12.9 us
    ppermute x3, waiting for transfers between devices, swap(): return lax.ppermute(array, axis, [(0, 1), (1, 0)])  11.9 us
    pallas_call x9, Pallas kernels, per_device(): stage(t)  8.48 us
  transfers between devices with their start and end apart: 18, of which 9 were waited for; matrix products, arithmetic and copies ran while one was open for 2% of the time, Pallas kernels for 4%

profile of v7, /device:TPU:192, one launch (start us, length us, event | category | flops | bytes accessed | tf_op | source)
XLA Modules:
  0.0 184.0 jit_solution(2887366026404845669)
XLA Ops:
  0.7 1.0 broadcast_select_fusion
  1.8 1.1 broadcast_in_dim.26
  2.9 7.0 %all-to-all-start.1 = ((bf16[16,2,16,1152]{3,2,1,0:T(8,128)(2,1)}), bf16[16,2,16,1152]{3,2,1,0:T(8,128)(2,1)S(1)}, u32[]{:S(2)}, u32[]{:S(2)}) async-start(bf16[16,2,16,1152]{3,2,1,0:T(8,128)(2,1)} %broadcast_in_dim.26), calls=%async_computation.1 | async-start | bytes 2359296 | tf_op jit(solution)/shard_map/all_to_all | solution.py:179
  9.9 9.1 %collective-permute-start = (bf16[2,16,1152]{2,0,1:T(2,128)(2,1)S(1)}, bf16[2,16,1152]{2,0,1:T(2,128)(2,1)S(1)}, u32[]{:S(2)}, u32[]{:S(2)}) collective-permute-start(bf16[2,16,1152]{2,0,1:T(2,128)(2,1)S(1)} %broadcast_select_fusion), channel_id=1, source_target_pairs={{0,256},{256,0},{1,257},{257,1},{2,258},{258,2},{3,259},{259,3},{4... | collective-permute-start | bytes 221192 | tf_op jit(solution)/shard_map/ppermute | solution.py:173
  19.1 9.1 %collective-permute-done = bf16[2,16,1152]{2,0,1:T(2,128)(2,1)S(1)} collective-permute-done((bf16[2,16,1152]{2,0,1:T(2,128)(2,1)S(1)}, bf16[2,16,1152]{2,0,1:T(2,128)(2,1)S(1)}, u32[]{:S(2)}, u32[]{:S(2)}) %collective-permute-start) | collective-permute-done | bytes 73760 | tf_op jit(solution)/shard_map/ppermute | solution.py:173
  28.2 0.9 all-to-all-done.1.own_ref
  29.2 1.1 broadcast_in_dim.25
  30.3 6.0 %all-to-all-start = ((bf16[16,2,16,1152]{3,2,1,0:T(8,128)(2,1)}), bf16[16,2,16,1152]{3,2,1,0:T(8,128)(2,1)S(1)}, u32[]{:S(2)}, u32[]{:S(2)}) async-start(bf16[16,2,16,1152]{3,2,1,0:T(8,128)(2,1)} %broadcast_in_dim.25), calls=%async_computation | async-start | bytes 2359296 | tf_op jit(solution)/shard_map/all_to_all | solution.py:179
  36.3 0.1 fusion.1
  36.3 0.1 stack_broadcast_in_dim_tile.6
  36.4 0.1 stack_broadcast_in_dim_tile.7
  36.5 0.1 slice_bitcast_fusion.1
  36.6 0.1 stack_reshape.6
  36.7 0.1 stack_reshape.7
  36.8 0.1 copy.71
  36.9 1.2 copy.70
  38.1 1.9 %collective-permute-start.1 = (bf16[16,2,16,1152]{3,2,1,0:T(8,128)(2,1)S(1)}, bf16[16,2,16,1152]{3,2,1,0:T(8,128)(2,1)}, u32[]{:S(2)}, u32[]{:S(2)}) collective-permute-start(bf16[16,2,16,1152]{3,2,1,0:T(8,128)(2,1)S(1)} %all-to-all-done.1.own_ref), channel_id=1, source_target_pairs={{0,8},{8,0},{1,9},{9,1},{2,10},{10,2},{3,11},{11,3},{4,12},{12,4},... | collective-permute-start | bytes 3538952 | tf_op jit(solution)/shard_map/ppermute | solution.py:173
  40.0 15.6 %all-to-all-done.far_ref = bf16[16,2,16,1152]{3,2,1,0:T(8,128)(2,1)S(1)} async-done(((bf16[16,2,16,1152]{3,2,1,0:T(8,128)(2,1)}), bf16[16,2,16,1152]{3,2,1,0:T(8,128)(2,1)S(1)}, u32[]{:S(2)}, u32[]{:S(2)}) %all-to-all-start) | async-done | bytes 1179680 | tf_op jit(solution)/shard_map/all_to_all | solution.py:179
  55.6 1.9 %collective-permute-start.2 = (bf16[16,2,16,1152]{3,2,1,0:T(8,128)(2,1)S(1)}, bf16[16,2,16,1152]{3,2,1,0:T(8,128)(2,1)}, u32[]{:S(2)}, u32[]{:S(2)}) collective-permute-start(bf16[16,2,16,1152]{3,2,1,0:T(8,128)(2,1)S(1)} %all-to-all-done.far_ref), channel_id=1, source_target_pairs={{0,8},{8,0},{1,9},{9,1},{2,10},{10,2},{3,11},{11,3},{4,12},{12,4},... | collective-permute-start | bytes 3538952 | tf_op jit(solution)/shard_map/ppermute | solution.py:173
  57.5 0.1 pad_add_fusion.1.sc_ref
  57.6 0.0 copy-start
  57.6 2.8 %collective-permute-done.2.far_other_ref = bf16[16,2,16,1152]{3,2,1,0:T(8,128)(2,1)} collective-permute-done((bf16[16,2,16,1152]{3,2,1,0:T(8,128)(2,1)S(1)}, bf16[16,2,16,1152]{3,2,1,0:T(8,128)(2,1)}, u32[]{:S(2)}, u32[]{:S(2)}) %collective-permute-start.2) | collective-permute-done | bytes 1179680 | tf_op jit(solution)/shard_map/ppermute | solution.py:173
  60.4 2.6 %place.1.w_ref = bf16[2,2,16,2,16,1152]{5,4,3,2,1,0:T(8,128)(2,1)S(1)} custom-call(s32[3]{0:T(128)S(1)} %pad_add_fusion.1.sc_ref, bf16[16,2,16,1152]{3,2,1,0:T(8,128)(2,1)S(1)} %all-to-all-done.1.own_ref, bf16[16,2,16,1152]{3,2,1,0:T(8,128)(2,1)} %collective-permute-done.1.own_other_ref, bf16[16,2,16,1152]{3,2,1,0:T(8,128)(2,1)S(1)} %all-to-all-done.far_ref, ...), custom_call_target="tpu_custom_call" | custom-call | tf_op jit(solution)/shard_map/place/pallas_call | solution.py:190
  63.1 0.6 stage.9
  63.6 0.7 collective-permute-start.3
  64.3 0.6 post.8
  64.9 0.0 collective-permute-done.3.x_ref
  64.9 0.6 stage.10
  65.5 0.7 collective-permute-start.4
  66.2 0.6 post.9
  66.7 0.6 stage.11
  67.3 0.7 collective-permute-start.5
  68.0 0.6 post.10
  68.6 0.6 stage.12
  69.1 0.7 collective-permute-start.6
  69.8 0.6 post.11
  70.4 0.6 stage.13
  71.0 0.7 collective-permute-start.7
  71.6 0.6 post.12
  72.2 0.7 stage.14
  73.0 1.3 collective-permute-start.8
  74.3 0.6 post.13
  74.8 47.4 %collective-permute-done.8.x_ref = bf16[2,64,1152]{2,1,0:T(8,128)(2,1)S(1)} collective-permute-done((bf16[2,64,1152]{2,1,0:T(8,128)(2,1)S(1)}, bf16[2,64,1152]{2,1,0:T(8,128)(2,1)S(1)}, u32[]{:S(2)}, u32[]{:S(2)}) %collective-permute-start.8) | collective-permute-done | bytes 294944 | tf_op jit(solution)/shard_map/ppermute | solution.py:299
  122.3 2.2 %stage.15 = (f32[2,64,1024]{2,1,0:T(8,128)S(1)}, bf16[2,2,16,2,16,1152]{5,4,3,2,1,0:T(8,128)(2,1)S(1)}, bf16[2,128,128]{2,1,0:T(8,128)(2,1)S(1)}, bf16[2,64,1152]{2,1,0:T(8,128)(2,1)S(1)}) custom-call(s32[3]{0:T(128)S(1)} %pad_add_fusion.1.sc_ref, ...), custom_call_target="tpu_custom_call", output_to_operand_aliasing={{1}: (6, {}), {2}: (7, {})} | custom-call | flops 671088640 | bytes 4718592 | tf_op jit(solution)/shard_map/stage/pallas_call | solution.py:294
  124.5 1.9 %collective-permute-start.9 = (bf16[2,64,1152]{2,1,0:T(8,128)(2,1)S(1)}, bf16[2,64,1152]{2,1,0:T(8,128)(2,1)S(1)}, u32[]{:S(2)}, u32[]{:S(2)}) collective-permute-start(bf16[2,64,1152]{2,1,0:T(8,128)(2,1)S(1)} %get-tuple-element.143), channel_id=1, source_target_pairs={{5,6},{6,7},{13,14},{14,15},{21,22},{22,23},{29,30},{30,31},{37,38... | collective-permute-start | bytes 884744 | tf_op jit(solution)/shard_map/ppermute | solution.py:299
  126.4 1.4 post.14
  127.8 5.7 %collective-permute-done.9.x_ref = bf16[2,64,1152]{2,1,0:T(8,128)(2,1)S(1)} collective-permute-done((bf16[2,64,1152]{2,1,0:T(8,128)(2,1)S(1)}, bf16[2,64,1152]{2,1,0:T(8,128)(2,1)S(1)}, u32[]{:S(2)}, u32[]{:S(2)}) %collective-permute-start.9) | collective-permute-done | bytes 294944 | tf_op jit(solution)/shard_map/ppermute | solution.py:299
  133.5 2.2 %stage.16 = (f32[2,64,1024]{2,1,0:T(8,128)S(1)}, bf16[2,2,16,2,16,1152]{5,4,3,2,1,0:T(8,128)(2,1)S(1)}, bf16[2,128,128]{2,1,0:T(8,128)(2,1)S(1)}, bf16[2,64,1152]{2,1,0:T(8,128)(2,1)S(1)}) custom-call(s32[3]{0:T(128)S(1)} %pad_add_fusion.1.sc_ref, ...), custom_call_target="tpu_custom_call", output_to_operand_aliasing={{1}: (6, {}), {2}: (7, {})} | custom-call | flops 671088640 | bytes 4718592 | tf_op jit(solution)/shard_map/stage/pallas_call | solution.py:294
  135.7 1.9 %collective-permute-start.10 = (bf16[2,64,1152]{2,1,0:T(8,128)(2,1)S(1)}, bf16[2,64,1152]{2,1,0:T(8,128)(2,1)S(1)}, u32[]{:S(2)}, u32[]{:S(2)}) collective-permute-start(bf16[2,64,1152]{2,1,0:T(8,128)(2,1)S(1)} %get-tuple-element.152), channel_id=1, source_target_pairs={{6,7},{14,15},{22,23},{30,31},{38,39},{46,47},{54,55},{62,63},{70,... | collective-permute-start | bytes 884744 | tf_op jit(solution)/shard_map/ppermute | solution.py:299
  137.6 1.4 post.15
  139.0 2.8 %collective-permute-done.10.x_ref = bf16[2,64,1152]{2,1,0:T(8,128)(2,1)S(1)} collective-permute-done((bf16[2,64,1152]{2,1,0:T(8,128)(2,1)S(1)}, bf16[2,64,1152]{2,1,0:T(8,128)(2,1)S(1)}, u32[]{:S(2)}, u32[]{:S(2)}) %collective-permute-start.10) | collective-permute-done | bytes 294944 | tf_op jit(solution)/shard_map/ppermute | solution.py:299
  141.8 0.6 stage.17
  142.4 0.7 collective-permute-start.12
  143.0 0.7 collective-permute-start.11
  143.7 0.6 last_gradient.1
  144.3 0.7 mul.35
  145.0 14.7 %all-to-all-start.2 = ((f32[64,1,16]{2,1,0:T(1,128)}), f32[64,1,16]{2,1,0:T(1,128)S(1)}, u32[]{:S(2)}, u32[]{:S(2)}) async-start(f32[64,1,16]{2,1,0:T(1,128)} %bitcast.12), calls=%async_computation.2 | async-start | bytes 65536 | tf_op jit(solution)/shard_map/all_to_all | solution.py:311
  159.7 0.6 last_store.1
  160.2 16.1 %all-to-all-done.2 = f32[64,1,16]{2,1,0:T(1,128)S(1)} async-done(((f32[64,1,16]{2,1,0:T(1,128)}), f32[64,1,16]{2,1,0:T(1,128)S(1)}, u32[]{:S(2)}, u32[]{:S(2)}) %all-to-all-start.2) | async-done | bytes 4128 | tf_op jit(solution)/shard_map/all_to_all | solution.py:311
  176.4 0.7 collective-permute-start.13
  177.1 1.3 collective-permute-start.14
  178.4 0.5 reduce_sum.19
  178.9 4.3 %collective-permute-done.14 = bf16[2,128,128]{2,1,0:T(8,128)(2,1)S(1)} collective-permute-done((bf16[2,128,128]{2,1,0:T(8,128)(2,1)S(1)}, bf16[2,128,128]{2,1,0:T(8,128)(2,1)S(1)}, u32[]{:S(2)}, u32[]{:S(2)}) %collective-permute-start.14) | collective-permute-done | bytes 65568 | tf_op jit(solution)/shard_map/ppermute | solution.py:316
  183.3 0.8 copy.66
  (32 shorter events, 0.2 us)
Async XLA Ops:
  0.6 35.6 %copy-start.4 = (s32[128]{0:T(128)S(1)}, s32[128]{0:T(128)}, u32[]{:S(2)}) copy-start(s32[128]{0:T(128)} %param.10) | copy-start | bytes 1540
  0.6 35.9 %copy-start.3 = (f32[128,2]{0,1:T(2,128)S(1)}, f32[128,2]{0,1:T(2,128)}, u32[]{:S(2)}) copy-start(f32[128,2]{0,1:T(2,128)} %param.11) | copy-start | bytes 3076
  0.7 36.1 %copy-start.1 = (bf16[128,2,1024]{2,1,0:T(2,128)(2,1)S(1)}, bf16[128,2,1024]{2,1,0:T(2,128)(2,1)}, u32[]{:S(2)}) copy-start(bf16[128,2,1024]{2,1,0:T(2,128)(2,1)} %param.12) | copy-start | bytes 1572868
  2.9 26.3 %all-to-all-start.1 = ((bf16[16,2,16,1152]{3,2,1,0:T(8,128)(2,1)}), bf16[16,2,16,1152]{3,2,1,0:T(8,128)(2,1)S(1)}, u32[]{:S(2)}, u32[]{:S(2)}) async-start(bf16[16,2,16,1152]{3,2,1,0:T(8,128)(2,1)} %broadcast_in_dim.26), calls=%async_computation.1 | async-start | bytes 2359296 | tf_op jit(solution)/shard_map/all_to_all | solution.py:179
  9.9 18.3 %collective-permute-start = (bf16[2,16,1152]{2,0,1:T(2,128)(2,1)S(1)}, bf16[2,16,1152]{2,0,1:T(2,128)(2,1)S(1)}, u32[]{:S(2)}, u32[]{:S(2)}) collective-permute-start(bf16[2,16,1152]{2,0,1:T(2,128)(2,1)S(1)} %broadcast_select_fusion), channel_id=1, source_target_pairs={{0,256},{256,0},{1,257},{257,1},{2,258},{258,2},{3,259},{259,3},{4... | collective-permute-start | bytes 221192 | tf_op jit(solution)/shard_map/ppermute | solution.py:173
  30.3 25.3 %all-to-all-start = ((bf16[16,2,16,1152]{3,2,1,0:T(8,128)(2,1)}), bf16[16,2,16,1152]{3,2,1,0:T(8,128)(2,1)S(1)}, u32[]{:S(2)}, u32[]{:S(2)}) async-start(bf16[16,2,16,1152]{3,2,1,0:T(8,128)(2,1)} %broadcast_in_dim.25), calls=%async_computation | async-start | bytes 2359296 | tf_op jit(solution)/shard_map/all_to_all | solution.py:179
  38.1 19.6 %collective-permute-start.1 = (bf16[16,2,16,1152]{3,2,1,0:T(8,128)(2,1)S(1)}, bf16[16,2,16,1152]{3,2,1,0:T(8,128)(2,1)}, u32[]{:S(2)}, u32[]{:S(2)}) collective-permute-start(bf16[16,2,16,1152]{3,2,1,0:T(8,128)(2,1)S(1)} %all-to-all-done.1.own_ref), channel_id=1, source_target_pairs={{0,8},{8,0},{1,9},{9,1},{2,10},{10,2},{3,11},{11,3},{4,12},{12,4},... | collective-permute-start | bytes 3538952 | tf_op jit(solution)/shard_map/ppermute | solution.py:173
  55.6 4.9 %collective-permute-start.2 = (bf16[16,2,16,1152]{3,2,1,0:T(8,128)(2,1)S(1)}, bf16[16,2,16,1152]{3,2,1,0:T(8,128)(2,1)}, u32[]{:S(2)}, u32[]{:S(2)}) collective-permute-start(bf16[16,2,16,1152]{3,2,1,0:T(8,128)(2,1)S(1)} %all-to-all-done.far_ref), channel_id=1, source_target_pairs={{0,8},{8,0},{1,9},{9,1},{2,10},{10,2},{3,11},{11,3},{4,12},{12,4},... | collective-permute-start | bytes 3538952 | tf_op jit(solution)/shard_map/ppermute | solution.py:173
  57.6 5.5 %copy-start = (s32[128,128]{1,0:T(8,128)S(1)}, s32[128,128]{1,0:T(8,128)}, u32[]{:S(2)}) copy-start(s32[128,128]{1,0:T(8,128)} %receivers_ref.17) | copy-start | bytes 196612
  63.6 1.3 collective-permute-start.3
  65.5 1.3 collective-permute-start.4
  67.3 1.3 collective-permute-start.5
  69.1 1.3 collective-permute-start.6
  71.0 1.3 collective-permute-start.7
  73.0 49.3 %collective-permute-start.8 = (bf16[2,64,1152]{2,1,0:T(8,128)(2,1)S(1)}, bf16[2,64,1152]{2,1,0:T(8,128)(2,1)S(1)}, u32[]{:S(2)}, u32[]{:S(2)}) collective-permute-start(bf16[2,64,1152]{2,1,0:T(8,128)(2,1)S(1)} %get-tuple-element.134), channel_id=1, source_target_pairs={{4,5},{5,6},{12,13},{13,14},{20,21},{21,22},{28,29},{29,30},{36,37... | collective-permute-start | bytes 884744 | tf_op jit(solution)/shard_map/ppermute | solution.py:299
  124.5 9.0 %collective-permute-start.9 = (bf16[2,64,1152]{2,1,0:T(8,128)(2,1)S(1)}, bf16[2,64,1152]{2,1,0:T(8,128)(2,1)S(1)}, u32[]{:S(2)}, u32[]{:S(2)}) collective-permute-start(bf16[2,64,1152]{2,1,0:T(8,128)(2,1)S(1)} %get-tuple-element.143), channel_id=1, source_target_pairs={{5,6},{6,7},{13,14},{14,15},{21,22},{22,23},{29,30},{30,31},{37,38... | collective-permute-start | bytes 884744 | tf_op jit(solution)/shard_map/ppermute | solution.py:299
  135.7 6.1 %collective-permute-start.10 = (bf16[2,64,1152]{2,1,0:T(8,128)(2,1)S(1)}, bf16[2,64,1152]{2,1,0:T(8,128)(2,1)S(1)}, u32[]{:S(2)}, u32[]{:S(2)}) collective-permute-start(bf16[2,64,1152]{2,1,0:T(8,128)(2,1)S(1)} %get-tuple-element.152), channel_id=1, source_target_pairs={{6,7},{14,15},{22,23},{30,31},{38,39},{46,47},{54,55},{62,63},{70,... | collective-permute-start | bytes 884744 | tf_op jit(solution)/shard_map/ppermute | solution.py:299
  141.8 41.4 %copy-start.2 = (f32[128,2,128]{2,1,0:T(2,128)S(1)}, f32[128,2,128]{2,1,0:T(2,128)}, u32[]{:S(2)}) copy-start(f32[128,2,128]{2,1,0:T(2,128)} %param.14) | copy-start | bytes 393220
  142.4 34.0 %collective-permute-start.12 = (bf16[2,128,128]{2,1,0:T(8,128)(2,1)S(1)}, bf16[2,128,128]{2,1,0:T(8,128)(2,1)S(1)}, u32[]{:S(2)}, u32[]{:S(2)}) collective-permute-start(bf16[2,128,128]{2,1,0:T(8,128)(2,1)S(1)} %get-tuple-element.161), channel_id=1, source_target_pairs={{7,2},{15,10},{23,18},{31,26},{39,34},{47,42},{55,50},{63,58},{71,... | collective-permute-start | bytes 196616 | tf_op jit(solution)/shard_map/ppermute | solution.py:307
  143.0 33.3 %collective-permute-start.11 = (bf16[2,128,128]{2,1,0:T(8,128)(2,1)S(1)}, bf16[2,128,128]{2,1,0:T(8,128)(2,1)S(1)}, u32[]{:S(2)}, u32[]{:S(2)}) collective-permute-start(bf16[2,128,128]{2,1,0:T(8,128)(2,1)S(1)} %get-tuple-element.161), channel_id=1, source_target_pairs={{7,5},{15,13},{23,21},{31,29},{39,37},{47,45},{55,53},{63,61},{71,... | collective-permute-start | bytes 196616 | tf_op jit(solution)/shard_map/ppermute | solution.py:307
  145.0 31.4 %all-to-all-start.2 = ((f32[64,1,16]{2,1,0:T(1,128)}), f32[64,1,16]{2,1,0:T(1,128)S(1)}, u32[]{:S(2)}, u32[]{:S(2)}) async-start(f32[64,1,16]{2,1,0:T(1,128)} %bitcast.12), calls=%async_computation.2 | async-start | bytes 65536 | tf_op jit(solution)/shard_map/all_to_all | solution.py:311
  176.4 0.7 collective-permute-start.13
  177.1 6.2 %collective-permute-start.14 = (bf16[2,128,128]{2,1,0:T(8,128)(2,1)S(1)}, bf16[2,128,128]{2,1,0:T(8,128)(2,1)S(1)}, u32[]{:S(2)}, u32[]{:S(2)}) collective-permute-start(bf16[2,128,128]{2,1,0:T(8,128)(2,1)S(1)} %add.35), channel_id=1, source_target_pairs={{5,6},{2,1},{0,3},{13,14},{10,9},{8,11},{21,22},{18,17},{16,19},{2... | collective-permute-start | bytes 196616 | tf_op jit(solution)/shard_map/ppermute | solution.py:316

commit v8 on v7

--- a/solution.py
+++ b/solution.py
@@ -202,7 +202,7 @@
     last = stages - 1
     if stages != 8:
         return [[[(last, i)] for i in range(last)]]
-    return [[[(7, 5)], [(7, 2)]], [[(5, 4), (2, 0)]], [[(5, 6), (2, 1), (0, 3)]]]
+    return [[[(7, 6)], [(7, 4)], [(7, 1)]], [[(4, 5), (1, 0)]], [[(1, 2), (0, 3)]]]
 
 
 def per_device(lower, coupling, source_cell, source_wave, inflow, receiver_cell, observed, adjoint):

time: 185 us -> 185 us (level)
  the two profiles are of different devices: /device:TPU:192 before, /device:TPU:225 now
where the time goes in v8:
time: 185 us; the launch traced here: 184 us
  waiting for transfers between devices  96.1 us (52%)
  starting transfers between devices  60.9 us (33%)
  Pallas kernels  18.5 us (10%)
  local copies, waits for them, and re-layouts  5.53 us (3%)
    ppermute x8, waiting for transfers between devices, per_device(): x = lax.ppermute(y[0], 'fac', pairs)  57.5 us
    all_to_all x1, starting transfers between devices, per_device(): terms = lax.all_to_all(terms, SRC, 0, 0, tiled=True)  20.8 us
    ppermute x3, starting transfers between devices, swap(): return lax.ppermute(array, axis, [(0, 1), (1, 0)])  16.4 us
    all_to_all x2, waiting for transfers between devices, plane_gather(): return lax.all_to_all(spread, ('y', 'x'), 0, 0, tiled=True)  15.2 us
    all_to_all x1, waiting for transfers between devices, per_device(): terms = lax.all_to_all(terms, SRC, 0, 0, tiled=True)  15 us
    all_to_all x2, starting transfers between devices, plane_gather(): return lax.all_to_all(spread, ('y', 'x'), 0, 0, tiled=True)  11.8 us
    pallas_call x9, Pallas kernels, per_device(): stage(t)  8.48 us
    ppermute x3, waiting for transfers between devices, swap(): return lax.ppermute(array, axis, [(0, 1), (1, 0)])  8.31 us
  transfers between devices with their start and end apart: 19, of which 7 were waited for; matrix products, arithmetic and copies ran while one was open for 2% of the time, Pallas kernels for 4%

profile of v8, /device:TPU:225, one launch (start us, length us, event | category | flops | bytes accessed | tf_op | source)
XLA Modules:
  0.0 184.0 jit_solution(18351014262732858556)
XLA Ops:
  0.7 1.0 broadcast_select_fusion
  1.8 1.1 broadcast_in_dim.26
  2.9 6.8 %all-to-all-start.1 = ((bf16[16,2,16,1152]{3,2,1,0:T(8,128)(2,1)}), bf16[16,2,16,1152]{3,2,1,0:T(8,128)(2,1)S(1)}, u32[]{:S(2)}, u32[]{:S(2)}) async-start(bf16[16,2,16,1152]{3,2,1,0:T(8,128)(2,1)} %broadcast_in_dim.26), calls=%async_computation.1 | async-start | bytes 2359296 | tf_op jit(solution)/shard_map/all_to_all | solution.py:179
  9.6 7.9 %collective-permute-start = (bf16[2,16,1152]{2,0,1:T(2,128)(2,1)S(1)}, bf16[2,16,1152]{2,0,1:T(2,128)(2,1)S(1)}, u32[]{:S(2)}, u32[]{:S(2)}) collective-permute-start(bf16[2,16,1152]{2,0,1:T(2,128)(2,1)S(1)} %broadcast_select_fusion), channel_id=1, source_target_pairs={{0,256},{256,0},{1,257},{257,1},{2,258},{258,2},{3,259},{259,3},{4... | collective-permute-start | bytes 221192 | tf_op jit(solution)/shard_map/ppermute | solution.py:173
  17.6 5.9 %collective-permute-done = bf16[2,16,1152]{2,0,1:T(2,128)(2,1)S(1)} collective-permute-done((bf16[2,16,1152]{2,0,1:T(2,128)(2,1)S(1)}, bf16[2,16,1152]{2,0,1:T(2,128)(2,1)S(1)}, u32[]{:S(2)}, u32[]{:S(2)}) %collective-permute-start) | collective-permute-done | bytes 73760 | tf_op jit(solution)/shard_map/ppermute | solution.py:173
  23.5 3.6 %all-to-all-done.1.own_ref = bf16[16,2,16,1152]{3,2,1,0:T(8,128)(2,1)S(1)} async-done(((bf16[16,2,16,1152]{3,2,1,0:T(8,128)(2,1)}), bf16[16,2,16,1152]{3,2,1,0:T(8,128)(2,1)S(1)}, u32[]{:S(2)}, u32[]{:S(2)}) %all-to-all-start.1) | async-done | bytes 1179680 | tf_op jit(solution)/shard_map/all_to_all | solution.py:179
  27.0 1.1 broadcast_in_dim.25
  28.1 5.0 %all-to-all-start = ((bf16[16,2,16,1152]{3,2,1,0:T(8,128)(2,1)}), bf16[16,2,16,1152]{3,2,1,0:T(8,128)(2,1)S(1)}, u32[]{:S(2)}, u32[]{:S(2)}) async-start(bf16[16,2,16,1152]{3,2,1,0:T(8,128)(2,1)} %broadcast_in_dim.25), calls=%async_computation | async-start | bytes 2359296 | tf_op jit(solution)/shard_map/all_to_all | solution.py:179
  33.2 0.1 fusion.1
  33.2 0.1 stack_broadcast_in_dim_tile.6
  33.3 0.1 stack_broadcast_in_dim_tile.7
  33.4 0.1 slice_bitcast_fusion.1
  33.5 0.1 stack_reshape.6
  33.6 0.1 stack_reshape.7
  33.6 0.1 copy.71
  33.8 1.2 copy.70
  34.9 3.4 %collective-permute-start.1 = (bf16[16,2,16,1152]{3,2,1,0:T(8,128)(2,1)S(1)}, bf16[16,2,16,1152]{3,2,1,0:T(8,128)(2,1)}, u32[]{:S(2)}, u32[]{:S(2)}) collective-permute-start(bf16[16,2,16,1152]{3,2,1,0:T(8,128)(2,1)S(1)} %all-to-all-done.1.own_ref), channel_id=1, source_target_pairs={{0,8},{8,0},{1,9},{9,1},{2,10},{10,2},{3,11},{11,3},{4,12},{12,4},... | collective-permute-start | bytes 3538952 | tf_op jit(solution)/shard_map/ppermute | solution.py:173
  38.3 11.7 %all-to-all-done.far_ref = bf16[16,2,16,1152]{3,2,1,0:T(8,128)(2,1)S(1)} async-done(((bf16[16,2,16,1152]{3,2,1,0:T(8,128)(2,1)}), bf16[16,2,16,1152]{3,2,1,0:T(8,128)(2,1)S(1)}, u32[]{:S(2)}, u32[]{:S(2)}) %all-to-all-start) | async-done | bytes 1179680 | tf_op jit(solution)/shard_map/all_to_all | solution.py:179
  50.0 5.1 %collective-permute-start.2 = (bf16[16,2,16,1152]{3,2,1,0:T(8,128)(2,1)S(1)}, bf16[16,2,16,1152]{3,2,1,0:T(8,128)(2,1)}, u32[]{:S(2)}, u32[]{:S(2)}) collective-permute-start(bf16[16,2,16,1152]{3,2,1,0:T(8,128)(2,1)S(1)} %all-to-all-done.far_ref), channel_id=1, source_target_pairs={{0,8},{8,0},{1,9},{9,1},{2,10},{10,2},{3,11},{11,3},{4,12},{12,4},... | collective-permute-start | bytes 3538952 | tf_op jit(solution)/shard_map/ppermute | solution.py:173
  55.1 0.1 pad_add_fusion.1.sc_ref
  55.3 0.0 copy-start
  55.3 0.0 collective-permute-done.1.own_other_ref
  55.3 2.4 %collective-permute-done.2.far_other_ref = bf16[16,2,16,1152]{3,2,1,0:T(8,128)(2,1)} collective-permute-done((bf16[16,2,16,1152]{3,2,1,0:T(8,128)(2,1)S(1)}, bf16[16,2,16,1152]{3,2,1,0:T(8,128)(2,1)}, u32[]{:S(2)}, u32[]{:S(2)}) %collective-permute-start.2) | collective-permute-done | bytes 1179680 | tf_op jit(solution)/shard_map/ppermute | solution.py:173
  57.7 2.6 %place.1.w_ref = bf16[2,2,16,2,16,1152]{5,4,3,2,1,0:T(8,128)(2,1)S(1)} custom-call(s32[3]{0:T(128)S(1)} %pad_add_fusion.1.sc_ref, bf16[16,2,16,1152]{3,2,1,0:T(8,128)(2,1)S(1)} %all-to-all-done.1.own_ref, bf16[16,2,16,1152]{3,2,1,0:T(8,128)(2,1)} %collective-permute-done.1.own_other_ref, bf16[16,2,16,1152]{3,2,1,0:T(8,128)(2,1)S(1)} %all-to-all-done.far_ref, ...), custom_call_target="tpu_custom_call" | custom-call | tf_op jit(solution)/shard_map/place/pallas_call | solution.py:190
  60.4 0.6 stage.9
  60.9 0.7 collective-permute-start.3
  61.6 0.6 post.8
  62.2 0.6 stage.10
  62.7 0.7 collective-permute-start.4
  63.4 0.6 post.9
  64.0 0.6 stage.11
  64.6 0.7 collective-permute-start.5
  65.3 0.6 post.10
  65.8 0.6 stage.12
  66.4 0.7 collective-permute-start.6
  67.1 0.6 post.11
  67.7 0.6 stage.13
  68.2 0.7 collective-permute-start.7
  68.9 0.6 post.12
  69.5 0.7 stage.14
  70.2 0.7 collective-permute-start.8
  70.9 0.6 post.13
  71.5 0.0 collective-permute-done.8.x_ref
  71.5 0.6 stage.15
  72.1 1.3 collective-permute-start.9
  73.4 0.6 post.14
  73.9 52.8 %collective-permute-done.9.x_ref = bf16[2,64,1152]{2,1,0:T(8,128)(2,1)S(1)} collective-permute-done((bf16[2,64,1152]{2,1,0:T(8,128)(2,1)S(1)}, bf16[2,64,1152]{2,1,0:T(8,128)(2,1)S(1)}, u32[]{:S(2)}, u32[]{:S(2)}) %collective-permute-start.9) | collective-permute-done | bytes 294944 | tf_op jit(solution)/shard_map/ppermute | solution.py:299
  126.7 2.2 %stage.16 = (f32[2,64,1024]{2,1,0:T(8,128)S(1)}, bf16[2,2,16,2,16,1152]{5,4,3,2,1,0:T(8,128)(2,1)S(1)}, bf16[2,128,128]{2,1,0:T(8,128)(2,1)S(1)}, bf16[2,64,1152]{2,1,0:T(8,128)(2,1)S(1)}) custom-call(s32[3]{0:T(128)S(1)} %pad_add_fusion.1.sc_ref, ...), custom_call_target="tpu_custom_call", output_to_operand_aliasing={{1}: (6, {}), {2}: (7, {})} | custom-call | flops 671088640 | bytes 4718592 | tf_op jit(solution)/shard_map/stage/pallas_call | solution.py:294
  129.0 1.3 collective-permute-start.10
  130.3 1.4 post.15
  131.7 4.7 %collective-permute-done.10.x_ref = bf16[2,64,1152]{2,1,0:T(8,128)(2,1)S(1)} collective-permute-done((bf16[2,64,1152]{2,1,0:T(8,128)(2,1)S(1)}, bf16[2,64,1152]{2,1,0:T(8,128)(2,1)S(1)}, u32[]{:S(2)}, u32[]{:S(2)}) %collective-permute-start.10) | collective-permute-done | bytes 294944 | tf_op jit(solution)/shard_map/ppermute | solution.py:299
  136.4 2.2 %stage.17 = (f32[2,64,1024]{2,1,0:T(8,128)S(1)}, bf16[2,2,16,2,16,1152]{5,4,3,2,1,0:T(8,128)(2,1)S(1)}, bf16[2,128,128]{2,1,0:T(8,128)(2,1)S(1)}) custom-call(s32[3]{0:T(128)S(1)} %pad_add_fusion.1.sc_ref, bf16[2,64,1152]{2,1,0:T(8,128)(2,1)S(1)} %collective-permute-done.10.x_ref, ...), custom_call_target="tpu_custom_call", output_to_operand_aliasing={{1}: (6, {}), {2}: (7, {})} | custom-call | flops 671088640 | bytes 4718592 | tf_op jit(solution)/shard_map/stage/pallas_call | solution.py:294
  138.7 1.3 collective-permute-start.13
  140.0 1.3 collective-permute-start.12
  141.3 1.3 collective-permute-start.11
  142.6 0.6 last_gradient.1
  143.2 0.7 mul.35
  143.9 20.8 %all-to-all-start.2 = ((f32[64,1,16]{2,1,0:T(1,128)}), f32[64,1,16]{2,1,0:T(1,128)S(1)}, u32[]{:S(2)}, u32[]{:S(2)}) async-start(f32[64,1,16]{2,1,0:T(1,128)} %bitcast.12), calls=%async_computation.2 | async-start | bytes 65536 | tf_op jit(solution)/shard_map/all_to_all | solution.py:311
  164.7 1.4 last_store.1
  166.2 15.0 %all-to-all-done.2 = f32[64,1,16]{2,1,0:T(1,128)S(1)} async-done(((f32[64,1,16]{2,1,0:T(1,128)}), f32[64,1,16]{2,1,0:T(1,128)S(1)}, u32[]{:S(2)}, u32[]{:S(2)}) %all-to-all-start.2) | async-done | bytes 4128 | tf_op jit(solution)/shard_map/all_to_all | solution.py:311
  181.2 0.7 collective-permute-start.14
  182.0 0.7 collective-permute-start.15
  182.6 0.5 reduce_sum.19
  183.2 0.8 copy.66
  (34 shorter events, 0.2 us)
Async XLA Ops:
  0.6 32.5 %copy-start.4 = (s32[128]{0:T(128)S(1)}, s32[128]{0:T(128)}, u32[]{:S(2)}) copy-start(s32[128]{0:T(128)} %param.10) | copy-start | bytes 1540
  0.6 32.8 %copy-start.3 = (f32[128,2]{0,1:T(2,128)S(1)}, f32[128,2]{0,1:T(2,128)}, u32[]{:S(2)}) copy-start(f32[128,2]{0,1:T(2,128)} %param.11) | copy-start | bytes 3076
  0.7 33.0 %copy-start.1 = (bf16[128,2,1024]{2,1,0:T(2,128)(2,1)S(1)}, bf16[128,2,1024]{2,1,0:T(2,128)(2,1)}, u32[]{:S(2)}) copy-start(bf16[128,2,1024]{2,1,0:T(2,128)(2,1)} %param.12) | copy-start | bytes 1572868
  2.9 24.2 %all-to-all-start.1 = ((bf16[16,2,16,1152]{3,2,1,0:T(8,128)(2,1)}), bf16[16,2,16,1152]{3,2,1,0:T(8,128)(2,1)S(1)}, u32[]{:S(2)}, u32[]{:S(2)}) async-start(bf16[16,2,16,1152]{3,2,1,0:T(8,128)(2,1)} %broadcast_in_dim.26), calls=%async_computation.1 | async-start | bytes 2359296 | tf_op jit(solution)/shard_map/all_to_all | solution.py:179
  9.6 13.8 %collective-permute-start = (bf16[2,16,1152]{2,0,1:T(2,128)(2,1)S(1)}, bf16[2,16,1152]{2,0,1:T(2,128)(2,1)S(1)}, u32[]{:S(2)}, u32[]{:S(2)}) collective-permute-start(bf16[2,16,1152]{2,0,1:T(2,128)(2,1)S(1)} %broadcast_select_fusion), channel_id=1, source_target_pairs={{0,256},{256,0},{1,257},{257,1},{2,258},{258,2},{3,259},{259,3},{4... | collective-permute-start | bytes 221192 | tf_op jit(solution)/shard_map/ppermute | solution.py:173
  28.1 21.9 %all-to-all-start = ((bf16[16,2,16,1152]{3,2,1,0:T(8,128)(2,1)}), bf16[16,2,16,1152]{3,2,1,0:T(8,128)(2,1)S(1)}, u32[]{:S(2)}, u32[]{:S(2)}) async-start(bf16[16,2,16,1152]{3,2,1,0:T(8,128)(2,1)} %broadcast_in_dim.25), calls=%async_computation | async-start | bytes 2359296 | tf_op jit(solution)/shard_map/all_to_all | solution.py:179
  34.9 20.3 %collective-permute-start.1 = (bf16[16,2,16,1152]{3,2,1,0:T(8,128)(2,1)S(1)}, bf16[16,2,16,1152]{3,2,1,0:T(8,128)(2,1)}, u32[]{:S(2)}, u32[]{:S(2)}) collective-permute-start(bf16[16,2,16,1152]{3,2,1,0:T(8,128)(2,1)S(1)} %all-to-all-done.1.own_ref), channel_id=1, source_target_pairs={{0,8},{8,0},{1,9},{9,1},{2,10},{10,2},{3,11},{11,3},{4,12},{12,4},... | collective-permute-start | bytes 3538952 | tf_op jit(solution)/shard_map/ppermute | solution.py:173
  50.0 7.7 %collective-permute-start.2 = (bf16[16,2,16,1152]{3,2,1,0:T(8,128)(2,1)S(1)}, bf16[16,2,16,1152]{3,2,1,0:T(8,128)(2,1)}, u32[]{:S(2)}, u32[]{:S(2)}) collective-permute-start(bf16[16,2,16,1152]{3,2,1,0:T(8,128)(2,1)S(1)} %all-to-all-done.far_ref), channel_id=1, source_target_pairs={{0,8},{8,0},{1,9},{9,1},{2,10},{10,2},{3,11},{11,3},{4,12},{12,4},... | collective-permute-start | bytes 3538952 | tf_op jit(solution)/shard_map/ppermute | solution.py:173
  55.3 5.1 %copy-start = (s32[128,128]{1,0:T(8,128)S(1)}, s32[128,128]{1,0:T(8,128)}, u32[]{:S(2)}) copy-start(s32[128,128]{1,0:T(8,128)} %receivers_ref.17) | copy-start | bytes 196612
  60.9 1.3 collective-permute-start.3
  62.7 1.3 collective-permute-start.4
  64.6 1.3 collective-permute-start.5
  66.4 1.3 collective-permute-start.6
  68.2 1.3 collective-permute-start.7
  70.2 1.3 collective-permute-start.8
  72.1 54.7 %collective-permute-start.9 = (bf16[2,64,1152]{2,1,0:T(8,128)(2,1)S(1)}, bf16[2,64,1152]{2,1,0:T(8,128)(2,1)S(1)}, u32[]{:S(2)}, u32[]{:S(2)}) collective-permute-start(bf16[2,64,1152]{2,1,0:T(8,128)(2,1)S(1)} %get-tuple-element.144), channel_id=1, source_target_pairs={{5,6},{6,7},{13,14},{14,15},{21,22},{22,23},{29,30},{30,31},{37,38... | collective-permute-start | bytes 884744 | tf_op jit(solution)/shard_map/ppermute | solution.py:299
  129.0 7.5 %collective-permute-start.10 = (bf16[2,64,1152]{2,1,0:T(8,128)(2,1)S(1)}, bf16[2,64,1152]{2,1,0:T(8,128)(2,1)S(1)}, u32[]{:S(2)}, u32[]{:S(2)}) collective-permute-start(bf16[2,64,1152]{2,1,0:T(8,128)(2,1)S(1)} %get-tuple-element.153), channel_id=1, source_target_pairs={{6,7},{14,15},{22,23},{30,31},{38,39},{46,47},{54,55},{62,63},{70,... | collective-permute-start | bytes 884744 | tf_op jit(solution)/shard_map/ppermute | solution.py:299
  136.4 46.8 %copy-start.2 = (f32[128,2,128]{2,1,0:T(2,128)S(1)}, f32[128,2,128]{2,1,0:T(2,128)}, u32[]{:S(2)}) copy-start(f32[128,2,128]{2,1,0:T(2,128)} %param.14) | copy-start | bytes 393220
  138.7 42.6 %collective-permute-start.13 = (bf16[2,128,128]{2,1,0:T(8,128)(2,1)S(1)}, bf16[2,128,128]{2,1,0:T(8,128)(2,1)S(1)}, u32[]{:S(2)}, u32[]{:S(2)}) collective-permute-start(bf16[2,128,128]{2,1,0:T(8,128)(2,1)S(1)} %get-tuple-element.162), channel_id=1, source_target_pairs={{7,1},{15,9},{23,17},{31,25},{39,33},{47,41},{55,49},{63,57},{71,6... | collective-permute-start | bytes 196616 | tf_op jit(solution)/shard_map/ppermute | solution.py:307
  140.0 41.3 %collective-permute-start.12 = (bf16[2,128,128]{2,1,0:T(8,128)(2,1)S(1)}, bf16[2,128,128]{2,1,0:T(8,128)(2,1)S(1)}, u32[]{:S(2)}, u32[]{:S(2)}) collective-permute-start(bf16[2,128,128]{2,1,0:T(8,128)(2,1)S(1)} %get-tuple-element.162), channel_id=1, source_target_pairs={{7,4},{15,12},{23,20},{31,28},{39,36},{47,44},{55,52},{63,60},{71,... | collective-permute-start | bytes 196616 | tf_op jit(solution)/shard_map/ppermute | solution.py:307
  141.3 40.0 %collective-permute-start.11 = (bf16[2,128,128]{2,1,0:T(8,128)(2,1)S(1)}, bf16[2,128,128]{2,1,0:T(8,128)(2,1)S(1)}, u32[]{:S(2)}, u32[]{:S(2)}) collective-permute-start(bf16[2,128,128]{2,1,0:T(8,128)(2,1)S(1)} %get-tuple-element.162), channel_id=1, source_target_pairs={{7,6},{15,14},{23,22},{31,30},{39,38},{47,46},{55,54},{63,62},{71,... | collective-permute-start | bytes 196616 | tf_op jit(solution)/shard_map/ppermute | solution.py:307
  143.9 37.3 %all-to-all-start.2 = ((f32[64,1,16]{2,1,0:T(1,128)}), f32[64,1,16]{2,1,0:T(1,128)S(1)}, u32[]{:S(2)}, u32[]{:S(2)}) async-start(f32[64,1,16]{2,1,0:T(1,128)} %bitcast.12), calls=%async_computation.2 | async-start | bytes 65536 | tf_op jit(solution)/shard_map/all_to_all | solution.py:311
  181.2 0.7 collective-permute-start.14
  182.0 1.2 collective-permute-start.15

commit v9 on v8

--- a/solution.py
+++ b/solution.py
@@ -202,7 +202,7 @@
     last = stages - 1
     if stages != 8:
         return [[[(last, i)] for i in range(last)]]
-    return [[[(7, 6)], [(7, 4)], [(7, 1)]], [[(4, 5), (1, 0)]], [[(1, 2), (0, 3)]]]
+    return [[[(7, 6)], [(7, 2)]], [[(2, 0), (6, 5)]], [[(2, 1), (0, 3), (6, 4)]]]
 
 
 def per_device(lower, coupling, source_cell, source_wave, inflow, receiver_cell, observed, adjoint):

time: 185 us -> 188 us (1.016)
  the two profiles are of different devices: /device:TPU:225 before, /device:TPU:128 now
where the time goes in v9:
time: 188 us
  waiting for transfers between devices  108 us (57%)
  starting transfers between devices  53.1 us (28%)
  Pallas kernels  18.4 us (10%)
  local copies, waits for them, and re-layouts  5.54 us (3%)
    ppermute x8, waiting for transfers between devices, per_device(): x = lax.ppermute(y[0], 'fac', pairs)  44.3 us
    ppermute x2, waiting for transfers between devices, per_device(): lax.ppermute(picked, 'fac', p)  21.9 us
    all_to_all x1, waiting for transfers between devices, per_device(): terms = lax.all_to_all(terms, SRC, 0, 0, tiled=True)  16.1 us
    all_to_all x2, waiting for transfers between devices, plane_gather(): return lax.all_to_all(spread, ('y', 'x'), 0, 0, tiled=True)  16 us
    ppermute x3, starting transfers between devices, swap(): return lax.ppermute(array, axis, [(0, 1), (1, 0)])  14.7 us
    all_to_all x1, starting transfers between devices, per_device(): terms = lax.all_to_all(terms, SRC, 0, 0, tiled=True)  14.7 us
    all_to_all x2, starting transfers between devices, plane_gather(): return lax.all_to_all(spread, ('y', 'x'), 0, 0, tiled=True)  12.5 us
    ppermute x3, waiting for transfers between devices, swap(): return lax.ppermute(array, axis, [(0, 1), (1, 0)])  9.57 us
  transfers between devices with their start and end apart: 18, of which 9 were waited for; matrix products, arithmetic and copies ran while one was open for 2% of the time, Pallas kernels for 4%

profile of v9, /device:TPU:128, one launch (start us, length us, event | category | flops | bytes accessed | tf_op | source)
XLA Modules:
  0.0 187.8 jit_solution(16710453917695202659)
XLA Ops:
  0.7 1.0 broadcast_select_fusion
  1.8 1.1 broadcast_in_dim.26
  2.9 7.0 %all-to-all-start.1 = ((bf16[16,2,16,1152]{3,2,1,0:T(8,128)(2,1)}), bf16[16,2,16,1152]{3,2,1,0:T(8,128)(2,1)S(1)}, u32[]{:S(2)}, u32[]{:S(2)}) async-start(bf16[16,2,16,1152]{3,2,1,0:T(8,128)(2,1)} %broadcast_in_dim.26), calls=%async_computation.1 | async-start | bytes 2359296 | tf_op jit(solution)/shard_map/all_to_all | solution.py:179
  9.9 10.9 %collective-permute-start = (bf16[2,16,1152]{2,0,1:T(2,128)(2,1)S(1)}, bf16[2,16,1152]{2,0,1:T(2,128)(2,1)S(1)}, u32[]{:S(2)}, u32[]{:S(2)}) collective-permute-start(bf16[2,16,1152]{2,0,1:T(2,128)(2,1)S(1)} %broadcast_select_fusion), channel_id=1, source_target_pairs={{0,256},{256,0},{1,257},{257,1},{2,258},{258,2},{3,259},{259,3},{4... | collective-permute-start | bytes 221192 | tf_op jit(solution)/shard_map/ppermute | solution.py:173
  20.9 6.8 %collective-permute-done = bf16[2,16,1152]{2,0,1:T(2,128)(2,1)S(1)} collective-permute-done((bf16[2,16,1152]{2,0,1:T(2,128)(2,1)S(1)}, bf16[2,16,1152]{2,0,1:T(2,128)(2,1)S(1)}, u32[]{:S(2)}, u32[]{:S(2)}) %collective-permute-start) | collective-permute-done | bytes 73760 | tf_op jit(solution)/shard_map/ppermute | solution.py:173
  27.6 1.5 all-to-all-done.1.own_ref
  29.2 1.1 broadcast_in_dim.25
  30.3 5.4 %all-to-all-start = ((bf16[16,2,16,1152]{3,2,1,0:T(8,128)(2,1)}), bf16[16,2,16,1152]{3,2,1,0:T(8,128)(2,1)S(1)}, u32[]{:S(2)}, u32[]{:S(2)}) async-start(bf16[16,2,16,1152]{3,2,1,0:T(8,128)(2,1)} %broadcast_in_dim.25), calls=%async_computation | async-start | bytes 2359296 | tf_op jit(solution)/shard_map/all_to_all | solution.py:179
  35.7 0.1 fusion.1
  35.8 0.1 stack_broadcast_in_dim_tile.6
  35.9 0.1 stack_broadcast_in_dim_tile.7
  36.0 0.1 slice_bitcast_fusion.1
  36.0 0.1 stack_reshape.6
  36.1 0.1 stack_reshape.7
  36.2 0.1 copy.71
  36.3 1.2 copy.70
  37.5 1.9 %collective-permute-start.1 = (bf16[16,2,16,1152]{3,2,1,0:T(8,128)(2,1)S(1)}, bf16[16,2,16,1152]{3,2,1,0:T(8,128)(2,1)}, u32[]{:S(2)}, u32[]{:S(2)}) collective-permute-start(bf16[16,2,16,1152]{3,2,1,0:T(8,128)(2,1)S(1)} %all-to-all-done.1.own_ref), channel_id=1, source_target_pairs={{0,8},{8,0},{1,9},{9,1},{2,10},{10,2},{3,11},{11,3},{4,12},{12,4},... | collective-permute-start | bytes 3538952 | tf_op jit(solution)/shard_map/ppermute | solution.py:173
  39.4 14.4 %all-to-all-done.far_ref = bf16[16,2,16,1152]{3,2,1,0:T(8,128)(2,1)S(1)} async-done(((bf16[16,2,16,1152]{3,2,1,0:T(8,128)(2,1)}), bf16[16,2,16,1152]{3,2,1,0:T(8,128)(2,1)S(1)}, u32[]{:S(2)}, u32[]{:S(2)}) %all-to-all-start) | async-done | bytes 1179680 | tf_op jit(solution)/shard_map/all_to_all | solution.py:179
  53.9 1.9 %collective-permute-start.2 = (bf16[16,2,16,1152]{3,2,1,0:T(8,128)(2,1)S(1)}, bf16[16,2,16,1152]{3,2,1,0:T(8,128)(2,1)}, u32[]{:S(2)}, u32[]{:S(2)}) collective-permute-start(bf16[16,2,16,1152]{3,2,1,0:T(8,128)(2,1)S(1)} %all-to-all-done.far_ref), channel_id=1, source_target_pairs={{0,8},{8,0},{1,9},{9,1},{2,10},{10,2},{3,11},{11,3},{4,12},{12,4},... | collective-permute-start | bytes 3538952 | tf_op jit(solution)/shard_map/ppermute | solution.py:173
  55.8 0.1 pad_add_fusion.1.sc_ref
  55.9 0.0 copy-start
  55.9 2.8 %collective-permute-done.2.far_other_ref = bf16[16,2,16,1152]{3,2,1,0:T(8,128)(2,1)} collective-permute-done((bf16[16,2,16,1152]{3,2,1,0:T(8,128)(2,1)S(1)}, bf16[16,2,16,1152]{3,2,1,0:T(8,128)(2,1)}, u32[]{:S(2)}, u32[]{:S(2)}) %collective-permute-start.2) | collective-permute-done | bytes 1179680 | tf_op jit(solution)/shard_map/ppermute | solution.py:173
  58.7 2.6 %place.1.w_ref = bf16[2,2,16,2,16,1152]{5,4,3,2,1,0:T(8,128)(2,1)S(1)} custom-call(s32[3]{0:T(128)S(1)} %pad_add_fusion.1.sc_ref, bf16[16,2,16,1152]{3,2,1,0:T(8,128)(2,1)S(1)} %all-to-all-done.1.own_ref, bf16[16,2,16,1152]{3,2,1,0:T(8,128)(2,1)} %collective-permute-done.1.own_other_ref, bf16[16,2,16,1152]{3,2,1,0:T(8,128)(2,1)S(1)} %all-to-all-done.far_ref, ...), custom_call_target="tpu_custom_call" | custom-call | tf_op jit(solution)/shard_map/place/pallas_call | solution.py:190
  61.4 0.6 stage.9
  61.9 0.7 collective-permute-start.3
  62.6 0.6 post.8
  63.2 0.6 stage.10
  63.8 0.7 collective-permute-start.4
  64.4 0.6 post.9
  65.0 0.6 stage.11
  65.6 0.7 collective-permute-start.5
  66.3 0.6 post.10
  66.9 0.6 stage.12
  67.4 1.3 collective-permute-start.6
  68.7 0.6 post.11
  69.3 34.7 %collective-permute-done.6.x_ref = bf16[2,64,1152]{2,1,0:T(8,128)(2,1)S(1)} collective-permute-done((bf16[2,64,1152]{2,1,0:T(8,128)(2,1)S(1)}, bf16[2,64,1152]{2,1,0:T(8,128)(2,1)S(1)}, u32[]{:S(2)}, u32[]{:S(2)}) %collective-permute-start.6) | collective-permute-done | bytes 294944 | tf_op jit(solution)/shard_map/ppermute | solution.py:299
  104.0 2.2 %stage.13 = (f32[2,64,1024]{2,1,0:T(8,128)S(1)}, bf16[2,2,16,2,16,1152]{5,4,3,2,1,0:T(8,128)(2,1)S(1)}, bf16[2,128,128]{2,1,0:T(8,128)(2,1)S(1)}, bf16[2,64,1152]{2,1,0:T(8,128)(2,1)S(1)}) custom-call(s32[3]{0:T(128)S(1)} %pad_add_fusion.1.sc_ref, ...), custom_call_target="tpu_custom_call", output_to_operand_aliasing={{1}: (6, {}), {2}: (7, {})} | custom-call | flops 671088640 | bytes 4718592 | tf_op jit(solution)/shard_map/stage/pallas_call | solution.py:294
  106.2 1.9 %collective-permute-start.7 = (bf16[2,64,1152]{2,1,0:T(8,128)(2,1)S(1)}, bf16[2,64,1152]{2,1,0:T(8,128)(2,1)S(1)}, u32[]{:S(2)}, u32[]{:S(2)}) collective-permute-start(bf16[2,64,1152]{2,1,0:T(8,128)(2,1)S(1)} %get-tuple-element.125), channel_id=1, source_target_pairs={{3,4},{4,5},{11,12},{12,13},{19,20},{20,21},{27,28},{28,29},{35,36... | collective-permute-start | bytes 884744 | tf_op jit(solution)/shard_map/ppermute | solution.py:299
  108.1 1.4 post.12
  109.6 6.8 %collective-permute-done.7.x_ref = bf16[2,64,1152]{2,1,0:T(8,128)(2,1)S(1)} collective-permute-done((bf16[2,64,1152]{2,1,0:T(8,128)(2,1)S(1)}, bf16[2,64,1152]{2,1,0:T(8,128)(2,1)S(1)}, u32[]{:S(2)}, u32[]{:S(2)}) %collective-permute-start.7) | collective-permute-done | bytes 294944 | tf_op jit(solution)/shard_map/ppermute | solution.py:299
  116.4 2.4 %stage.14 = (f32[2,64,1024]{2,1,0:T(8,128)S(1)}, bf16[2,2,16,2,16,1152]{5,4,3,2,1,0:T(8,128)(2,1)S(1)}, bf16[2,128,128]{2,1,0:T(8,128)(2,1)S(1)}, bf16[2,64,1152]{2,1,0:T(8,128)(2,1)S(1)}) custom-call(s32[3]{0:T(128)S(1)} %pad_add_fusion.1.sc_ref, ...), custom_call_target="tpu_custom_call", output_to_operand_aliasing={{1}: (6, {}), {2}: (7, {})} | custom-call | flops 671088640 | bytes 4718592 | tf_op jit(solution)/shard_map/stage/pallas_call | solution.py:294
  118.8 1.3 collective-permute-start.8
  120.1 1.4 post.13
  121.5 2.8 %collective-permute-done.8.x_ref = bf16[2,64,1152]{2,1,0:T(8,128)(2,1)S(1)} collective-permute-done((bf16[2,64,1152]{2,1,0:T(8,128)(2,1)S(1)}, bf16[2,64,1152]{2,1,0:T(8,128)(2,1)S(1)}, u32[]{:S(2)}, u32[]{:S(2)}) %collective-permute-start.8) | collective-permute-done | bytes 294944 | tf_op jit(solution)/shard_map/ppermute | solution.py:299
  124.3 0.5 stage.15
  124.9 0.7 collective-permute-start.9
  125.5 0.6 post.14
  126.1 0.6 stage.16
  126.7 0.7 collective-permute-start.10
  127.4 0.6 post.15
  128.0 0.0 copy-start.2
  128.0 0.6 stage.17
  128.5 0.7 collective-permute-start.12
  129.2 0.7 collective-permute-start.11
  129.9 0.6 last_gradient.1
  130.5 0.7 mul.35
  131.2 14.7 %all-to-all-start.2 = ((f32[64,1,16]{2,1,0:T(1,128)}), f32[64,1,16]{2,1,0:T(1,128)S(1)}, u32[]{:S(2)}, u32[]{:S(2)}) async-start(f32[64,1,16]{2,1,0:T(1,128)} %bitcast.12), calls=%async_computation.2 | async-start | bytes 65536 | tf_op jit(solution)/shard_map/all_to_all | solution.py:311
  145.9 0.6 last_store.1
  146.4 16.1 %all-to-all-done.2 = f32[64,1,16]{2,1,0:T(1,128)S(1)} async-done(((f32[64,1,16]{2,1,0:T(1,128)}), f32[64,1,16]{2,1,0:T(1,128)S(1)}, u32[]{:S(2)}, u32[]{:S(2)}) %all-to-all-start.2) | async-done | bytes 4128 | tf_op jit(solution)/shard_map/all_to_all | solution.py:311
  162.6 0.7 collective-permute-start.13
  163.3 1.3 collective-permute-start.14
  164.6 0.5 reduce_sum.19
  165.1 21.9 %collective-permute-done.14 = bf16[2,128,128]{2,1,0:T(8,128)(2,1)S(1)} collective-permute-done((bf16[2,128,128]{2,1,0:T(8,128)(2,1)S(1)}, bf16[2,128,128]{2,1,0:T(8,128)(2,1)S(1)}, u32[]{:S(2)}, u32[]{:S(2)}) %collective-permute-start.14) | collective-permute-done | bytes 65568 | tf_op jit(solution)/shard_map/ppermute | solution.py:316
  187.0 0.8 copy.66
  (32 shorter events, 0.2 us)
Async XLA Ops:
  0.6 35.1 %copy-start.4 = (s32[128]{0:T(128)S(1)}, s32[128]{0:T(128)}, u32[]{:S(2)}) copy-start(s32[128]{0:T(128)} %param.10) | copy-start | bytes 1540
  0.6 35.3 %copy-start.3 = (f32[128,2]{0,1:T(2,128)S(1)}, f32[128,2]{0,1:T(2,128)}, u32[]{:S(2)}) copy-start(f32[128,2]{0,1:T(2,128)} %param.11) | copy-start | bytes 3076
  0.7 35.5 %copy-start.1 = (bf16[128,2,1024]{2,1,0:T(2,128)(2,1)S(1)}, bf16[128,2,1024]{2,1,0:T(2,128)(2,1)}, u32[]{:S(2)}) copy-start(bf16[128,2,1024]{2,1,0:T(2,128)(2,1)} %param.12) | copy-start | bytes 1572868
  2.9 26.3 %all-to-all-start.1 = ((bf16[16,2,16,1152]{3,2,1,0:T(8,128)(2,1)}), bf16[16,2,16,1152]{3,2,1,0:T(8,128)(2,1)S(1)}, u32[]{:S(2)}, u32[]{:S(2)}) async-start(bf16[16,2,16,1152]{3,2,1,0:T(8,128)(2,1)} %broadcast_in_dim.26), calls=%async_computation.1 | async-start | bytes 2359296 | tf_op jit(solution)/shard_map/all_to_all | solution.py:179
  9.9 17.7 %collective-permute-start = (bf16[2,16,1152]{2,0,1:T(2,128)(2,1)S(1)}, bf16[2,16,1152]{2,0,1:T(2,128)(2,1)S(1)}, u32[]{:S(2)}, u32[]{:S(2)}) collective-permute-start(bf16[2,16,1152]{2,0,1:T(2,128)(2,1)S(1)} %broadcast_select_fusion), channel_id=1, source_target_pairs={{0,256},{256,0},{1,257},{257,1},{2,258},{258,2},{3,259},{259,3},{4... | collective-permute-start | bytes 221192 | tf_op jit(solution)/shard_map/ppermute | solution.py:173
  30.3 23.6 %all-to-all-start = ((bf16[16,2,16,1152]{3,2,1,0:T(8,128)(2,1)}), bf16[16,2,16,1152]{3,2,1,0:T(8,128)(2,1)S(1)}, u32[]{:S(2)}, u32[]{:S(2)}) async-start(bf16[16,2,16,1152]{3,2,1,0:T(8,128)(2,1)} %broadcast_in_dim.25), calls=%async_computation | async-start | bytes 2359296 | tf_op jit(solution)/shard_map/all_to_all | solution.py:179
  37.5 18.4 %collective-permute-start.1 = (bf16[16,2,16,1152]{3,2,1,0:T(8,128)(2,1)S(1)}, bf16[16,2,16,1152]{3,2,1,0:T(8,128)(2,1)}, u32[]{:S(2)}, u32[]{:S(2)}) collective-permute-start(bf16[16,2,16,1152]{3,2,1,0:T(8,128)(2,1)S(1)} %all-to-all-done.1.own_ref), channel_id=1, source_target_pairs={{0,8},{8,0},{1,9},{9,1},{2,10},{10,2},{3,11},{11,3},{4,12},{12,4},... | collective-permute-start | bytes 3538952 | tf_op jit(solution)/shard_map/ppermute | solution.py:173
  53.9 4.9 %collective-permute-start.2 = (bf16[16,2,16,1152]{3,2,1,0:T(8,128)(2,1)S(1)}, bf16[16,2,16,1152]{3,2,1,0:T(8,128)(2,1)}, u32[]{:S(2)}, u32[]{:S(2)}) collective-permute-start(bf16[16,2,16,1152]{3,2,1,0:T(8,128)(2,1)S(1)} %all-to-all-done.far_ref), channel_id=1, source_target_pairs={{0,8},{8,0},{1,9},{9,1},{2,10},{10,2},{3,11},{11,3},{4,12},{12,4},... | collective-permute-start | bytes 3538952 | tf_op jit(solution)/shard_map/ppermute | solution.py:173
  55.9 5.5 %copy-start = (s32[128,128]{1,0:T(8,128)S(1)}, s32[128,128]{1,0:T(8,128)}, u32[]{:S(2)}) copy-start(s32[128,128]{1,0:T(8,128)} %receivers_ref.17) | copy-start | bytes 196612
  61.9 1.3 collective-permute-start.3
  63.8 1.3 collective-permute-start.4
  65.6 1.3 collective-permute-start.5
  67.4 36.6 %collective-permute-start.6 = (bf16[2,64,1152]{2,1,0:T(8,128)(2,1)S(1)}, bf16[2,64,1152]{2,1,0:T(8,128)(2,1)S(1)}, u32[]{:S(2)}, u32[]{:S(2)}) collective-permute-start(bf16[2,64,1152]{2,1,0:T(8,128)(2,1)S(1)} %get-tuple-element.116), channel_id=1, source_target_pairs={{2,3},{3,4},{10,11},{11,12},{18,19},{19,20},{26,27},{27,28},{34,35... | collective-permute-start | bytes 884744 | tf_op jit(solution)/shard_map/ppermute | solution.py:299
  106.2 10.2 %collective-permute-start.7 = (bf16[2,64,1152]{2,1,0:T(8,128)(2,1)S(1)}, bf16[2,64,1152]{2,1,0:T(8,128)(2,1)S(1)}, u32[]{:S(2)}, u32[]{:S(2)}) collective-permute-start(bf16[2,64,1152]{2,1,0:T(8,128)(2,1)S(1)} %get-tuple-element.125), channel_id=1, source_target_pairs={{3,4},{4,5},{11,12},{12,13},{19,20},{20,21},{27,28},{28,29},{35,36... | collective-permute-start | bytes 884744 | tf_op jit(solution)/shard_map/ppermute | solution.py:299
  118.8 5.5 %collective-permute-start.8 = (bf16[2,64,1152]{2,1,0:T(8,128)(2,1)S(1)}, bf16[2,64,1152]{2,1,0:T(8,128)(2,1)S(1)}, u32[]{:S(2)}, u32[]{:S(2)}) collective-permute-start(bf16[2,64,1152]{2,1,0:T(8,128)(2,1)S(1)} %get-tuple-element.134), channel_id=1, source_target_pairs={{4,5},{5,6},{12,13},{13,14},{20,21},{21,22},{28,29},{29,30},{36,37... | collective-permute-start | bytes 884744 | tf_op jit(solution)/shard_map/ppermute | solution.py:299
  124.9 1.3 collective-permute-start.9
  126.7 1.3 collective-permute-start.10
  128.0 59.0 %copy-start.2 = (f32[128,2,128]{2,1,0:T(2,128)S(1)}, f32[128,2,128]{2,1,0:T(2,128)}, u32[]{:S(2)}) copy-start(f32[128,2,128]{2,1,0:T(2,128)} %param.14) | copy-start | bytes 393220
  128.5 34.0 %collective-permute-start.12 = (bf16[2,128,128]{2,1,0:T(8,128)(2,1)S(1)}, bf16[2,128,128]{2,1,0:T(8,128)(2,1)S(1)}, u32[]{:S(2)}, u32[]{:S(2)}) collective-permute-start(bf16[2,128,128]{2,1,0:T(8,128)(2,1)S(1)} %get-tuple-element.161), channel_id=1, source_target_pairs={{7,2},{15,10},{23,18},{31,26},{39,34},{47,42},{55,50},{63,58},{71,... | collective-permute-start | bytes 196616 | tf_op jit(solution)/shard_map/ppermute | solution.py:307
  129.2 33.4 %collective-permute-start.11 = (bf16[2,128,128]{2,1,0:T(8,128)(2,1)S(1)}, bf16[2,128,128]{2,1,0:T(8,128)(2,1)S(1)}, u32[]{:S(2)}, u32[]{:S(2)}) collective-permute-start(bf16[2,128,128]{2,1,0:T(8,128)(2,1)S(1)} %get-tuple-element.161), channel_id=1, source_target_pairs={{7,6},{15,14},{23,22},{31,30},{39,38},{47,46},{55,54},{63,62},{71,... | collective-permute-start | bytes 196616 | tf_op jit(solution)/shard_map/ppermute | solution.py:307
  131.2 31.4 %all-to-all-start.2 = ((f32[64,1,16]{2,1,0:T(1,128)}), f32[64,1,16]{2,1,0:T(1,128)S(1)}, u32[]{:S(2)}, u32[]{:S(2)}) async-start(f32[64,1,16]{2,1,0:T(1,128)} %bitcast.12), calls=%async_computation.2 | async-start | bytes 65536 | tf_op jit(solution)/shard_map/all_to_all | solution.py:311
  162.6 0.7 collective-permute-start.13
  163.3 23.7 %collective-permute-start.14 = (bf16[2,128,128]{2,1,0:T(8,128)(2,1)S(1)}, bf16[2,128,128]{2,1,0:T(8,128)(2,1)S(1)}, u32[]{:S(2)}, u32[]{:S(2)}) collective-permute-start(bf16[2,128,128]{2,1,0:T(8,128)(2,1)S(1)} %add.35), channel_id=1, source_target_pairs={{2,1},{0,3},{6,4},{10,9},{8,11},{14,12},{18,17},{16,19},{22,20},{2... | collective-permute-start | bytes 196616 | tf_op jit(solution)/shard_map/ppermute | solution.py:316
